TPU v7x, 32 devices: a whole 2x2x4 slice. The times are simulated.
32 devices in a mesh: groups: 2 (over y), wide: 2 (over x), narrow: 4 (over z), sub: 2 (over core).
Axes of the slice: x: 2, y: 2, z: 4, core: 2. Of those that a mesh axis runs over, the one named last changes fastest.
Arguments:
- radiance: bfloat16 [1024, 64, 512], P(('groups', 'wide', 'narrow', 'sub')), parts along dimension 0, may hold values from -6 to 6
- band_mask: int32 [512], replicated, may hold values from 0 to 1, as said below
- row_counts: int32 [32], P(('groups', 'wide', 'narrow', 'sub')), parts along dimension 0, may hold values from 16 to 32, as said below
- noise_kernel: float32 [8, 512], replicated, may hold values from -1 to 1
- smooth_kernel: float32 [25, 512], replicated, may hold values from 0.01 to 0.1
- start_basis: float32 [512, 128], replicated, may hold values from -6 to 6
Outputs:
- components: float32 [1024, 64, 128], P(('groups', 'wide', 'narrow', 'sub')), parts along dimension 0
There are 2 independent parts, one for each index of `groups`. A program takes and returns all parts, laid end to end along the dimension named above; an argument that names none is the same for every part. Nothing has to cross between parts.
Inputs may be any that keep to these rules, and one draw needn't show every extreme that they name: `band_mask`: exactly 425 of the 512 entries are 1, at bands drawn from the seed. `row_counts`: every draw holds a full device and one with half its rows valid.
All inputs are finite; a program needn't handle non-finite values.
Results may differ from a plain program's by a relative error of at most 0.0031.
Values may be sent and summed in bfloat16 or wider, within the bound.
No kernel may reach another device: no remote copies, remote signals or barrier semaphores. Data moves between devices by JAX's collectives and lax.ppermute only.
A program may use at most 192 MiB of HBM per device.

v0:
```python
import jax
import jax.numpy as jnp
from jax import lax
from jax.sharding import PartitionSpec as P

SWEEPS = 2


def extended(block, sides, width):
    for axis, dim in sides:
        count = lax.axis_size(axis)
        forward = [(i, i + 1) for i in range(count - 1)]
        backward = [(target, source) for source, target in forward]
        low = lax.ppermute(
            lax.slice_in_dim(block, block.shape[dim] - width, None, axis=dim), axis, forward
        )
        high = lax.ppermute(lax.slice_in_dim(block, 0, width, axis=dim), axis, backward)
        block = jnp.concatenate([low, block, high], axis=dim)
    return block


def filters(padded, noise_kernel, smooth_kernel):
    height = padded.shape[0] - 4
    across = padded.shape[1]
    framed = jnp.pad(padded, ((0, 0), (2, 2), (0, 0)))
    running = framed[2 : 2 + height, 2 : 2 + across].astype(jnp.float32)
    tap_index = 0
    for row_off in (-1, 0, 1):
        for col_off in (-1, 0, 1):
            if row_off == 0 and col_off == 0:
                continue
            window = framed[2 + row_off : 2 + row_off + height, 2 + col_off : 2 + col_off + across]
            running = running - noise_kernel[tap_index] * window.astype(jnp.float32)
            tap_index += 1
    smooth = jnp.zeros((height // 2, across // 2, padded.shape[2]), jnp.float32)
    for row_off in range(5):
        for col_off in range(5):
            window = framed[row_off : row_off + height : 2, col_off : col_off + across : 2]
            smooth = smooth + smooth_kernel[row_off * 5 + col_off] * window.astype(jnp.float32)
    return (running.astype(jnp.bfloat16), smooth.astype(jnp.bfloat16))


def gram(values):
    flattened = values.reshape(-1, values.shape[-1])
    return lax.dot_general(
        flattened, flattened, (((0,), (0,)), ((), ())), preferred_element_type=jnp.float32
    )


def project(operator, lower_noise, band_keep, start_basis):
    basis_now = start_basis * band_keep[:, None]
    for sweep in range(SWEEPS):
        mapped = jnp.dot(operator, basis_now, precision=lax.Precision.HIGHEST)
        gram_small = jnp.dot(mapped.T, mapped, precision=lax.Precision.HIGHEST)
        factor = jnp.linalg.cholesky(gram_small)
        basis_now = jax.scipy.linalg.solve_triangular(factor, mapped.T, lower=True).T
    weights = jax.scipy.linalg.solve_triangular(lower_noise, basis_now, lower=True, trans=1)
    return weights.astype(jnp.bfloat16)


def finish_grams(noise_gram, signal_gram, pixel_total, band_keep, start_basis):
    pair_mask = band_keep[:, None] * band_keep[None, :]
    fill = jnp.diag(1.0 - band_keep)
    lower_noise = jnp.linalg.cholesky(noise_gram * pair_mask / pixel_total + fill)
    partial_solve = jax.scipy.linalg.solve_triangular(
        lower_noise, signal_gram * pair_mask + fill, lower=True
    )
    operator = jax.scipy.linalg.solve_triangular(lower_noise, partial_solve.T, lower=True)
    return project(operator, lower_noise, band_keep, start_basis)


def local(radiance, band_mask, row_counts, noise_kernel, smooth_kernel, start_basis):
    height = radiance.shape[0]
    across = radiance.shape[1]
    band_keep = band_mask.astype(jnp.float32)
    row_valid = (jnp.arange(height, dtype=jnp.int32) < row_counts[0]).astype(jnp.float32)
    masked = radiance * (row_valid[:, None, None] * band_keep[None, None, :]).astype(jnp.bfloat16)
    padded = extended(masked, ((("wide", "narrow", "sub"), 0),), 2)
    noise_field, signal = filters(padded, noise_kernel, smooth_kernel)
    noise_field = noise_field * row_valid[:, None, None].astype(jnp.bfloat16)
    noise_gram = gram(noise_field)
    signal_gram = gram(signal)
    count_sum = row_counts[0].astype(jnp.float32)
    noise_gram, signal_gram, count_sum = lax.psum(
        (noise_gram, signal_gram, count_sum), ("wide", "narrow", "sub")
    )
    weights = finish_grams(noise_gram, signal_gram, across * count_sum, band_keep, start_basis)
    flattened = masked.reshape(height * across, masked.shape[2])
    result = jnp.dot(flattened, weights, preferred_element_type=jnp.float32)
    return result.reshape(height, across, weights.shape[1])


def solution(mesh):
    return jax.shard_map(
        local,
        mesh=mesh,
        in_specs=(
            P(("groups", "wide", "narrow", "sub"), None, None),
            P(),
            P(("groups", "wide", "narrow", "sub")),
            P(),
            P(),
            P(),
        ),
        out_specs=P(("groups", "wide", "narrow", "sub"), None, None),
        check_vma=False,
    )
```

profile of v0, /device:TPU:0, one launch (start us, length us, event | category | flops | bytes accessed | tf_op | source)
XLA Modules:
  0.0 494.2 jit_solution(5932911163382308182)
XLA Ops:
  8.0 1.7 broadcast_multiply_fusion
  9.8 2.4 collective-permute-start
  14.7 2.9 collective-permute-done.1
  19.7 5.2 %slice.375 = bf16[16,32,512]{2,1,0:T(8,128)(2,1)} slice(bf16[36,68,512]{2,1,0:T(8,128)(2,1)S(1)} %fusion.5), slice={[0:32:2], [1:65:2], [0:512:1]} | slice | bytes 1048576 | tf_op jit(solution)/shard_map/slice | solution.py:38
  24.9 5.3 %slice.377 = bf16[16,32,512]{2,1,0:T(8,128)(2,1)} slice(bf16[36,68,512]{2,1,0:T(8,128)(2,1)S(1)} %fusion.5), slice={[0:32:2], [2:66:2], [0:512:1]} | slice | bytes 1048576 | tf_op jit(solution)/shard_map/slice | solution.py:38
  30.3 5.3 %slice.379 = bf16[16,32,512]{2,1,0:T(8,128)(2,1)} slice(bf16[36,68,512]{2,1,0:T(8,128)(2,1)S(1)} %fusion.5), slice={[0:32:2], [3:67:2], [0:512:1]} | slice | bytes 1048576 | tf_op jit(solution)/shard_map/slice | solution.py:38
  35.6 5.3 %slice.381 = bf16[16,32,512]{2,1,0:T(8,128)(2,1)} slice(bf16[36,68,512]{2,1,0:T(8,128)(2,1)S(1)} %fusion.5), slice={[0:32:2], [4:68:2], [0:512:1]} | slice | bytes 1048576 | tf_op jit(solution)/shard_map/slice | solution.py:38
  40.9 5.2 %slice.383 = bf16[16,32,512]{2,1,0:T(8,128)(2,1)} slice(bf16[36,68,512]{2,1,0:T(8,128)(2,1)S(1)} %fusion.5), slice={[1:33:2], [0:64:2], [0:512:1]} | slice | bytes 1048576 | tf_op jit(solution)/shard_map/slice | solution.py:38
  46.1 5.2 %slice.385 = bf16[16,32,512]{2,1,0:T(8,128)(2,1)} slice(bf16[36,68,512]{2,1,0:T(8,128)(2,1)S(1)} %fusion.5), slice={[1:33:2], [1:65:2], [0:512:1]} | slice | bytes 1048576 | tf_op jit(solution)/shard_map/slice | solution.py:38
  51.3 5.3 %slice.387 = bf16[16,32,512]{2,1,0:T(8,128)(2,1)} slice(bf16[36,68,512]{2,1,0:T(8,128)(2,1)S(1)} %fusion.5), slice={[1:33:2], [2:66:2], [0:512:1]} | slice | bytes 1048576 | tf_op jit(solution)/shard_map/slice | solution.py:38
  56.6 5.3 %slice.389 = bf16[16,32,512]{2,1,0:T(8,128)(2,1)} slice(bf16[36,68,512]{2,1,0:T(8,128)(2,1)S(1)} %fusion.5), slice={[1:33:2], [3:67:2], [0:512:1]} | slice | bytes 1048576 | tf_op jit(solution)/shard_map/slice | solution.py:38
  61.9 5.3 %slice.391 = bf16[16,32,512]{2,1,0:T(8,128)(2,1)} slice(bf16[36,68,512]{2,1,0:T(8,128)(2,1)S(1)} %fusion.5), slice={[1:33:2], [4:68:2], [0:512:1]} | slice | bytes 1048576 | tf_op jit(solution)/shard_map/slice | solution.py:38
  67.2 5.2 %slice.393 = bf16[16,32,512]{2,1,0:T(8,128)(2,1)} slice(bf16[36,68,512]{2,1,0:T(8,128)(2,1)S(1)} %fusion.5), slice={[2:34:2], [0:64:2], [0:512:1]} | slice | bytes 1048576 | tf_op jit(solution)/shard_map/slice | solution.py:38
  72.4 5.2 %slice.395 = bf16[16,32,512]{2,1,0:T(8,128)(2,1)} slice(bf16[36,68,512]{2,1,0:T(8,128)(2,1)S(1)} %fusion.5), slice={[2:34:2], [1:65:2], [0:512:1]} | slice | bytes 1048576 | tf_op jit(solution)/shard_map/slice | solution.py:38
  77.6 5.3 %slice.397 = bf16[16,32,512]{2,1,0:T(8,128)(2,1)} slice(bf16[36,68,512]{2,1,0:T(8,128)(2,1)S(1)} %fusion.5), slice={[2:34:2], [2:66:2], [0:512:1]} | slice | bytes 1048576 | tf_op jit(solution)/shard_map/slice | solution.py:38
  82.9 5.3 %slice.399 = bf16[16,32,512]{2,1,0:T(8,128)(2,1)} slice(bf16[36,68,512]{2,1,0:T(8,128)(2,1)S(1)} %fusion.5), slice={[2:34:2], [3:67:2], [0:512:1]} | slice | bytes 1048576 | tf_op jit(solution)/shard_map/slice | solution.py:38
  88.3 5.3 %slice.401 = bf16[16,32,512]{2,1,0:T(8,128)(2,1)} slice(bf16[36,68,512]{2,1,0:T(8,128)(2,1)S(1)} %fusion.5), slice={[2:34:2], [4:68:2], [0:512:1]} | slice | bytes 1048576 | tf_op jit(solution)/shard_map/slice | solution.py:38
  93.6 5.2 %slice.403 = bf16[16,32,512]{2,1,0:T(8,128)(2,1)} slice(bf16[36,68,512]{2,1,0:T(8,128)(2,1)S(1)} %fusion.5), slice={[3:35:2], [0:64:2], [0:512:1]} | slice | bytes 1048576 | tf_op jit(solution)/shard_map/slice | solution.py:38
  98.8 5.2 %slice.405 = bf16[16,32,512]{2,1,0:T(8,128)(2,1)} slice(bf16[36,68,512]{2,1,0:T(8,128)(2,1)S(1)} %fusion.5), slice={[3:35:2], [1:65:2], [0:512:1]} | slice | bytes 1048576 | tf_op jit(solution)/shard_map/slice | solution.py:38
  104.0 5.3 %slice.407 = bf16[16,32,512]{2,1,0:T(8,128)(2,1)} slice(bf16[36,68,512]{2,1,0:T(8,128)(2,1)S(1)} %fusion.5), slice={[3:35:2], [2:66:2], [0:512:1]} | slice | bytes 1048576 | tf_op jit(solution)/shard_map/slice | solution.py:38
  109.3 5.3 %slice.409 = bf16[16,32,512]{2,1,0:T(8,128)(2,1)} slice(bf16[36,68,512]{2,1,0:T(8,128)(2,1)S(1)} %fusion.5), slice={[3:35:2], [3:67:2], [0:512:1]} | slice | bytes 1048576 | tf_op jit(solution)/shard_map/slice | solution.py:38
  114.6 5.3 %slice.411 = bf16[16,32,512]{2,1,0:T(8,128)(2,1)} slice(bf16[36,68,512]{2,1,0:T(8,128)(2,1)S(1)} %fusion.5), slice={[3:35:2], [4:68:2], [0:512:1]} | slice | bytes 1048576 | tf_op jit(solution)/shard_map/slice | solution.py:38
  120.0 5.2 %slice.413 = bf16[16,32,512]{2,1,0:T(8,128)(2,1)} slice(bf16[36,68,512]{2,1,0:T(8,128)(2,1)S(1)} %fusion.5), slice={[4:36:2], [0:64:2], [0:512:1]} | slice | bytes 1048576 | tf_op jit(solution)/shard_map/slice | solution.py:38
  125.2 5.2 %slice.415 = bf16[16,32,512]{2,1,0:T(8,128)(2,1)} slice(bf16[36,68,512]{2,1,0:T(8,128)(2,1)S(1)} %fusion.5), slice={[4:36:2], [1:65:2], [0:512:1]} | slice | bytes 1048576 | tf_op jit(solution)/shard_map/slice | solution.py:38
  130.4 5.3 %slice.417 = bf16[16,32,512]{2,1,0:T(8,128)(2,1)} slice(bf16[36,68,512]{2,1,0:T(8,128)(2,1)S(1)} %fusion.5), slice={[4:36:2], [2:66:2], [0:512:1]} | slice | bytes 1048576 | tf_op jit(solution)/shard_map/slice | solution.py:38
  135.7 5.3 %slice.419 = bf16[16,32,512]{2,1,0:T(8,128)(2,1)} slice(bf16[36,68,512]{2,1,0:T(8,128)(2,1)S(1)} %fusion.5), slice={[4:36:2], [3:67:2], [0:512:1]} | slice | bytes 1048576 | tf_op jit(solution)/shard_map/slice | solution.py:38
  141.0 5.5 %slice.421 = bf16[16,32,512]{2,1,0:T(8,128)(2,1)} slice(bf16[36,68,512]{2,1,0:T(8,128)(2,1)S(1)} %fusion.5), slice={[4:36:2], [4:68:2], [0:512:1]} | slice | bytes 1048576 | tf_op jit(solution)/shard_map/slice | solution.py:38
  146.5 15.4 %convolution_bitcast_fusion = f32[512,512]{0,1:T(8,128)} fusion(bf16[16,32,512]{2,1,0:T(8,128)(2,1)} %slice.421, bf16[16,32,512]{2,1,0:T(8,128)(2,1)} %slice.419, bf16[16,32,512]{2,1,0:T(8,128)(2,1)} %slice.417, bf16[16,32,512]{2,1,0:T(8,128)(2,1)} %slice.415, bf16[16,32,512]{2,1,0:T(8,128)(2,1)} %slice.413, bf16[16,32,512]{2,1,0:T(8,128)(2,1)} %slice.411, ...), kind=kOutput, calls=%fused_computation.20 | convolution fusion | flops 288096256 | bytes 14206976 | tf_op jit(solution)/shard_map/dot_general | solution.py:45
  161.9 11.9 %fusion.8 = f32[512,512]{0,1:T(8,128)} fusion(bf16[36,68,512]{2,1,0:T(8,128)(2,1)S(1)} %fusion.5, f32[512]{0:T(512)S(1)} %bitcast.166, bf16[2,64,512]{2,1,0:T(8,128)(2,1)S(1)} %collective-permute-done.1, bf16[32,64,512]{2,1,0:T(8,128)(2,1)S(1)} %copy-done.1, f32[512]{0:T(512)S(1)} %bitcast.167, f32[512]{0:T(512)S(1)} %bitcast.161, f32[512]{0:T(512)S(1)} %bitcast.162, ...), kind=kOutput, calls=%fused_computation.19 | convolution fusion | flops 1104150528 | bytes 16007680 | tf_op jit(solution)/shard_map/dot_general | solution.py:45
  173.8 34.7 %psum.22 = f32[]{:T(128)} all-reduce(f32[]{:T(128)S(6)} %convert_element_type.157), channel_id=1, replica_groups=mesh['groups'=2,'wide'=2,'narrow'=4,'sub'=2] {'wide','narrow','sub'}, use_global_device_ids=true, to_apply=%region_1.2 | all-reduce | flops 1 | bytes 8 | tf_op jit(solution)/shard_map/psum | solution.py:84
  209.2 68.8 %all-reduce.5.cloned.1.call-done = (f32[512,512]{0,1:T(8,128)}, f32[512,512]{0,1:T(8,128)}) async-done(((f32[512,512]{0,1:T(8,128)}, f32[512,512]{0,1:T(8,128)}), (f32[512,512]{0,1:T(8,128)}, f32[512,512]{0,1:T(8,128)})) %all-reduce.5.cloned.1.call-update) | async-done | bytes 2097168 | tf_op jit(solution)/shard_map/psum | solution.py:84
  278.0 2.8 select_add_fusion.1
  281.3 11.7 %cholesky.119 = f32[128,128]{1,0:T(8,128)S(1)} custom-call(f32[128,128]{1,0:T(8,128)S(1)} %cholesky.327), custom_call_target="Cholesky" | custom-call | tf_op jit(solution)/shard_map/jit(cholesky)/cholesky | solution.py:64
  293.1 9.8 %custom-call.39 = f32[1,128,128]{1,2,0:T(8,128)S(1)} custom-call(f32[1,128,128]{2,1,0:T(8,128)S(1)} %get-tuple-element.63), custom_call_target="InvertDiagBlocksLowerTriangular" | custom-call | tf_op jit(solution)/shard_map/jit(cholesky)/cholesky | solution.py:64
  303.6 11.7 %cholesky.242 = f32[128,128]{1,0:T(8,128)S(1)} custom-call(f32[128,128]{1,0:T(8,128)S(1)} %cholesky.331), custom_call_target="Cholesky" | custom-call | tf_op jit(solution)/shard_map/jit(cholesky)/cholesky | solution.py:64
  315.6 10.0 %custom-call.40 = f32[1,128,128]{1,2,0:T(8,128)S(1)} custom-call(f32[1,128,128]{2,1,0:T(8,128)S(1)} %get-tuple-element.61), custom_call_target="InvertDiagBlocksLowerTriangular" | custom-call | tf_op jit(solution)/shard_map/jit(cholesky)/cholesky | solution.py:64
  326.7 11.7 %cholesky.263 = f32[128,128]{1,0:T(8,128)S(1)} custom-call(f32[128,128]{1,0:T(8,128)S(1)} %cholesky.336), custom_call_target="Cholesky" | custom-call | tf_op jit(solution)/shard_map/jit(cholesky)/cholesky | solution.py:64
  338.6 9.8 %custom-call.41 = f32[1,128,128]{1,2,0:T(8,128)S(1)} custom-call(f32[1,128,128]{2,1,0:T(8,128)S(1)} %get-tuple-element.59), custom_call_target="InvertDiagBlocksLowerTriangular" | custom-call | tf_op jit(solution)/shard_map/jit(cholesky)/cholesky | solution.py:64
  349.2 12.1 %cholesky.280 = f32[128,128]{1,0:T(8,128)S(1)} custom-call(f32[128,128]{1,0:T(8,128)S(1)} %convolution_subtract_fusion.11), custom_call_target="Cholesky" | custom-call | tf_op jit(solution)/shard_map/jit(cholesky)/cholesky | solution.py:64
  365.9 10.7 %while.5 = (s32[]{:T(128)}, f32[512,512]{0,1:T(8,128)S(1)}, s32[4,2]{0,1:T(2,128)S(1)}, f32[4,128,128]{2,1,0:T(8,128)}, s32[]{:T(128)}) while((s32[]{:T(128)}, f32[512,512]{0,1:T(8,128)S(1)}, s32[4,2]{0,1:T(2,128)S(1)}, f32[4,128,128]{2,1,0:T(8,128)}, s32[]{:T(128)}) %tuple.71), condition=%wide.while_cond.1, body=%wide.while_body.1.sunk | while | flops 2 | bytes 393829 | solution.py:57
  376.6 40.1 %custom-call.42 = f32[4,128,128]{1,2,0:T(8,128)S(1)} custom-call(f32[4,128,128]{2,1,0:T(8,128)} %get-tuple-element.23), custom_call_target="InvertDiagBlocksLowerTriangular" | custom-call | tf_op jit(solution)/shard_map/jit(_solve_triangular)/triangular_solve | solution.py:57
  419.6 1.5 convolution_subtract_fusion.5
  428.3 11.9 %cholesky.307 = f32[128,128]{1,0:T(8,128)S(1)} custom-call(f32[128,128]{1,0:T(8,128)S(1)} %fusion.78), custom_call_target="Cholesky" | custom-call | tf_op jit(solution)/shard_map/jit(cholesky)/cholesky | solution.py:55
  441.6 9.8 %custom-call.47 = f32[1,128,128]{1,2,0:T(8,128)S(1)} custom-call(f32[1,128,128]{2,1,0:T(8,128)S(1)} %fusion.68), custom_call_target="InvertDiagBlocksLowerTriangular" | custom-call | tf_op jit(solution)/shard_map/jit(_solve_triangular)/triangular_solve | solution.py:56
  451.8 2.2 fusion.24
  455.5 11.7 %cholesky.318 = f32[128,128]{1,0:T(8,128)S(1)} custom-call(f32[128,128]{1,0:T(8,128)S(1)} %fusion.76), custom_call_target="Cholesky" | custom-call | tf_op jit(solution)/shard_map/jit(cholesky)/cholesky | solution.py:55
  468.5 10.0 %custom-call.48 = f32[1,128,128]{1,2,0:T(8,128)S(1)} custom-call(f32[1,128,128]{2,1,0:T(8,128)S(1)} %fusion.69), custom_call_target="InvertDiagBlocksLowerTriangular" | custom-call | tf_op jit(solution)/shard_map/jit(_solve_triangular)/triangular_solve | solution.py:56
  485.5 1.7 fusion.58
  (131 shorter events, 43.2 us)
Async XLA Ops:
  6.5 6.9 %copy-start.9 = (f32[25,512]{1,0:T(8,128)S(1)}, f32[25,512]{1,0:T(8,128)}, u32[]{:S(2)}) copy-start(f32[25,512]{1,0:T(8,128)} %param.15) | copy-start | bytes 153604
  6.5 7.0 %copy-start.10 = (f32[8,512]{1,0:T(8,128)S(1)}, f32[8,512]{1,0:T(8,128)}, u32[]{:S(2)}) copy-start(f32[8,512]{1,0:T(8,128)} %param.14) | copy-start | bytes 49156
  6.5 271.4 %all-reduce.5.cloned.1.call-start = ((), (), s32[]{:S(2)}) async-start(), calls=%async_computation | async-start | bytes 4194304 | tf_op jit(solution)/shard_map/psum | solution.py:84
  9.7 7.8 %copy-start = (bf16[32,64,512]{2,1,0:T(8,128)(2,1)}, bf16[32,64,512]{2,1,0:T(8,128)(2,1)S(1)}, u32[]{:S(2)}) copy-start(bf16[32,64,512]{2,1,0:T(8,128)(2,1)S(1)} %broadcast_multiply_fusion) | copy-start | bytes 6291460
  9.8 4.9 collective-permute-start
  12.2 5.4 %collective-permute-start.1 = (bf16[2,64,512]{2,1,0:T(8,128)(2,1)S(1)}, bf16[2,64,512]{2,1,0:T(8,128)(2,1)S(1)}, u32[]{:S(2)}, u32[]{:S(2)}) collective-permute-start(bf16[2,64,512]{2,1,0:T(8,128)(2,1)S(1)} %get-tuple-element.57), channel_id=1, source_target_pairs={{1,0},{2,1},{3,2},{4,3},{5,4},{6,5},{7,6},{8,7},{9,8},{10,9},{11,1... | collective-permute-start | bytes 393224 | tf_op jit(solution)/shard_map/ppermute | solution.py:17
  146.5 15.4 %copy-start.1 = (bf16[32,64,512]{2,1,0:T(8,128)(2,1)S(1)}, bf16[32,64,512]{2,1,0:T(8,128)(2,1)}, u32[]{:S(2)}) copy-start(bf16[32,64,512]{2,1,0:T(8,128)(2,1)} %copy-done) | copy-start | bytes 6291460
  146.5 15.4 %copy-start.13 = (bf16[32]{0:T(256)(128)(2,1)S(1)}, bf16[32]{0:T(256)(128)(2,1)}, u32[]{:S(2)}) copy-start(bf16[32]{0:T(256)(128)(2,1)} %fusion.102) | copy-start | bytes 196
  161.9 47.3 %copy-start.11 = (s32[512]{0:T(512)S(1)}, s32[512]{0:T(512)}, u32[]{:S(2)}) copy-start(s32[512]{0:T(512)} %param.12) | copy-start | bytes 6148
  338.6 78.2 %copy-start.3 = (f32[512,512]{0,1:T(8,128)S(1)}, f32[512,512]{0,1:T(8,128)}, u32[]{:S(2)}) copy-start(f32[512,512]{0,1:T(8,128)} %get-tuple-element.98) | copy-start | bytes 3145732
  416.7 9.3 %copy-start.4 = (f32[4,128,128]{1,2,0:T(8,128)}, f32[4,128,128]{1,2,0:T(8,128)S(1)}, u32[]{:S(2)}) copy-start(f32[4,128,128]{1,2,0:T(8,128)S(1)} %custom-call.42) | copy-start | bytes 786436
  422.1 4.4 copy-start.12
  423.1 4.4 copy-start.6
  424.5 26.8 %copy-start.7 = (f32[128,512]{1,0:T(8,128)}, f32[128,512]{1,0:T(8,128)S(1)}, u32[]{:S(2)}) copy-start(f32[128,512]{1,0:T(8,128)S(1)} %fusion.88) | copy-start | bytes 786436
  426.5 24.9 %copy-start.8 = (f32[128,512]{1,0:T(8,128)}, f32[128,512]{1,0:T(8,128)S(1)}, u32[]{:S(2)}) copy-start(f32[128,512]{1,0:T(8,128)S(1)} %fusion.90) | copy-start | bytes 786436
  451.8 33.6 %copy-start.2 = (bf16[32,64,512]{2,1,0:T(8,128)(2,1)S(1)}, bf16[32,64,512]{2,1,0:T(8,128)(2,1)}, u32[]{:S(2)}) copy-start(bf16[32,64,512]{2,1,0:T(8,128)(2,1)} %copy-done) | copy-start | bytes 6291460
  454.1 0.7 copy-start.5
Sparse Core Ops, SparseCore 0:
  174.0 103.9 all-reduce.4
where the time goes:
time: 498 us; the launch traced here: 494 us
  other arithmetic  173 us (35%)
  local copies, waits for them, and re-layouts  141 us (28%)
  waiting for transfers between devices  71.6 us (14%)
  matrix products  52.7 us (11%)
  blocking collectives  34.7 us (7%)
  between operations  18.1 us (4%)
    slice x25, local copies, waits for them, and re-layouts, filters(): window = framed[row_off:row_off + height:2, col_off:col_off + across:2]  127 us
    another operation x14, other arithmetic, finish_grams(): jnp.linalg.cholesky(noise_gram * pair_mask / pixel_total + fill)  78.9 us
    psum x1, waiting for transfers between devices, local(): lax.psum((noise_gram, signal_gram, count_sum), ('wide', 'narrow', 'sub'))  68.8 us
    another operation x3, other arithmetic, project(): jax.scipy.linalg.solve_triangular(lower_noise, basis_now, lower=True, tra...  40.3 us
    psum x1, blocking collectives, local(): lax.psum((noise_gram, signal_gram, count_sum), ('wide', 'narrow', 'sub'))  34.7 us
    dot_general x2, matrix products, gram(): lax.dot_general(flattened, flattened, (((0,), (0,)), ((), ())), preferred...  27.3 us
    another operation x6, other arithmetic, project(): factor = jnp.linalg.cholesky(gram_small)  25 us
    another operation x4, other arithmetic, project(): jax.scipy.linalg.solve_triangular(factor, mapped.T, lower=True)  21 us
  transfers between devices with their start and end apart: 3, of which 2 were waited for; matrix products, arithmetic and copies ran while one was open for 0% of the time, Pallas kernels for 0%

commit v1 on v0

v1 whole, which is shorter than its diff:
```python
import jax
import jax.numpy as jnp
from jax import lax
from jax.experimental import pallas as pl
from jax.experimental.pallas import tpu as pltpu
from jax.sharding import PartitionSpec as P

SWEEPS = 2
VALID = 425
AXES = ("wide", "narrow", "sub")
LANES = 128
USED = 448
STARTS = (0, 448, 768, 960)
PACKED = 1024
PITCH = 72
HIGH = lax.Precision.HIGHEST
F32 = jnp.float32
BF16 = jnp.bfloat16


def mm(a, b, dims=((1,), (0,))):
    return lax.dot_general(a, b, (dims, ((), ())), precision=HIGH, preferred_element_type=F32)


def front_kernel(count_ref, low_ref, x_ref, high_ref, pick_ref, taps_ref, out_ref, xs, taps, nf, sg):
    height = x_ref.shape[0] // 64
    count = count_ref[0]
    pitch = xs.shape[0] // 4
    taps[...] = mm(taps_ref[...], pick_ref[...].astype(F32))
    xs[...] = jnp.zeros_like(xs)
    pick = pick_ref[...]

    def place(block, first_row, limit):
        values = jnp.dot(block, pick, preferred_element_type=F32)
        for k in range(block.shape[0] // 64):
            row = first_row + k
            piece = values[k * 64 : (k + 1) * 64]
            if limit is not None:
                piece = jnp.where(row < limit, piece, 0.0)
            start = pl.multiple_of(8 + (row + 2) * PITCH, 8)
            for tile in range(4):
                xs[pl.ds(start + tile * pitch, 64), :] = piece[:, tile * LANES : (tile + 1) * LANES]

    place(low_ref[...], -2, None)
    place(high_ref[...], height, None)

    def place_body(chunk, carry):
        place(x_ref[pl.ds(pl.multiple_of(chunk * 256, 256), 256), :], chunk * 4, count)
        return carry

    lax.fori_loop(0, height // 4, place_body, 0)

    def column(base, offset):
        return xs[pl.ds(base + offset, 32, stride=2), :]

    def noise_body(row, carry):
        valid = row < count
        for tile in range(4):
            lanes = slice(tile * LANES, (tile + 1) * LANES)
            tap = lambda k: taps[k : k + 1, lanes]
            even = odd = None
            for index, row_off in enumerate((-1, 0, 1)):
                base = tile * pitch + 8 + (row + 2 + row_off) * PITCH
                here_even = column(base, 0)
                next_even = column(base, 2)
                prev_odd = column(base, -1)
                here_odd = column(base, 1)
                if row_off == 0:
                    left, right = tap(3), tap(4)
                    part_even = here_even - left * prev_odd - right * here_odd
                    part_odd = here_odd - left * here_even - right * next_even
                else:
                    first = 0 if row_off == -1 else 5
                    left, mid, right = tap(first), tap(first + 1), tap(first + 2)
                    part_even = -(left * prev_odd + mid * here_even + right * here_odd)
                    part_odd = -(left * here_even + mid * here_odd + right * next_even)
                even = part_even if even is None else even + part_even
                odd = part_odd if odd is None else odd + part_odd
            start = pl.multiple_of(row * 64, 64)
            nf[pl.ds(start, 32), lanes] = jnp.where(valid, even, 0.0).astype(BF16)
            nf[pl.ds(start + 32, 32), lanes] = jnp.where(valid, odd, 0.0).astype(BF16)
        return carry

    lax.fori_loop(0, height, noise_body, 0)

    def signal_body(row, carry):
        for tile in range(4):
            lanes = slice(tile * LANES, (tile + 1) * LANES)
            total = jnp.zeros((32, LANES), F32)
            for i in range(5):
                base = tile * pitch + 8 + (2 * row + i) * PITCH
                for j in range(5):
                    k = 8 + 5 * i + j
                    total = total + taps[k : k + 1, lanes] * column(base, j - 2)
            sg[pl.ds(pl.multiple_of(row * 32, 32), 32), lanes] = total.astype(BF16)
        return carry

    lax.fori_loop(0, height // 2, signal_body, 0)

    for half, field in enumerate((nf, sg)):
        for panel in range(4):
            low = panel * LANES
            block = lax.dot_general(
                field[:, low:], field[:, low : low + LANES], (((0,), (0,)), ((), ())), preferred_element_type=F32
            )
            rows = USED - low
            start = half * PACKED + STARTS[panel]
            block = block[:rows]
            if half == 0 and panel == 3:
                corner = (lax.broadcasted_iota(jnp.int32, block.shape, 0) == 63) & (
                    lax.broadcasted_iota(jnp.int32, block.shape, 1) == 127
                )
                block = jnp.where(corner, count.astype(F32), block)
            out_ref[start : start + rows, :] = block


def front(count, low, x, high, pick, taps):
    height = x.shape[0] // 64
    vmem = pl.BlockSpec(memory_space=pltpu.VMEM)
    return pl.pallas_call(
        front_kernel,
        out_shape=jax.ShapeDtypeStruct((2 * PACKED, LANES), F32),
        in_specs=[pl.BlockSpec(memory_space=pltpu.SMEM)] + [vmem] * 5,
        out_specs=vmem,
        scratch_shapes=[
            pltpu.VMEM((4 * (8 + (height + 3) * PITCH + 8), LANES), F32),
            pltpu.VMEM((40, 512), F32),
            pltpu.VMEM((height * 64, 512), BF16),
            pltpu.VMEM((height * 16, 512), BF16),
        ],
        compiler_params=pltpu.CompilerParams(vmem_limit_bytes=48 << 20),
    )(count, low, x, high, pick, taps)


def scatter_sum(x, axis):
    n = lax.axis_size(axis)
    blocks = x.reshape(n, x.shape[0] // n, x.shape[1])
    me = lax.axis_index(axis)
    total = lax.dynamic_index_in_dim(blocks, me, 0, keepdims=False)
    got = []
    for d in range(1, n):
        piece = lax.dynamic_index_in_dim(blocks, (me + d) % n, 0, keepdims=False)
        got.append(lax.ppermute(piece, axis, [(i, (i + d) % n) for i in range(n)]))
    for piece in got:
        total = total + piece
    return total


def gather_rows(x, axis):
    n = lax.axis_size(axis)
    me = lax.axis_index(axis)
    got = [x] + [lax.ppermute(x, axis, [(i, (i + d) % n) for i in range(n)]) for d in range(1, n)]
    if n == 2:
        return jnp.where(me == 0, jnp.concatenate(got), jnp.concatenate(got[::-1]))
    stacked = jnp.stack(got)
    return jnp.concatenate([lax.dynamic_index_in_dim(stacked, (me - j) % n, 0, keepdims=False) for j in range(n)])


def total_sum(x):
    short = [axis for axis in ("sub", "wide", "narrow") if lax.axis_size(axis) <= 4]
    long = tuple(axis for axis in AXES if axis not in short)
    for axis in short:
        x = scatter_sum(x, axis)
    if long:
        x = lax.psum(x, long)
    for axis in reversed(short):
        x = gather_rows(x, axis)
    return x


def spread(x, row):
    return jnp.broadcast_to(x[row : row + 1, :], (8, LANES))


def inverse_factor(tiles, steps):
    lane = lax.broadcasted_iota(jnp.int32, (8, LANES), 1)
    sub = lax.broadcasted_iota(jnp.int32, (8, LANES), 0)
    tiles = list(tiles)
    for step in range(steps):
        base = step * 8
        inside = (lane >= base) & (lane < base + 8)

        def columns(x):
            return [jnp.broadcast_to(x[:, base + c : base + c + 1], (8, LANES)) for c in range(8)]

        head = tiles[step]
        cols = columns(head)
        head = jnp.where(inside, jnp.where(sub == lane - base, 1.0, 0.0), head)
        rows, inverses, tops = [], [], {}
        pivots = jnp.ones((8, LANES), F32)
        for r in range(8):
            pivot = spread(cols[r], r)
            inverse = 1.0 / pivot
            pivots = jnp.where(sub == r, pivot, pivots)
            row = spread(head, r)
            scale = jnp.where(sub > r, cols[r] * inverse, 0.0)
            rows.append(row)
            inverses.append(inverse)
            head = head - scale * row
            for c in range(r + 1, 8):
                tops[r, c] = spread(cols[c], r)
                cols[c] = cols[c] - scale * tops[r, c]
        tiles[step] = jnp.where(lane <= base + sub, head * lax.rsqrt(pivots), 0.0)
        for m in range(step + 1, len(tiles)):
            tile = tiles[m]
            cols = columns(tile)
            tile = jnp.where(inside, 0.0, tile)
            for r in range(8):
                scale = cols[r] * inverses[r]
                tile = tile - scale * rows[r]
                for c in range(r + 1, 8):
                    cols[c] = cols[c] - scale * tops[r, c]
            tiles[m] = tile
    return tiles


def finish_kernel(sums_ref, pick_ref, start_ref, out_ref, panels, signal, lower, inverse, work, factor):
    pick = pick_ref[...]
    total = 64.0 * sums_ref[PACKED - 1 : PACKED, LANES - 1 : LANES]

    for panel in range(4):
        rows = USED - panel * LANES
        block = sums_ref[STARTS[panel] : STARTS[panel] + rows, :] / total
        if panel == 3:
            r = lax.broadcasted_iota(jnp.int32, block.shape, 0)
            c = lax.broadcasted_iota(jnp.int32, block.shape, 1)
            block = jnp.where((r >= VALID - 384) | (c >= VALID - 384), jnp.where(r == c, 1.0, 0.0), block)
        panels[STARTS[panel] : STARTS[panel] + rows, :] = block

    signal[...] = jnp.zeros_like(signal)
    for panel in range(4):
        low = panel * LANES
        rows = USED - low
        start = PACKED + STARTS[panel]
        signal[low:USED, low : low + LANES] = sums_ref[start : start + rows, :]
        for other in range(panel + 1, 4):
            first = other * LANES
            count = min(LANES, USED - first)
            piece = sums_ref[start + first - low : start + first - low + count, :]
            signal[low : low + LANES, first : first + count] = piece.T
    r = lax.broadcasted_iota(jnp.int32, (64, LANES), 0)
    c = lax.broadcasted_iota(jnp.int32, (64, LANES), 1)
    signal[384:USED, 384:] = jnp.where((r == c) & (r >= VALID - 384), 1.0, signal[384:USED, 384:])

    inverse[...] = jnp.zeros_like(inverse)
    for j in range(4):
        start = STARTS[j]
        low = j * LANES
        size = min(LANES, USED - low)
        tiles = [panels[start + 8 * m : start + 8 * m + 8, :] for m in range(size // 8)]
        tiles = inverse_factor(tiles, 16 if j < 3 else (VALID - 384 + 7) // 8)
        for m, tile in enumerate(tiles):
            inverse[low + 8 * m : low + 8 * m + 8, low : low + LANES] = tile
        own = inverse[low : low + size, low : low + LANES]
        if j > 0:
            inverse[low : low + size, :low] = -mm(own[:, :size], lower[low : low + size, :low])
        rest = USED - low - LANES
        if rest <= 0:
            continue
        below = mm(panels[start + LANES : start + LANES + rest, :], own, ((1,), (1,)))
        work[:rest, :] = below
        for k in range(j + 1, 4):
            skip = (k - j - 1) * LANES
            rows = USED - k * LANES
            size_k = min(LANES, rows)
            update = mm(work[skip:rest, :], work[skip : skip + size_k, :], ((1,), (1,)))
            if size_k < LANES:
                panels[STARTS[k] : STARTS[k] + rows, :size_k] -= update
            else:
                panels[STARTS[k] : STARTS[k] + rows, :] -= update
        gain = mm(work[:rest, :], inverse[low : low + LANES, : low + LANES])
        if j > 0:
            lower[low + LANES : USED, :low] += gain[:, :low]
        lower[low + LANES : USED, low : low + LANES] = gain[:, low:]

    basis = mm(pick.astype(F32), start_ref[...], ((0,), (0,)))[:USED]
    for sweep in range(SWEEPS):
        turned = mm(inverse[...], basis, ((0,), (0,)))
        turned = mm(signal[...], turned)
        mapped = mm(inverse[:, :USED], turned)
        gram = mm(mapped, mapped, ((0,), (0,)))
        tiles = inverse_factor([gram[8 * m : 8 * m + 8, :] for m in range(16)], 16)
        for m, tile in enumerate(tiles):
            factor[8 * m : 8 * m + 8, :] = tile
        basis = mm(mapped, factor[...], ((1,), (1,)))
    weights = mm(inverse[...], basis, ((0,), (0,))).astype(BF16)
    out_ref[...] = jnp.dot(pick, weights, preferred_element_type=F32).astype(BF16)


def finish(sums, pick, start_basis):
    vmem = pl.BlockSpec(memory_space=pltpu.VMEM)
    return pl.pallas_call(
        finish_kernel,
        out_shape=jax.ShapeDtypeStruct((512, LANES), BF16),
        in_specs=[vmem] * 3,
        out_specs=vmem,
        scratch_shapes=[
            pltpu.VMEM((PACKED, LANES), F32),
            pltpu.VMEM((USED, 512), F32),
            pltpu.VMEM((USED, 512), F32),
            pltpu.VMEM((USED, 512), F32),
            pltpu.VMEM((USED, LANES), F32),
            pltpu.VMEM((LANES, LANES), F32),
        ],
        compiler_params=pltpu.CompilerParams(vmem_limit_bytes=48 << 20),
    )(sums, pick, start_basis)


def local(radiance, band_mask, row_counts, noise_kernel, smooth_kernel, start_basis):
    height, across, bands = radiance.shape
    count = row_counts[0]
    chain = 1
    for axis in AXES:
        chain *= lax.axis_size(axis)
    up = [(i, i + 1) for i in range(chain - 1)]
    down = [(i + 1, i) for i in range(chain - 1)]
    row = jnp.arange(height, dtype=jnp.int32)
    zero = jnp.zeros((), radiance.dtype)
    tail = jnp.where((row[-2:] < count)[:, None, None], radiance[-2:], zero)
    lead = jnp.where((row[:1] < count)[:, None, None], radiance[:1], zero)
    low = lax.ppermute(tail.reshape(2 * across, bands), AXES, up)
    high = lax.ppermute(lead.reshape(across, bands), AXES, down)

    order = jnp.arange(bands, dtype=jnp.int32)
    place = jnp.sum(jnp.where(order[None, :] < order[:, None], band_mask[None, :], 0), axis=1)
    pick = ((place[:, None] == order[None, :]) & (band_mask[:, None] == 1)).astype(BF16)
    taps = jnp.concatenate([noise_kernel, smooth_kernel, jnp.zeros((7, bands), F32)])

    flat = radiance.reshape(height * across, bands)
    sums = total_sum(front(row_counts, low, flat, high, pick, taps))
    weights = finish(sums, pick, start_basis)
    keep = jnp.repeat(row < count, across)
    masked = jnp.where(keep[:, None], flat, zero)
    result = jnp.dot(masked, weights, preferred_element_type=F32)
    return result.reshape(height, across, weights.shape[1])


def solution(mesh):
    split = P(("groups",) + AXES)
    return jax.shard_map(
        local,
        mesh=mesh,
        in_specs=(P(("groups",) + AXES, None, None), P(), split, P(), P(), P()),
        out_specs=P(("groups",) + AXES, None, None),
        check_vma=False,
    )
```

time: 498 us -> 109 us (0.22)
  other arithmetic: 173 us -> 6.09 us
  local copies, waits for them, and re-layouts: 141 us -> 1.92 us
  matrix products: 52.7 us -> 1.72 us
  Pallas kernels: 0 us -> 49.9 us
  waiting for transfers between devices: 71.6 us -> 27.6 us
  blocking collectives: 34.7 us -> 0 us
  between operations: 18.1 us -> 0.96 us
  starting transfers between devices: 3.66 us -> 19.9 us
    another operation x27 -> x1, other arithmetic: 165 us -> 0.02 us  [gather_rows(): stacked = jnp.stack(got)]
    slice x29 -> x0, local copies, waits for them, and re-layouts: 128 us -> none  [the longest x25 127 us: filters(): window = framed[row_off:row_off + height:2, col_off:col_off + across:2]]
    psum x1 -> x0, waiting for transfers between devices: 68.8 us -> none  [local(): lax.psum((noise_gram, signal_gram, count_sum), ('wide', 'narrow', 'sub'))]
    pallas_call x0 -> x2, Pallas kernels: none -> 49.9 us  [the longest x1 39.2 us: finish(): pl.pallas_call(finish_kernel, out_shape=jax.ShapeDtypeStruct((512, LANES)...]
    psum x1 -> x0, blocking collectives: 34.7 us -> none  [local(): lax.psum((noise_gram, signal_gram, count_sum), ('wide', 'narrow', 'sub'))]
    dot_general x7 -> x1, matrix products: 33.4 us -> 1.72 us  [local(): result = jnp.dot(masked, weights, preferred_element_type=F32)]
    ppermute x2 -> x12, waiting for transfers between devices: 2.86 us -> 27.6 us  [the longest x5 13.4 us: gather_rows(): lax.ppermute(x, axis, [(i, (i + d) % n) for i in range(n)])]
    another operation x29 -> x0, matrix products: 19.2 us -> none  [the longest x7 5.61 us: project(): jax.scipy.linalg.solve_triangular(lower_noise, basis_now, lower=True, tra...]
  transfers between devices with their start and end apart: 3 -> 12, of which waited for: 2 -> 10; matrix products, arithmetic and copies ran while one was open for 0% -> 3% of each run, Pallas kernels for 0% -> 0%
where the time goes in v1:
time: 109 us; the launch traced here: 108 us
  Pallas kernels  49.9 us (46%)
  waiting for transfers between devices  27.6 us (25%)
  starting transfers between devices  19.9 us (18%)
  other arithmetic  6.09 us (6%)
  local copies, waits for them, and re-layouts  1.92 us (2%)
  matrix products  1.72 us (2%)
    pallas_call x1, Pallas kernels, finish(): pl.pallas_call(finish_kernel, out_shape=jax.ShapeDtypeStruct((512, LANES)...  39.2 us
    ppermute x5, waiting for transfers between devices, gather_rows(): lax.ppermute(x, axis, [(i, (i + d) % n) for i in range(n)])  13.4 us
    ppermute x5, waiting for transfers between devices, scatter_sum(): got.append(lax.ppermute(piece, axis, [(i, (i + d) % n) for i in range(n)]))  12.9 us
    ppermute x5, starting transfers between devices, scatter_sum(): got.append(lax.ppermute(piece, axis, [(i, (i + d) % n) for i in range(n)]))  11.5 us
    pallas_call x1, Pallas kernels, front(): pl.pallas_call(front_kernel, out_shape=jax.ShapeDtypeStruct((2 * PACKED,...  10.7 us
    ppermute x5, starting transfers between devices, gather_rows(): lax.ppermute(x, axis, [(i, (i + d) % n) for i in range(n)])  4.77 us
    ppermute x1, starting transfers between devices, local(): low = lax.ppermute(tail.reshape(2 * across, bands), AXES, up)  2.36 us
  transfers between devices with their start and end apart: 12, of which 10 were waited for; matrix products, arithmetic and copies ran while one was open for 3% of the time, Pallas kernels for 0%

profile of v1, /device:TPU:0, one launch (start us, length us, event | category | flops | bytes accessed | tf_op | source)
XLA Modules:
  0.0 108.1 jit_solution(6822780476660107100)
XLA Ops:
  0.7 0.1 slice_compare_fusion
  0.7 1.0 slice_select_fusion
  1.7 2.4 %collective-permute-start = (bf16[128,512]{1,0:T(8,128)(2,1)S(1)}, bf16[128,512]{1,0:T(8,128)(2,1)S(1)}, u32[]{:S(2)}, u32[]{:S(2)}) collective-permute-start(bf16[128,512]{1,0:T(8,128)(2,1)S(1)} %bitcast.59), channel_id=1, source_target_pairs={{0,1},{1,2},{2,3},{3,4},{4,5},{5,6},{6,7},{7,8},{8,9},{9,10},{10,1... | collective-permute-start | bytes 393224 | tf_op jit(solution)/shard_map/ppermute | solution.py:321
  4.1 0.8 select_bitcast_fusion
  5.0 1.3 %collective-permute-start.1 = (bf16[64,512]{1,0:T(8,128)(2,1)S(1)}, bf16[64,512]{1,0:T(8,128)(2,1)S(1)}, u32[]{:S(2)}, u32[]{:S(2)}) collective-permute-start(bf16[64,512]{1,0:T(8,128)(2,1)S(1)} %select_bitcast_fusion), channel_id=1, source_target_pairs={{1,0},{2,1},{3,2},{4,3},{5,4},{6,5},{7,6},{8,7},{9,8},{10,9},{11,1... | collective-permute-start | bytes 196616 | tf_op jit(solution)/shard_map/ppermute | solution.py:322
  6.3 0.8 select_reduce_fusion
  7.1 0.7 broadcast_compare_fusion
  7.8 0.2 fusion.5.pick_ref
  8.1 0.1 pad.14.clone
  8.1 0.9 maximum_maximum_fusion.taps_ref
  9.0 1.3 %collective-permute-done.1.high_ref = bf16[64,512]{1,0:T(8,128)(2,1)S(1)} collective-permute-done((bf16[64,512]{1,0:T(8,128)(2,1)S(1)}, bf16[64,512]{1,0:T(8,128)(2,1)S(1)}, u32[]{:S(2)}, u32[]{:S(2)}) %collective-permute-start.1) | collective-permute-done | bytes 65568 | tf_op jit(solution)/shard_map/ppermute | solution.py:322
  10.3 0.0 collective-permute-done.low_ref
  10.3 0.0 copy-start
  10.3 1.6 %copy-done = bf16[32,64,512]{2,1,0:T(8,128)(2,1)S(1)} copy-done((bf16[32,64,512]{2,1,0:T(8,128)(2,1)S(1)}, bf16[32,64,512]{2,1,0:T(8,128)(2,1)}, u32[]{:S(2)}) %copy-start) | copy-done | bytes 2097176
  11.9 10.7 %shard_map.64 = f32[2048,128]{1,0:T(8,128)S(1)} custom-call(s32[1]{0:T(128)} %copy.15.count_ref, bf16[128,512]{1,0:T(8,128)(2,1)S(1)} %collective-permute-done.low_ref, bf16[2048,512]{1,0:T(8,128)(2,1)S(1)} %bitcast.53, bf16[64,512]{1,0:T(8,128)(2,1)S(1)} %collective-permute-done.1.high_ref, bf16[512,512]{1,0:T(8,128)(2,1)S(1)} %fusion.5.pick_ref, ...), custom_call_target="tpu_custom_call" | custom-call | tf_op jit(solution)/shard_map/pallas_call | solution.py:120
  22.7 3.0 %collective-permute-start.2 = (f32[1024,128]{1,0:T(8,128)S(1)}, f32[1024,128]{1,0:T(8,128)S(1)}, u32[]{:S(2)}, u32[]{:S(2)}) collective-permute-start(f32[1024,128]{1,0:T(8,128)S(1)} %dynamic-slice_bitcast_fusion), channel_id=1, source_target_pairs={{0,1},{1,0},{2,3},{3,2},{4,5},{5,4},{6,7},{7,6},{8,9},{9,8},{10,11... | collective-permute-start | bytes 1572872 | tf_op jit(solution)/shard_map/ppermute | solution.py:143
  25.7 1.5 %collective-permute-done.2 = f32[1024,128]{1,0:T(8,128)S(1)} collective-permute-done((f32[1024,128]{1,0:T(8,128)S(1)}, f32[1024,128]{1,0:T(8,128)S(1)}, u32[]{:S(2)}, u32[]{:S(2)}) %collective-permute-start.2) | collective-permute-done | bytes 524320 | tf_op jit(solution)/shard_map/ppermute | solution.py:143
  27.2 0.1 bitcast_add_fusion
  27.3 3.8 %collective-permute-start.3 = (f32[512,128]{1,0:T(8,128)S(1)}, f32[512,128]{1,0:T(8,128)S(1)}, u32[]{:S(2)}, u32[]{:S(2)}) collective-permute-start(f32[512,128]{1,0:T(8,128)S(1)} %dynamic-slice_bitcast_fusion.1), channel_id=1, source_target_pairs={{0,8},{8,0},{1,9},{9,1},{2,10},{10,2},{3,11},{11,3},{4,12},{12,4},... | collective-permute-start | bytes 786440 | tf_op jit(solution)/shard_map/ppermute | solution.py:143
  31.1 6.6 %collective-permute-done.3 = f32[512,128]{1,0:T(8,128)S(1)} collective-permute-done((f32[512,128]{1,0:T(8,128)S(1)}, f32[512,128]{1,0:T(8,128)S(1)}, u32[]{:S(2)}, u32[]{:S(2)}) %collective-permute-start.3) | collective-permute-done | bytes 262176 | tf_op jit(solution)/shard_map/ppermute | solution.py:143
  37.8 0.1 collective-permute-start.4
  37.8 4.7 %collective-permute-start.5 = (f32[128,128]{1,0:T(8,128)S(1)}, f32[128,128]{1,0:T(8,128)S(1)}, u32[]{:S(2)}, u32[]{:S(2)}) collective-permute-start(f32[128,128]{1,0:T(8,128)S(1)} %get-tuple-element.17), channel_id=1, source_target_pairs={{0,4},{2,6},{4,0},{6,2},{1,5},{3,7},{5,1},{7,3},{8,12},{10,14},{12... | collective-permute-start | bytes 196616 | tf_op jit(solution)/shard_map/ppermute | solution.py:143
  42.5 0.0 collective-permute-start.6
  42.5 2.5 %collective-permute-done.4 = f32[128,128]{1,0:T(8,128)S(1)} collective-permute-done((f32[128,128]{1,0:T(8,128)S(1)}, f32[128,128]{1,0:T(8,128)S(1)}, u32[]{:S(2)}, u32[]{:S(2)}) %collective-permute-start.4) | collective-permute-done | bytes 65568 | tf_op jit(solution)/shard_map/ppermute | solution.py:143
  45.0 1.7 %collective-permute-done.5 = f32[128,128]{1,0:T(8,128)S(1)} collective-permute-done((f32[128,128]{1,0:T(8,128)S(1)}, f32[128,128]{1,0:T(8,128)S(1)}, u32[]{:S(2)}, u32[]{:S(2)}) %collective-permute-start.5) | collective-permute-done | bytes 65568 | tf_op jit(solution)/shard_map/ppermute | solution.py:143
  46.7 0.6 collective-permute-done.6
  47.3 1.3 %collective-permute-start.7 = (f32[128,128]{1,0:T(8,128)S(1)}, f32[128,128]{1,0:T(8,128)S(1)}, u32[]{:S(2)}, u32[]{:S(2)}) collective-permute-start(f32[128,128]{1,0:T(8,128)S(1)} %fusion.8), channel_id=1, source_target_pairs={{0,2},{2,4},{4,6},{6,0},{1,3},{3,5},{5,7},{7,1},{8,10},{10,12},{12... | collective-permute-start | bytes 196616 | tf_op jit(solution)/shard_map/ppermute | solution.py:152
  48.6 1.7 %collective-permute-start.8 = (f32[128,128]{1,0:T(8,128)S(1)}, f32[128,128]{1,0:T(8,128)S(1)}, u32[]{:S(2)}, u32[]{:S(2)}) collective-permute-start(f32[128,128]{1,0:T(8,128)S(1)} %fusion.8), channel_id=1, source_target_pairs={{0,4},{2,6},{4,0},{6,2},{1,5},{3,7},{5,1},{7,3},{8,12},{10,14},{12... | collective-permute-start | bytes 196616 | tf_op jit(solution)/shard_map/ppermute | solution.py:152
  50.3 0.8 collective-permute-start.9
  51.2 2.6 %collective-permute-done.7 = f32[128,128]{1,0:T(8,128)S(1)} collective-permute-done((f32[128,128]{1,0:T(8,128)S(1)}, f32[128,128]{1,0:T(8,128)S(1)}, u32[]{:S(2)}, u32[]{:S(2)}) %collective-permute-start.7) | collective-permute-done | bytes 65568 | tf_op jit(solution)/shard_map/ppermute | solution.py:152
  53.8 1.7 %collective-permute-done.8 = f32[128,128]{1,0:T(8,128)S(1)} collective-permute-done((f32[128,128]{1,0:T(8,128)S(1)}, f32[128,128]{1,0:T(8,128)S(1)}, u32[]{:S(2)}, u32[]{:S(2)}) %collective-permute-start.8) | collective-permute-done | bytes 65568 | tf_op jit(solution)/shard_map/ppermute | solution.py:152
  55.5 0.0 collective-permute-done.9
  55.7 0.8 collective-permute-start.10
  56.5 7.0 %collective-permute-done.10 = f32[512,128]{1,0:T(8,128)S(1)} collective-permute-done((f32[512,128]{1,0:T(8,128)S(1)}, f32[512,128]{1,0:T(8,128)S(1)}, u32[]{:S(2)}, u32[]{:S(2)}) %collective-permute-start.10) | collective-permute-done | bytes 262176 | tf_op jit(solution)/shard_map/ppermute | solution.py:152
  63.6 0.0 copy-start.2
  63.7 0.1 broadcast_select_fusion
  63.7 0.0 copy-start.1
  63.7 0.1 collective-permute-start.11
  63.8 2.0 %collective-permute-done.11 = f32[1024,128]{1,0:T(8,128)} collective-permute-done((f32[1024,128]{1,0:T(8,128)S(1)}, f32[1024,128]{1,0:T(8,128)}, u32[]{:S(2)}, u32[]{:S(2)}) %collective-permute-start.11) | collective-permute-done | bytes 524320 | tf_op jit(solution)/shard_map/ppermute | solution.py:152
  65.8 1.3 %maximum_select_fusion.sums_ref = f32[2048,128]{1,0:T(8,128)S(1)} fusion(f32[1024,128]{1,0:T(8,128)} %collective-permute-done.11, f32[1024,128]{1,0:T(8,128)S(1)} %broadcast_select_fusion, pred[]{:T(512)S(6)} %eq.34), kind=kLoop, calls=%fused_computation.3 | loop fusion | flops 786432 | bytes 2097153 | tf_op jit(solution)/shard_map/jit(_where)/select_n | solution.py:154
  67.2 0.0 copy-done.2
  67.2 39.2 %shard_map.65 = bf16[512,128]{1,0:T(8,128)(2,1)S(1)} custom-call(f32[2048,128]{1,0:T(8,128)S(1)} %maximum_select_fusion.sums_ref, bf16[512,512]{1,0:T(8,128)(2,1)S(1)} %fusion.5.pick_ref, f32[512,128]{1,0:T(8,128)S(1)} %copy-done.2), custom_call_target="tpu_custom_call" | custom-call | tf_op jit(solution)/shard_map/pallas_call | solution.py:292
  106.4 0.0 copy-done.1
  106.4 1.7 %fusion = f32[32,64,128]{2,1,0:T(8,128)} fusion(bf16[32,64,512]{2,1,0:T(8,128)(2,1)S(1)} %copy-done.1, pred[32]{0:T(512)(128)(4,1)S(1)} %iota_compare_fusion.2, bf16[512,128]{1,0:T(8,128)(2,1)S(1)} %shard_map.65), kind=kOutput, calls=%fused_computation | convolution fusion | flops 269484032 | bytes 3276832 | tf_op jit(solution)/shard_map/dot_general | solution.py:334
  (20 shorter events, 0.3 us)
Async XLA Ops:
  1.7 8.6 %collective-permute-start = (bf16[128,512]{1,0:T(8,128)(2,1)S(1)}, bf16[128,512]{1,0:T(8,128)(2,1)S(1)}, u32[]{:S(2)}, u32[]{:S(2)}) collective-permute-start(bf16[128,512]{1,0:T(8,128)(2,1)S(1)} %bitcast.59), channel_id=1, source_target_pairs={{0,1},{1,2},{2,3},{3,4},{4,5},{5,6},{6,7},{7,8},{8,9},{9,10},{10,1... | collective-permute-start | bytes 393224 | tf_op jit(solution)/shard_map/ppermute | solution.py:321
  5.0 5.3 %collective-permute-start.1 = (bf16[64,512]{1,0:T(8,128)(2,1)S(1)}, bf16[64,512]{1,0:T(8,128)(2,1)S(1)}, u32[]{:S(2)}, u32[]{:S(2)}) collective-permute-start(bf16[64,512]{1,0:T(8,128)(2,1)S(1)} %select_bitcast_fusion), channel_id=1, source_target_pairs={{1,0},{2,1},{3,2},{4,3},{5,4},{6,5},{7,6},{8,7},{9,8},{10,9},{11,1... | collective-permute-start | bytes 196616 | tf_op jit(solution)/shard_map/ppermute | solution.py:322
  10.3 1.6 %copy-start = (bf16[32,64,512]{2,1,0:T(8,128)(2,1)S(1)}, bf16[32,64,512]{2,1,0:T(8,128)(2,1)}, u32[]{:S(2)}) copy-start(bf16[32,64,512]{2,1,0:T(8,128)(2,1)} %param.6) | copy-start | bytes 6291460
  22.7 4.5 %collective-permute-start.2 = (f32[1024,128]{1,0:T(8,128)S(1)}, f32[1024,128]{1,0:T(8,128)S(1)}, u32[]{:S(2)}, u32[]{:S(2)}) collective-permute-start(f32[1024,128]{1,0:T(8,128)S(1)} %dynamic-slice_bitcast_fusion), channel_id=1, source_target_pairs={{0,1},{1,0},{2,3},{3,2},{4,5},{5,4},{6,7},{7,6},{8,9},{9,8},{10,11... | collective-permute-start | bytes 1572872 | tf_op jit(solution)/shard_map/ppermute | solution.py:143
  27.3 10.4 %collective-permute-start.3 = (f32[512,128]{1,0:T(8,128)S(1)}, f32[512,128]{1,0:T(8,128)S(1)}, u32[]{:S(2)}, u32[]{:S(2)}) collective-permute-start(f32[512,128]{1,0:T(8,128)S(1)} %dynamic-slice_bitcast_fusion.1), channel_id=1, source_target_pairs={{0,8},{8,0},{1,9},{9,1},{2,10},{10,2},{3,11},{11,3},{4,12},{12,4},... | collective-permute-start | bytes 786440 | tf_op jit(solution)/shard_map/ppermute | solution.py:143
  37.8 7.2 %collective-permute-start.4 = (f32[128,128]{1,0:T(8,128)S(1)}, f32[128,128]{1,0:T(8,128)S(1)}, u32[]{:S(2)}, u32[]{:S(2)}) collective-permute-start(f32[128,128]{1,0:T(8,128)S(1)} %get-tuple-element.15), channel_id=1, source_target_pairs={{0,2},{2,4},{4,6},{6,0},{1,3},{3,5},{5,7},{7,1},{8,10},{10,12},{12... | collective-permute-start | bytes 196616 | tf_op jit(solution)/shard_map/ppermute | solution.py:143
  37.8 8.8 %collective-permute-start.5 = (f32[128,128]{1,0:T(8,128)S(1)}, f32[128,128]{1,0:T(8,128)S(1)}, u32[]{:S(2)}, u32[]{:S(2)}) collective-permute-start(f32[128,128]{1,0:T(8,128)S(1)} %get-tuple-element.17), channel_id=1, source_target_pairs={{0,4},{2,6},{4,0},{6,2},{1,5},{3,7},{5,1},{7,3},{8,12},{10,14},{12... | collective-permute-start | bytes 196616 | tf_op jit(solution)/shard_map/ppermute | solution.py:143
  42.5 4.8 %collective-permute-start.6 = (f32[128,128]{1,0:T(8,128)S(1)}, f32[128,128]{1,0:T(8,128)S(1)}, u32[]{:S(2)}, u32[]{:S(2)}) collective-permute-start(f32[128,128]{1,0:T(8,128)S(1)} %get-tuple-element.16), channel_id=1, source_target_pairs={{0,6},{2,0},{4,2},{6,4},{1,7},{3,1},{5,3},{7,5},{8,14},{10,8},{12,... | collective-permute-start | bytes 196616 | tf_op jit(solution)/shard_map/ppermute | solution.py:143
  47.3 6.5 %collective-permute-start.7 = (f32[128,128]{1,0:T(8,128)S(1)}, f32[128,128]{1,0:T(8,128)S(1)}, u32[]{:S(2)}, u32[]{:S(2)}) collective-permute-start(f32[128,128]{1,0:T(8,128)S(1)} %fusion.8), channel_id=1, source_target_pairs={{0,2},{2,4},{4,6},{6,0},{1,3},{3,5},{5,7},{7,1},{8,10},{10,12},{12... | collective-permute-start | bytes 196616 | tf_op jit(solution)/shard_map/ppermute | solution.py:152
  48.6 6.9 %collective-permute-start.8 = (f32[128,128]{1,0:T(8,128)S(1)}, f32[128,128]{1,0:T(8,128)S(1)}, u32[]{:S(2)}, u32[]{:S(2)}) collective-permute-start(f32[128,128]{1,0:T(8,128)S(1)} %fusion.8), channel_id=1, source_target_pairs={{0,4},{2,6},{4,0},{6,2},{1,5},{3,7},{5,1},{7,3},{8,12},{10,14},{12... | collective-permute-start | bytes 196616 | tf_op jit(solution)/shard_map/ppermute | solution.py:152
  50.3 5.2 %collective-permute-start.9 = (f32[128,128]{1,0:T(8,128)S(1)}, f32[128,128]{1,0:T(8,128)S(1)}, u32[]{:S(2)}, u32[]{:S(2)}) collective-permute-start(f32[128,128]{1,0:T(8,128)S(1)} %fusion.8), channel_id=1, source_target_pairs={{0,6},{2,0},{4,2},{6,4},{1,7},{3,1},{5,3},{7,5},{8,14},{10,8},{12,... | collective-permute-start | bytes 196616 | tf_op jit(solution)/shard_map/ppermute | solution.py:152
  55.7 7.8 %collective-permute-start.10 = (f32[512,128]{1,0:T(8,128)S(1)}, f32[512,128]{1,0:T(8,128)S(1)}, u32[]{:S(2)}, u32[]{:S(2)}) collective-permute-start(f32[512,128]{1,0:T(8,128)S(1)} %pad_maximum_fusion.1), channel_id=1, source_target_pairs={{0,8},{8,0},{1,9},{9,1},{2,10},{10,2},{3,11},{11,3},{4,12},{12,4},... | collective-permute-start | bytes 786440 | tf_op jit(solution)/shard_map/ppermute | solution.py:152
  63.6 3.6 %copy-start.2 = (f32[512,128]{1,0:T(8,128)S(1)}, f32[512,128]{1,0:T(8,128)}, u32[]{:S(2)}) copy-start(f32[512,128]{1,0:T(8,128)} %start_ref.1) | copy-start | bytes 786436
  63.7 42.7 %copy-start.1 = (bf16[32,64,512]{2,1,0:T(8,128)(2,1)S(1)}, bf16[32,64,512]{2,1,0:T(8,128)(2,1)}, u32[]{:S(2)}) copy-start(bf16[32,64,512]{2,1,0:T(8,128)(2,1)} %param.6) | copy-start | bytes 6291460
  63.7 2.1 %collective-permute-start.11 = (f32[1024,128]{1,0:T(8,128)S(1)}, f32[1024,128]{1,0:T(8,128)}, u32[]{:S(2)}, u32[]{:S(2)}) collective-permute-start(f32[1024,128]{1,0:T(8,128)S(1)} %broadcast_select_fusion), channel_id=1, source_target_pairs={{0,1},{1,0},{2,3},{3,2},{4,5},{5,4},{6,7},{7,6},{8,9},{9,8},{10,11... | collective-permute-start | bytes 1572872 | tf_op jit(solution)/shard_map/ppermute | solution.py:152

commit v2 on v1

v2 whole, which is shorter than its diff:
```python
import jax
import jax.numpy as jnp
from jax import lax
from jax.experimental import pallas as pl
from jax.experimental.pallas import tpu as pltpu
from jax.sharding import PartitionSpec as P

SWEEPS = 2
VALID = 425
AXES = ("wide", "narrow", "sub")
LANES = 128
USED = 432
PACKED = 832
SQUARE, THIRD, LAST = 0, 128, 256
BELOW = (304, 608, 784)
PITCH = 72
GROUP = 8
HIGH = lax.Precision.HIGHEST
F32 = jnp.float32
BF16 = jnp.bfloat16


def mm(a, b, dims=((1,), (0,))):
    return lax.dot_general(a, b, (dims, ((), ())), precision=HIGH, preferred_element_type=F32)


def front_kernel(count_ref, low_ref, x_ref, high_ref, pick_ref, taps_ref, keep_ref, send_ref, xs, taps, nf, sg):
    height = x_ref.shape[0] // 64
    count = count_ref[0]
    pitch = xs.shape[0] // 4
    taps[...] = mm(taps_ref[...], pick_ref[...].astype(F32))
    xs[...] = jnp.zeros_like(xs)
    pick = pick_ref[...]

    def place(block, first_row, limit):
        values = jnp.dot(block, pick, preferred_element_type=F32)
        for k in range(block.shape[0] // 64):
            row = first_row + k
            piece = values[k * 64 : (k + 1) * 64]
            if limit is not None:
                piece = jnp.where(row < limit, piece, 0.0)
            start = pl.multiple_of(8 + (row + 2) * PITCH, 8)
            for tile in range(4):
                xs[pl.ds(start + tile * pitch, 64), :] = piece[:, tile * LANES : (tile + 1) * LANES]

    place(low_ref[...], -2, None)
    place(high_ref[...], height, None)

    def place_body(chunk, carry):
        place(x_ref[pl.ds(pl.multiple_of(chunk * 256, 256), 256), :], chunk * 4, count)
        return carry

    lax.fori_loop(0, height // 4, place_body, 0)

    def column(base, offset):
        return xs[pl.ds(base + offset, 32, stride=2), :]

    def noise_body(row, carry):
        valid = row < count
        for tile in range(4):
            lanes = slice(tile * LANES, (tile + 1) * LANES)
            tap = lambda k: taps[k : k + 1, lanes]
            even = odd = None
            for index, row_off in enumerate((-1, 0, 1)):
                base = tile * pitch + 8 + (row + 2 + row_off) * PITCH
                here_even = column(base, 0)
                next_even = column(base, 2)
                prev_odd = column(base, -1)
                here_odd = column(base, 1)
                if row_off == 0:
                    left, right = tap(3), tap(4)
                    part_even = here_even - left * prev_odd - right * here_odd
                    part_odd = here_odd - left * here_even - right * next_even
                else:
                    first = 0 if row_off == -1 else 5
                    left, mid, right = tap(first), tap(first + 1), tap(first + 2)
                    part_even = -(left * prev_odd + mid * here_even + right * here_odd)
                    part_odd = -(left * here_even + mid * here_odd + right * next_even)
                even = part_even if even is None else even + part_even
                odd = part_odd if odd is None else odd + part_odd
            start = pl.multiple_of(row * 64, 64)
            nf[pl.ds(start, 32), lanes] = jnp.where(valid, even, 0.0).astype(BF16)
            nf[pl.ds(start + 32, 32), lanes] = jnp.where(valid, odd, 0.0).astype(BF16)
        return carry

    lax.fori_loop(0, height, noise_body, 0)

    def signal_body(row, carry):
        for tile in range(4):
            lanes = slice(tile * LANES, (tile + 1) * LANES)
            total = jnp.zeros((32, LANES), F32)
            for i in range(5):
                base = tile * pitch + 8 + (2 * row + i) * PITCH
                for j in range(5):
                    k = 8 + 5 * i + j
                    total = total + taps[k : k + 1, lanes] * column(base, j - 2)
            sg[pl.ds(pl.multiple_of(row * 32, 32), 32), lanes] = total.astype(BF16)
        return carry

    lax.fori_loop(0, height // 2, signal_body, 0)

    r = lax.broadcasted_iota(jnp.int32, (LANES, LANES), 0)
    c = lax.broadcasted_iota(jnp.int32, (LANES, LANES), 1)
    for half, field in enumerate((nf, sg)):

        def put(start, block):
            @pl.when(count_ref[1] == half)
            def _():
                keep_ref[start : start + block.shape[0], :] = block

            @pl.when(count_ref[1] != half)
            def _():
                send_ref[start : start + block.shape[0], :] = block

        corners = []
        for panel in range(4):
            low = panel * LANES
            block = lax.dot_general(
                field[:, low:], field[:, low : low + LANES], (((0,), (0,)), ((), ())), preferred_element_type=F32
            )
            corners.append(block[:LANES])
            if panel < 3:
                put(BELOW[panel], block[LANES : USED - low])
        put(SQUARE, jnp.where(r >= c, corners[0], corners[1]))
        put(THIRD, corners[2])
        diagonal = jnp.sum(jnp.where(r == c, corners[1], 0.0), axis=0, keepdims=True)
        tail = corners[3][: USED - 384]
        row = lax.broadcasted_iota(jnp.int32, tail.shape, 0)
        tail = jnp.where(row == 47, diagonal, jnp.where(row == 46, count.astype(F32), tail))
        put(LAST, tail)


def front(count, low, x, high, pick, taps):
    height = x.shape[0] // 64
    vmem = pl.BlockSpec(memory_space=pltpu.VMEM)
    return pl.pallas_call(
        front_kernel,
        out_shape=(jax.ShapeDtypeStruct((PACKED, LANES), F32),) * 2,
        in_specs=[pl.BlockSpec(memory_space=pltpu.SMEM)] + [vmem] * 5,
        out_specs=(vmem, vmem),
        scratch_shapes=[
            pltpu.VMEM((4 * (8 + (height + 3) * PITCH + 8), LANES), F32),
            pltpu.VMEM((40, 512), F32),
            pltpu.VMEM((height * 64, 512), BF16),
            pltpu.VMEM((height * 16, 512), BF16),
        ],
        compiler_params=pltpu.CompilerParams(vmem_limit_bytes=48 << 20),
    )(count, low, x, high, pick, taps)


def scatter_sum(x, axis):
    n = lax.axis_size(axis)
    blocks = x.reshape(n, x.shape[0] // n, x.shape[1])
    me = lax.axis_index(axis)
    total = lax.dynamic_index_in_dim(blocks, me, 0, keepdims=False)
    got = []
    for d in range(1, n):
        piece = lax.dynamic_index_in_dim(blocks, (me + d) % n, 0, keepdims=False)
        got.append(lax.ppermute(piece, axis, [(i, (i + d) % n) for i in range(n)]))
    for piece in got:
        total = total + piece
    return total


def gather_rows(x, axis):
    n = lax.axis_size(axis)
    me = lax.axis_index(axis)
    got = [x] + [lax.ppermute(x, axis, [(i, (i + d) % n) for i in range(n)]) for d in range(1, n)]
    if n == 2:
        return jnp.where(me == 0, jnp.concatenate(got), jnp.concatenate(got[::-1]))
    stacked = jnp.stack(got)
    return jnp.concatenate([lax.dynamic_index_in_dim(stacked, (me - j) % n, 0, keepdims=False) for j in range(n)])


def exchange(x):
    return lax.ppermute(x, "sub", [(0, 1), (1, 0)])


def total_sum(keep, send):
    x = keep + exchange(send)
    short = [axis for axis in ("wide", "narrow") if lax.axis_size(axis) <= 4]
    long = tuple(axis for axis in ("wide", "narrow") if axis not in short)
    for axis in short:
        x = scatter_sum(x, axis)
    if long:
        x = lax.psum(x, long)
    for axis in reversed(short):
        x = gather_rows(x, axis)
    return x, exchange(x)


def spread(x, row):
    return jnp.broadcast_to(x[row : row + 1, :], (8, LANES))


def three_parts(x):
    high = x.astype(BF16).astype(F32)
    rest = x - high
    mid = rest.astype(BF16).astype(F32)
    return high, mid, rest - mid


def inverse_factor(tiles):
    lane = lax.broadcasted_iota(jnp.int32, (8, LANES), 1)
    sub = lax.broadcasted_iota(jnp.int32, (8, LANES), 0)
    tiles = list(tiles)
    count = len(tiles)
    for first in range(0, count, GROUP):
        last = min(first + GROUP, count)
        ahead = None
        done = []
        for step in range(first, last):
            base = step * 8
            inside = (lane >= base) & (lane < base + 8)

            def columns(x, start):
                return [jnp.broadcast_to(x[:, start + c : start + c + 1], (8, LANES)) for c in range(8)]

            head = tiles[step]
            cols = columns(head, base) if ahead is None else ahead
            head = jnp.where(inside, jnp.where(sub == lane - base, 1.0, 0.0), head)
            pivots = jnp.ones((8, LANES), F32)
            pairs = []
            for r in (0, 2, 4, 6):
                q = r + 1
                a, b, c = spread(cols[r], r), spread(cols[q], r), spread(cols[q], q)
                det = a * c - b * b
                inv = 1.0 / det
                ai, bi, ci = a * inv, b * inv, c * inv
                u, v = cols[r], cols[q]
                below = sub > q
                alpha = jnp.where(below, u * ci - v * bi, 0.0)
                beta = jnp.where(below, v * ai - u * bi, 0.0)
                row_r, row_q = spread(head, r), spread(head, q)
                tops = {}
                for k in range(q + 1, 8):
                    tops[k] = (spread(cols[k], r), spread(cols[k], q))
                    cols[k] = cols[k] - alpha * tops[k][0] - beta * tops[k][1]
                ainv = 1.0 / a
                head = head - (alpha + jnp.where(sub == q, b * ainv, 0.0)) * row_r - beta * row_q
                pivots = jnp.where(sub == r, a, jnp.where(sub == q, det * ainv, pivots))
                pairs.append((r, ai, bi, ci, row_r, row_q, tops))
            scaled = head * lax.rsqrt(pivots)
            own = lane <= base + sub
            tiles[step] = jnp.where(own, scaled, 0.0)
            done.append((scaled, jnp.where(own | (lane >= last * 8), scaled, 0.0)))
            ahead = None
            for m in range(step + 1, last):
                tile = tiles[m]
                cols = columns(tile, base)
                if m == step + 1:
                    ahead = columns(tile, base + 8)
                tile = jnp.where(inside, 0.0, tile)
                for r, ai, bi, ci, row_r, row_q, tops in pairs:
                    u, v = cols[r], cols[r + 1]
                    alpha = u * ci - v * bi
                    beta = v * ai - u * bi
                    tile = tile - alpha * row_r - beta * row_q
                    for k in tops:
                        cols[k] = cols[k] - alpha * tops[k][0] - beta * tops[k][1]
                    if m == step + 1:
                        for c in range(8):
                            ahead[c] = ahead[c] - alpha * spread(u, c) - beta * spread(v, c)
                tiles[m] = tile
        if last < count:
            far = lane >= 8 * last
            keep = far | (lane < 8 * first)
            left = three_parts(jnp.concatenate([jnp.where(far, x, 0.0) for x, _ in done], axis=0))
            right = three_parts(jnp.concatenate([y for _, y in done], axis=0))
            left = jnp.concatenate([left[k] for k in (0, 0, 1, 0, 1, 2)], axis=0).astype(BF16)
            right = jnp.concatenate([right[k] for k in (0, 1, 0, 2, 1, 0)], axis=0).astype(BF16)
            update = lax.dot_general(left, right, (((0,), (0,)), ((), ())), preferred_element_type=F32)
            for m in range(last, count):
                tiles[m] = jnp.where(keep, tiles[m], 0.0) - update[8 * m : 8 * m + 8]
    return tiles


def factor_block(block):
    tiles = [block[8 * m : 8 * m + 8, :] for m in range(block.shape[0] // 8)]
    return jnp.concatenate(inverse_factor(tiles), axis=0)


def widen(x, width):
    return jnp.concatenate([x, jnp.zeros((x.shape[0], width - x.shape[1]), x.dtype)], axis=1)


def unpack(sums, start):
    r = lax.broadcasted_iota(jnp.int32, (LANES, LANES), 0)
    c = lax.broadcasted_iota(jnp.int32, (LANES, LANES), 1)
    part = lambda first, rows: sums[pl.ds(start + first, rows), :]
    square = part(SQUARE, LANES)
    turned = square.T
    corner = jnp.where(r >= c, square, turned)
    second = jnp.where(r == c, part(LAST + 47, 1), jnp.where(r < c, square, turned))
    blocks = [
        (corner, part(BELOW[0], USED - 128)),
        (second, part(BELOW[1], USED - 256)),
        (part(THIRD, LANES), part(BELOW[2], USED - 384)),
    ]
    return [jnp.concatenate(pair, axis=0) for pair in blocks] + [part(LAST, USED - 384)]


def fill_unit(block):
    r = lax.broadcasted_iota(jnp.int32, block.shape, 0)
    c = lax.broadcasted_iota(jnp.int32, block.shape, 1)
    return jnp.where((r >= VALID - 384) | (c >= VALID - 384), jnp.where(r == c, 1.0, 0.0), block)


def finish_kernel(side_ref, mine_ref, other_ref, pick_ref, start_ref, out_ref, sums, signal, inverse):
    side = side_ref[0]
    sums[pl.ds(pl.multiple_of(side * PACKED, 8), PACKED), :] = mine_ref[...]
    sums[pl.ds(pl.multiple_of((1 - side) * PACKED, 8), PACKED), :] = other_ref[...]

    signal[...] = jnp.zeros_like(signal)
    panels = unpack(sums, PACKED)
    panels[3] = fill_unit(panels[3])
    for panel in range(4):
        low = panel * LANES
        signal[low:USED, low : low + LANES] = panels[panel]
        for other in range(panel + 1, 4):
            first = other * LANES
            size = min(LANES, USED - first)
            signal[low : low + LANES, first : first + size] = panels[panel][first - low : first - low + size].T
    basis = mm(start_ref[...], pick_ref[...].astype(F32), ((0,), (0,)))[:, :USED]

    total = 64.0 * sums[LAST + 46 : LAST + 47, :]
    panels = [block / total for block in unpack(sums, 0)]
    panels[3] = fill_unit(panels[3])
    inverse[...] = jnp.zeros_like(inverse)
    known = None
    for j in range(4):
        low = j * LANES
        size = min(LANES, USED - low)
        own = factor_block(panels[j][:size])
        inverse[low : low + size, low : low + LANES] = own
        if j == 3:
            inverse[low:USED, :low] = -mm(own[:, :size], known)
            break
        below = mm(panels[j][LANES:], own, ((1,), (1,)))
        for k in range(j + 1, 4):
            skip = (k - j - 1) * LANES
            width = min(LANES, USED - k * LANES)
            update = mm(below[skip:], below[skip : skip + width], ((1,), (1,)))
            panels[k] = panels[k] - (update if width == LANES else widen(update, LANES))
        gain = mm(below, own)
        if j == 0:
            known = gain
        else:
            left = -mm(own, known[:LANES])
            inverse[low : low + LANES, :low] = left
            known = jnp.concatenate([known[LANES:] + mm(below, left), gain], axis=1)

    turned = mm(basis, inverse[...])
    mapped = mm(mm(turned[:, :USED], signal[...]), inverse[...], ((1,), (1,)))
    for sweep in range(SWEEPS):
        square = mm(mapped, mapped, ((1,), (1,)))
        turned = mm(mapped, inverse[...])
        if sweep + 1 < SWEEPS:
            ahead = mm(mm(turned[:, :USED], signal[...]), inverse[...], ((1,), (1,)))
        scale = factor_block(square)
        if sweep + 1 < SWEEPS:
            mapped = mm(scale, ahead)
    weights = mm(scale, turned).astype(BF16)
    out_ref[...] = lax.dot_general(
        pick_ref[...], weights, (((1,), (1,)), ((), ())), preferred_element_type=F32
    ).astype(BF16)


def finish(side, mine, other, pick, start_basis):
    vmem = pl.BlockSpec(memory_space=pltpu.VMEM)
    return pl.pallas_call(
        finish_kernel,
        out_shape=jax.ShapeDtypeStruct((512, LANES), BF16),
        in_specs=[pl.BlockSpec(memory_space=pltpu.SMEM)] + [vmem] * 4,
        out_specs=vmem,
        scratch_shapes=[
            pltpu.VMEM((2 * PACKED, LANES), F32),
            pltpu.VMEM((USED, 512), F32),
            pltpu.VMEM((USED, 512), F32),
        ],
        compiler_params=pltpu.CompilerParams(vmem_limit_bytes=48 << 20),
    )(side, mine, other, pick, start_basis)


def local(radiance, band_mask, row_counts, noise_kernel, smooth_kernel, start_basis):
    height, across, bands = radiance.shape
    count = row_counts[0]
    chain = 1
    for axis in AXES:
        chain *= lax.axis_size(axis)
    up = [(i, i + 1) for i in range(chain - 1)]
    down = [(i + 1, i) for i in range(chain - 1)]
    row = jnp.arange(height, dtype=jnp.int32)
    zero = jnp.zeros((), radiance.dtype)
    tail = jnp.where((row[-2:] < count)[:, None, None], radiance[-2:], zero)
    lead = jnp.where((row[:1] < count)[:, None, None], radiance[:1], zero)
    low = lax.ppermute(tail.reshape(2 * across, bands), AXES, up)
    high = lax.ppermute(lead.reshape(across, bands), AXES, down)

    order = jnp.arange(bands, dtype=jnp.int32)
    place = jnp.sum(jnp.where(order[None, :] < order[:, None], band_mask[None, :], 0), axis=1)
    pick = ((place[:, None] == order[None, :]) & (band_mask[:, None] == 1)).astype(BF16)
    taps = jnp.concatenate([noise_kernel, smooth_kernel, jnp.zeros((7, bands), F32)])

    flat = radiance.reshape(height * across, bands)
    side = lax.axis_index("sub").astype(jnp.int32)
    keep, send = front(jnp.stack([count, side]), low, flat, high, pick, taps)
    mine, other = total_sum(keep, send)
    weights = finish(side[None], mine, other, pick, start_basis)
    keep = jnp.repeat(row < count, across)
    masked = jnp.where(keep[:, None], flat, zero)
    result = jnp.dot(masked, weights, preferred_element_type=F32)
    return result.reshape(height, across, weights.shape[1])


def solution(mesh):
    split = P(("groups",) + AXES)
    return jax.shard_map(
        local,
        mesh=mesh,
        in_specs=(P(("groups",) + AXES, None, None), P(), split, P(), P(), P()),
        out_specs=P(("groups",) + AXES, None, None),
        check_vma=False,
    )
```

time: 109 us -> 92.4 us (0.85)
  Pallas kernels: 49.9 us -> 35 us
  waiting for transfers between devices: 27.6 us -> 23.6 us
  starting transfers between devices: 19.9 us -> 22.5 us
    pallas_call x1, Pallas kernels: 39.2 us -> 21.1 us  [finish(): pl.pallas_call(finish_kernel, out_shape=jax.ShapeDtypeStruct((512, LANES)...]
    ppermute x5 -> x4, waiting for transfers between devices: 13.4 us -> 9.61 us  [gather_rows(): lax.ppermute(x, axis, [(i, (i + d) % n) for i in range(n)])]
    pallas_call x1, Pallas kernels: 10.7 us -> 13.9 us  [front(): pl.pallas_call(front_kernel, out_shape=(jax.ShapeDtypeStruct((PACKED, LAN...]
    ppermute x0 -> x2, waiting for transfers between devices: none -> 3.14 us  [exchange(): return lax.ppermute(x, 'sub', [(0, 1), (1, 0)])]
    ppermute x0 -> x2, starting transfers between devices: none -> 2.78 us  [exchange(): return lax.ppermute(x, 'sub', [(0, 1), (1, 0)])]
    ppermute x5 -> x4, waiting for transfers between devices: 12.9 us -> 10.8 us  [scatter_sum(): got.append(lax.ppermute(piece, axis, [(i, (i + d) % n) for i in range(n)]))]
    select_n x2 -> x1, other arithmetic: 1.38 us -> 0.05 us  [gather_rows(): return jnp.where(me == 0, jnp.concatenate(got), jnp.concatenate(got[::-1]))]
    ppermute x1, waiting for transfers between devices: 1.28 us -> 0.01 us  [local(): high = lax.ppermute(lead.reshape(across, bands), AXES, down)]
  transfers between devices with their start and end apart: 12 -> 12, of which waited for: 10 -> 8; matrix products, arithmetic and copies ran while one was open for 3% -> 4% of each run, Pallas kernels for 0% -> 0%
where the time goes in v2:
time: 92.4 us; the launch traced here: 92 us
  Pallas kernels  35 us (38%)
  waiting for transfers between devices  23.6 us (26%)
  starting transfers between devices  22.5 us (24%)
  other arithmetic  5.49 us (6%)
  local copies, waits for them, and re-layouts  2.78 us (3%)
  matrix products  1.72 us (2%)
    pallas_call x1, Pallas kernels, finish(): pl.pallas_call(finish_kernel, out_shape=jax.ShapeDtypeStruct((512, LANES)...  21.1 us
    pallas_call x1, Pallas kernels, front(): pl.pallas_call(front_kernel, out_shape=(jax.ShapeDtypeStruct((PACKED, LAN...  13.9 us
    ppermute x4, starting transfers between devices, scatter_sum(): got.append(lax.ppermute(piece, axis, [(i, (i + d) % n) for i in range(n)]))  11.3 us
    ppermute x4, waiting for transfers between devices, scatter_sum(): got.append(lax.ppermute(piece, axis, [(i, (i + d) % n) for i in range(n)]))  10.8 us
    ppermute x4, waiting for transfers between devices, gather_rows(): lax.ppermute(x, axis, [(i, (i + d) % n) for i in range(n)])  9.61 us
    ppermute x4, starting transfers between devices, gather_rows(): lax.ppermute(x, axis, [(i, (i + d) % n) for i in range(n)])  4.08 us
    ppermute x2, waiting for transfers between devices, exchange(): return lax.ppermute(x, 'sub', [(0, 1), (1, 0)])  3.14 us
    ppermute x1, starting transfers between devices, local(): low = lax.ppermute(tail.reshape(2 * across, bands), AXES, up)  3.04 us
  transfers between devices with their start and end apart: 12, of which 8 were waited for; matrix products, arithmetic and copies ran while one was open for 4% of the time, Pallas kernels for 0%

profile of v2, /device:TPU:0, one launch (start us, length us, event | category | flops | bytes accessed | tf_op | source)
XLA Modules:
  0.0 92.0 jit_solution(6909567154729071836)
XLA Ops:
  0.7 0.8 select_bitcast_fusion
  1.6 1.3 %collective-permute-start.1 = (bf16[64,512]{1,0:T(8,128)(2,1)S(1)}, bf16[64,512]{1,0:T(8,128)(2,1)S(1)}, u32[]{:S(2)}, u32[]{:S(2)}) collective-permute-start(bf16[64,512]{1,0:T(8,128)(2,1)S(1)} %select_bitcast_fusion), channel_id=1, source_target_pairs={{1,0},{2,1},{3,2},{4,3},{5,4},{6,5},{7,6},{8,7},{9,8},{10,9},{11,1... | collective-permute-start | bytes 196616 | tf_op jit(solution)/shard_map/ppermute | solution.py:398
  2.9 0.1 slice_compare_fusion
  2.9 1.0 %slice_select_fusion = bf16[2,64,512]{2,1,0:T(8,128)(2,1)S(1)} fusion(bf16[32,64,512]{2,1,0:T(8,128)(2,1)} %param.6, pred[2]{0:T(512)(128)(4,1)S(1)} %slice_compare_fusion), kind=kLoop, calls=%fused_computation.15 | loop fusion | flops 65536 | bytes 262146 | tf_op jit(solution)/shard_map/jit(_where)/select_n | solution.py:395
  3.9 3.0 %collective-permute-start = (bf16[128,512]{1,0:T(8,128)(2,1)S(1)}, bf16[128,512]{1,0:T(8,128)(2,1)S(1)}, u32[]{:S(2)}, u32[]{:S(2)}) collective-permute-start(bf16[128,512]{1,0:T(8,128)(2,1)S(1)} %bitcast.53), channel_id=1, source_target_pairs={{0,1},{1,2},{2,3},{3,4},{4,5},{5,6},{6,7},{7,8},{8,9},{9,10},{10,1... | collective-permute-start | bytes 393224 | tf_op jit(solution)/shard_map/ppermute | solution.py:397
  7.0 0.7 broadcast_compare_fusion
  7.6 0.8 select_reduce_fusion
  8.5 0.1 pad.10.clone
  8.6 0.2 fusion.5.pick_ref
  8.8 0.9 maximum_maximum_fusion.taps_ref
  9.7 0.1 pad_add_fusion.count_ref
  9.8 0.0 collective-permute-done.1.high_ref
  9.8 0.0 collective-permute-done.low_ref
  9.8 0.0 copy-start
  9.8 1.6 %copy-done = bf16[32,64,512]{2,1,0:T(8,128)(2,1)S(1)} copy-done((bf16[32,64,512]{2,1,0:T(8,128)(2,1)S(1)}, bf16[32,64,512]{2,1,0:T(8,128)(2,1)}, u32[]{:S(2)}) %copy-start) | copy-done | bytes 2097176
  11.4 13.9 %shard_map.64 = (f32[832,128]{1,0:T(8,128)S(1)}, f32[832,128]{1,0:T(8,128)S(1)}) custom-call(s32[2]{0:T(128)S(1)} %pad_add_fusion.count_ref, bf16[128,512]{1,0:T(8,128)(2,1)S(1)} %collective-permute-done.low_ref, bf16[2048,512]{1,0:T(8,128)(2,1)S(1)} %bitcast.47, bf16[64,512]{1,0:T(8,128)(2,1)S(1)} %collective-permute-done.1.high_ref, ...), custom_call_target="tpu_custom_call" | custom-call | tf_op jit(solution)/shard_map/pallas_call | solution.py:136
  25.3 2.7 %collective-permute-start.2 = (f32[832,128]{1,0:T(8,128)S(1)}, f32[832,128]{1,0:T(8,128)S(1)}, u32[]{:S(2)}, u32[]{:S(2)}) collective-permute-start(f32[832,128]{1,0:T(8,128)S(1)} %get-tuple-element.8), channel_id=1, source_target_pairs={{0,1},{1,0},{2,3},{3,2},{4,5},{5,4},{6,7},{7,6},{8,9},{9,8},{10,11... | collective-permute-start | bytes 1277960 | tf_op jit(solution)/shard_map/ppermute | solution.py:176
  28.0 1.4 %collective-permute-done.2 = f32[832,128]{1,0:T(8,128)S(1)} collective-permute-done((f32[832,128]{1,0:T(8,128)S(1)}, f32[832,128]{1,0:T(8,128)S(1)}, u32[]{:S(2)}, u32[]{:S(2)}) %collective-permute-start.2) | collective-permute-done | bytes 426016 | tf_op jit(solution)/shard_map/ppermute | solution.py:176
  29.5 7.5 %collective-permute-start.3 = (f32[416,128]{1,0:T(8,128)S(1)}, f32[416,128]{1,0:T(8,128)S(1)}, u32[]{:S(2)}, u32[]{:S(2)}) collective-permute-start(f32[416,128]{1,0:T(8,128)S(1)} %dynamic-slice_bitcast_fusion), channel_id=1, source_target_pairs={{0,8},{8,0},{1,9},{9,1},{2,10},{10,2},{3,11},{11,3},{4,12},{12,4},... | collective-permute-start | bytes 638984 | tf_op jit(solution)/shard_map/ppermute | solution.py:159
  37.0 5.6 %collective-permute-done.3 = f32[416,128]{1,0:T(8,128)S(1)} collective-permute-done((f32[416,128]{1,0:T(8,128)S(1)}, f32[416,128]{1,0:T(8,128)S(1)}, u32[]{:S(2)}, u32[]{:S(2)}) %collective-permute-start.3) | collective-permute-done | bytes 213024 | tf_op jit(solution)/shard_map/ppermute | solution.py:159
  42.6 0.1 collective-permute-start.4
  42.7 3.8 %collective-permute-start.6 = (f32[104,128]{1,0:T(8,128)S(1)}, f32[104,128]{1,0:T(8,128)S(1)}, u32[]{:S(2)}, u32[]{:S(2)}) collective-permute-start(f32[104,128]{1,0:T(8,128)S(1)} %get-tuple-element.20), channel_id=1, source_target_pairs={{0,6},{2,0},{4,2},{6,4},{1,7},{3,1},{5,3},{7,5},{8,14},{10,8},{12,... | collective-permute-start | bytes 159752 | tf_op jit(solution)/shard_map/ppermute | solution.py:159
  46.5 0.0 collective-permute-start.5
  46.5 0.0 copy-start.2
  46.5 2.5 %collective-permute-done.4 = f32[104,128]{1,0:T(8,128)S(1)} collective-permute-done((f32[104,128]{1,0:T(8,128)S(1)}, f32[104,128]{1,0:T(8,128)S(1)}, u32[]{:S(2)}, u32[]{:S(2)}) %collective-permute-start.4) | collective-permute-done | bytes 53280 | tf_op jit(solution)/shard_map/ppermute | solution.py:159
  48.9 0.0 collective-permute-done.6
  48.9 2.8 %collective-permute-done.5 = f32[104,128]{1,0:T(8,128)S(1)} collective-permute-done((f32[104,128]{1,0:T(8,128)S(1)}, f32[104,128]{1,0:T(8,128)S(1)}, u32[]{:S(2)}, u32[]{:S(2)}) %collective-permute-start.5) | collective-permute-done | bytes 53280 | tf_op jit(solution)/shard_map/ppermute | solution.py:159
  51.8 1.3 %collective-permute-start.9 = (f32[104,128]{1,0:T(8,128)S(1)}, f32[104,128]{1,0:T(8,128)S(1)}, u32[]{:S(2)}, u32[]{:S(2)}) collective-permute-start(f32[104,128]{1,0:T(8,128)S(1)} %fusion.8), channel_id=1, source_target_pairs={{0,6},{2,0},{4,2},{6,4},{1,7},{3,1},{5,3},{7,5},{8,14},{10,8},{12,... | collective-permute-start | bytes 159752 | tf_op jit(solution)/shard_map/ppermute | solution.py:168
  53.1 0.0 collective-permute-start.8
  53.1 1.0 %collective-permute-start.7 = (f32[104,128]{1,0:T(8,128)S(1)}, f32[104,128]{1,0:T(8,128)S(1)}, u32[]{:S(2)}, u32[]{:S(2)}) collective-permute-start(f32[104,128]{1,0:T(8,128)S(1)} %fusion.8), channel_id=1, source_target_pairs={{0,2},{2,4},{4,6},{6,0},{1,3},{3,5},{5,7},{7,1},{8,10},{10,12},{12... | collective-permute-start | bytes 159752 | tf_op jit(solution)/shard_map/ppermute | solution.py:168
  54.2 2.2 %collective-permute-done.9 = f32[104,128]{1,0:T(8,128)S(1)} collective-permute-done((f32[104,128]{1,0:T(8,128)S(1)}, f32[104,128]{1,0:T(8,128)S(1)}, u32[]{:S(2)}, u32[]{:S(2)}) %collective-permute-start.9) | collective-permute-done | bytes 53280 | tf_op jit(solution)/shard_map/ppermute | solution.py:168
  56.4 2.9 %collective-permute-done.8 = f32[104,128]{1,0:T(8,128)S(1)} collective-permute-done((f32[104,128]{1,0:T(8,128)S(1)}, f32[104,128]{1,0:T(8,128)S(1)}, u32[]{:S(2)}, u32[]{:S(2)}) %collective-permute-start.8) | collective-permute-done | bytes 53280 | tf_op jit(solution)/shard_map/ppermute | solution.py:168
  59.3 0.0 collective-permute-done.7
  59.4 0.7 pad_maximum_fusion.1
  60.1 0.0 copy-start.1
  60.1 1.7 %collective-permute-start.10 = (f32[416,128]{1,0:T(8,128)}, f32[416,128]{1,0:T(8,128)}, u32[]{:S(2)}, u32[]{:S(2)}) collective-permute-start(f32[416,128]{1,0:T(8,128)} %pad_maximum_fusion.1), channel_id=1, source_target_pairs={{0,8},{8,0},{1,9},{9,1},{2,10},{10,2},{3,11},{11,3},{4,12},{12,4},... | collective-permute-start | bytes 638984 | tf_op jit(solution)/shard_map/ppermute | solution.py:168
  61.8 4.5 %collective-permute-done.10 = f32[416,128]{1,0:T(8,128)} collective-permute-done((f32[416,128]{1,0:T(8,128)}, f32[416,128]{1,0:T(8,128)}, u32[]{:S(2)}, u32[]{:S(2)}) %collective-permute-start.10) | collective-permute-done | bytes 213024 | tf_op jit(solution)/shard_map/ppermute | solution.py:168
  66.3 1.0 %constant_dynamic-update-slice_fusion.9 = (f32[832,128]{1,0:T(8,128)S(1)}, f32[832,128]{1,0:T(8,128)S(1)}) fusion(f32[416,128]{1,0:T(8,128)} %collective-permute-done.10, f32[832,128]{1,0:T(8,128)S(1)} %get-tuple-element.9), kind=kLoop, calls=%fused_computation.37 | loop fusion | bytes 638976
  67.4 0.1 collective-permute-start.11
  67.5 1.7 %collective-permute-done.11.other_ref = f32[832,128]{1,0:T(8,128)S(1)} collective-permute-done((f32[832,128]{1,0:T(8,128)S(1)}, f32[832,128]{1,0:T(8,128)S(1)}, u32[]{:S(2)}, u32[]{:S(2)}) %collective-permute-start.11) | collective-permute-done | bytes 426016 | tf_op jit(solution)/shard_map/ppermute | solution.py:176
  69.2 0.0 copy-done.2
  69.2 21.1 %shard_map.65 = bf16[512,128]{1,0:T(8,128)(2,1)S(1)} custom-call(s32[1]{0:T(128)} %bitcast.1.side_ref, f32[832,128]{1,0:T(8,128)S(1)} %broadcast_select_fusion.mine_ref, f32[832,128]{1,0:T(8,128)S(1)} %collective-permute-done.11.other_ref, bf16[512,512]{1,0:T(8,128)(2,1)S(1)} %fusion.5.pick_ref, f32[512,128]{1,0:T(8,128)S(1)} %copy-done.2), custom_call_target="tpu_custom_call" | custom-call | tf_op jit(solution)/shard_map/pallas_call | solution.py:371
  90.3 0.0 copy-done.1
  90.3 1.7 %fusion = f32[32,64,128]{2,1,0:T(8,128)} fusion(bf16[32,64,512]{2,1,0:T(8,128)(2,1)S(1)} %copy-done.1, pred[32]{0:T(512)(128)(4,1)S(1)} %iota_compare_fusion.2, bf16[512,128]{1,0:T(8,128)(2,1)S(1)} %shard_map.65), kind=kOutput, calls=%fused_computation | convolution fusion | flops 269484032 | bytes 3276832 | tf_op jit(solution)/shard_map/dot_general | solution.py:412
  (19 shorter events, 0.3 us)
Async XLA Ops:
  1.6 8.2 %collective-permute-start.1 = (bf16[64,512]{1,0:T(8,128)(2,1)S(1)}, bf16[64,512]{1,0:T(8,128)(2,1)S(1)}, u32[]{:S(2)}, u32[]{:S(2)}) collective-permute-start(bf16[64,512]{1,0:T(8,128)(2,1)S(1)} %select_bitcast_fusion), channel_id=1, source_target_pairs={{1,0},{2,1},{3,2},{4,3},{5,4},{6,5},{7,6},{8,7},{9,8},{10,9},{11,1... | collective-permute-start | bytes 196616 | tf_op jit(solution)/shard_map/ppermute | solution.py:398
  3.9 5.9 %collective-permute-start = (bf16[128,512]{1,0:T(8,128)(2,1)S(1)}, bf16[128,512]{1,0:T(8,128)(2,1)S(1)}, u32[]{:S(2)}, u32[]{:S(2)}) collective-permute-start(bf16[128,512]{1,0:T(8,128)(2,1)S(1)} %bitcast.53), channel_id=1, source_target_pairs={{0,1},{1,2},{2,3},{3,4},{4,5},{5,6},{6,7},{7,8},{8,9},{9,10},{10,1... | collective-permute-start | bytes 393224 | tf_op jit(solution)/shard_map/ppermute | solution.py:397
  9.8 1.6 %copy-start = (bf16[32,64,512]{2,1,0:T(8,128)(2,1)S(1)}, bf16[32,64,512]{2,1,0:T(8,128)(2,1)}, u32[]{:S(2)}) copy-start(bf16[32,64,512]{2,1,0:T(8,128)(2,1)} %param.6) | copy-start | bytes 6291460
  25.3 4.1 %collective-permute-start.2 = (f32[832,128]{1,0:T(8,128)S(1)}, f32[832,128]{1,0:T(8,128)S(1)}, u32[]{:S(2)}, u32[]{:S(2)}) collective-permute-start(f32[832,128]{1,0:T(8,128)S(1)} %get-tuple-element.8), channel_id=1, source_target_pairs={{0,1},{1,0},{2,3},{3,2},{4,5},{5,4},{6,7},{7,6},{8,9},{9,8},{10,11... | collective-permute-start | bytes 1277960 | tf_op jit(solution)/shard_map/ppermute | solution.py:176
  29.5 13.0 %collective-permute-start.3 = (f32[416,128]{1,0:T(8,128)S(1)}, f32[416,128]{1,0:T(8,128)S(1)}, u32[]{:S(2)}, u32[]{:S(2)}) collective-permute-start(f32[416,128]{1,0:T(8,128)S(1)} %dynamic-slice_bitcast_fusion), channel_id=1, source_target_pairs={{0,8},{8,0},{1,9},{9,1},{2,10},{10,2},{3,11},{11,3},{4,12},{12,4},... | collective-permute-start | bytes 638984 | tf_op jit(solution)/shard_map/ppermute | solution.py:159
  42.6 6.4 %collective-permute-start.4 = (f32[104,128]{1,0:T(8,128)S(1)}, f32[104,128]{1,0:T(8,128)S(1)}, u32[]{:S(2)}, u32[]{:S(2)}) collective-permute-start(f32[104,128]{1,0:T(8,128)S(1)} %get-tuple-element.19), channel_id=1, source_target_pairs={{0,2},{2,4},{4,6},{6,0},{1,3},{3,5},{5,7},{7,1},{8,10},{10,12},{12... | collective-permute-start | bytes 159752 | tf_op jit(solution)/shard_map/ppermute | solution.py:159
  42.7 6.3 %collective-permute-start.6 = (f32[104,128]{1,0:T(8,128)S(1)}, f32[104,128]{1,0:T(8,128)S(1)}, u32[]{:S(2)}, u32[]{:S(2)}) collective-permute-start(f32[104,128]{1,0:T(8,128)S(1)} %get-tuple-element.20), channel_id=1, source_target_pairs={{0,6},{2,0},{4,2},{6,4},{1,7},{3,1},{5,3},{7,5},{8,14},{10,8},{12,... | collective-permute-start | bytes 159752 | tf_op jit(solution)/shard_map/ppermute | solution.py:159
  46.5 5.3 %collective-permute-start.5 = (f32[104,128]{1,0:T(8,128)S(1)}, f32[104,128]{1,0:T(8,128)S(1)}, u32[]{:S(2)}, u32[]{:S(2)}) collective-permute-start(f32[104,128]{1,0:T(8,128)S(1)} %get-tuple-element.21), channel_id=1, source_target_pairs={{0,4},{2,6},{4,0},{6,2},{1,5},{3,7},{5,1},{7,3},{8,12},{10,14},{12... | collective-permute-start | bytes 159752 | tf_op jit(solution)/shard_map/ppermute | solution.py:159
  46.5 22.7 %copy-start.2 = (f32[512,128]{1,0:T(8,128)S(1)}, f32[512,128]{1,0:T(8,128)}, u32[]{:S(2)}) copy-start(f32[512,128]{1,0:T(8,128)} %start_ref.1) | copy-start | bytes 786436
  51.8 4.6 %collective-permute-start.9 = (f32[104,128]{1,0:T(8,128)S(1)}, f32[104,128]{1,0:T(8,128)S(1)}, u32[]{:S(2)}, u32[]{:S(2)}) collective-permute-start(f32[104,128]{1,0:T(8,128)S(1)} %fusion.8), channel_id=1, source_target_pairs={{0,6},{2,0},{4,2},{6,4},{1,7},{3,1},{5,3},{7,5},{8,14},{10,8},{12,... | collective-permute-start | bytes 159752 | tf_op jit(solution)/shard_map/ppermute | solution.py:168
  53.1 6.2 %collective-permute-start.8 = (f32[104,128]{1,0:T(8,128)S(1)}, f32[104,128]{1,0:T(8,128)S(1)}, u32[]{:S(2)}, u32[]{:S(2)}) collective-permute-start(f32[104,128]{1,0:T(8,128)S(1)} %fusion.8), channel_id=1, source_target_pairs={{0,4},{2,6},{4,0},{6,2},{1,5},{3,7},{5,1},{7,3},{8,12},{10,14},{12... | collective-permute-start | bytes 159752 | tf_op jit(solution)/shard_map/ppermute | solution.py:168
  53.1 6.2 %collective-permute-start.7 = (f32[104,128]{1,0:T(8,128)S(1)}, f32[104,128]{1,0:T(8,128)S(1)}, u32[]{:S(2)}, u32[]{:S(2)}) collective-permute-start(f32[104,128]{1,0:T(8,128)S(1)} %fusion.8), channel_id=1, source_target_pairs={{0,2},{2,4},{4,6},{6,0},{1,3},{3,5},{5,7},{7,1},{8,10},{10,12},{12... | collective-permute-start | bytes 159752 | tf_op jit(solution)/shard_map/ppermute | solution.py:168
  60.1 30.2 %copy-start.1 = (bf16[32,64,512]{2,1,0:T(8,128)(2,1)S(1)}, bf16[32,64,512]{2,1,0:T(8,128)(2,1)}, u32[]{:S(2)}) copy-start(bf16[32,64,512]{2,1,0:T(8,128)(2,1)} %param.6) | copy-start | bytes 6291460
  60.1 6.2 %collective-permute-start.10 = (f32[416,128]{1,0:T(8,128)}, f32[416,128]{1,0:T(8,128)}, u32[]{:S(2)}, u32[]{:S(2)}) collective-permute-start(f32[416,128]{1,0:T(8,128)} %pad_maximum_fusion.1), channel_id=1, source_target_pairs={{0,8},{8,0},{1,9},{9,1},{2,10},{10,2},{3,11},{11,3},{4,12},{12,4},... | collective-permute-start | bytes 638984 | tf_op jit(solution)/shard_map/ppermute | solution.py:168
  67.4 1.8 %collective-permute-start.11 = (f32[832,128]{1,0:T(8,128)S(1)}, f32[832,128]{1,0:T(8,128)S(1)}, u32[]{:S(2)}, u32[]{:S(2)}) collective-permute-start(f32[832,128]{1,0:T(8,128)S(1)} %broadcast_select_fusion.mine_ref), channel_id=1, source_target_pairs={{0,1},{1,0},{2,3},{3,2},{4,5},{5,4},{6,7},{7,6},{8,9},{9,8},{10,11... | collective-permute-start | bytes 1277960 | tf_op jit(solution)/shard_map/ppermute | solution.py:176

commit v3 on v2

--- a/solution.py
+++ b/solution.py
@@ -24,142 +24,252 @@
     return lax.dot_general(a, b, (dims, ((), ())), precision=HIGH, preferred_element_type=F32)
 
 
-def front_kernel(count_ref, low_ref, x_ref, high_ref, pick_ref, taps_ref, keep_ref, send_ref, xs, taps, nf, sg):
-    height = x_ref.shape[0] // 64
+def place(xs, values, rows, slot, row, limit):
+    pitch = xs.shape[0] // 4
+    for k in range(rows):
+        piece = values[k * 64 : (k + 1) * 64]
+        if limit is not None:
+            piece = jnp.where(row + k < limit, piece, 0.0)
+        start = pl.multiple_of(8 + (slot + k) * PITCH, 8)
+        for tile in range(4):
+            xs[pl.ds(start + tile * pitch, 64), :] = piece[:, tile * LANES : (tile + 1) * LANES]
+
+
+def clear_gaps(xs, slots):
+    pitch = xs.shape[0] // 4
+    zeros = jnp.zeros((8, LANES), F32)
+    for tile in range(4):
+        for slot in range(slots + 1):
+            start = tile * pitch + slot * PITCH
+            xs[start : start + 8, :] = zeros
+
+
+def noise_tile(xs, taps, slot, valid, tile):
+    pitch = xs.shape[0] // 4
+    lanes = slice(tile * LANES, (tile + 1) * LANES)
+    tap = lambda k: taps[k : k + 1, lanes]
+    even = odd = None
+    for row_off in (-1, 0, 1):
+        base = tile * pitch + 8 + (slot + row_off) * PITCH
+        here_even = xs[pl.ds(base, 32, stride=2), :]
+        next_even = xs[pl.ds(base + 2, 32, stride=2), :]
+        prev_odd = xs[pl.ds(base - 1, 32, stride=2), :]
+        here_odd = xs[pl.ds(base + 1, 32, stride=2), :]
+        if row_off == 0:
+            left, right = tap(3), tap(4)
+            part_even = here_even - left * prev_odd - right * here_odd
+            part_odd = here_odd - left * here_even - right * next_even
+        else:
+            first = 0 if row_off == -1 else 5
+            left, mid, right = tap(first), tap(first + 1), tap(first + 2)
+            part_even = -(left * prev_odd + mid * here_even + right * here_odd)
+            part_odd = -(left * here_even + mid * here_odd + right * next_even)
+        even = part_even if even is None else even + part_even
+        odd = part_odd if odd is None else odd + part_odd
+    return jnp.where(valid, even, 0.0).astype(BF16), jnp.where(valid, odd, 0.0).astype(BF16)
+
+
+def signal_tile(xs, taps, slot, tile):
+    pitch = xs.shape[0] // 4
+    lanes = slice(tile * LANES, (tile + 1) * LANES)
+    total = None
+    for i in range(5):
+        base = tile * pitch + 8 + (slot + i) * PITCH
+        for j in range(5):
+            k = 8 + 5 * i + j
+            term = taps[k : k + 1, lanes] * xs[pl.ds(base + j - 2, 32, stride=2), :]
+            total = term if total is None else total + term
+    return total.astype(BF16)
+
+
+def packed_gram(field):
+    r = lax.broadcasted_iota(jnp.int32, (LANES, LANES), 0)
+    c = lax.broadcasted_iota(jnp.int32, (LANES, LANES), 1)
+    corners, blocks = [], []
+    for panel in range(4):
+        low = panel * LANES
+        block = lax.dot_general(
+            field[:, low:], field[:, low : low + LANES], (((0,), (0,)), ((), ())), preferred_element_type=F32
+        )
+        corners.append(block[:LANES])
+        if panel < 3:
+            blocks.append((BELOW[panel], block[LANES : USED - low]))
+    blocks.append((SQUARE, jnp.where(r >= c, corners[0], corners[1])))
+    blocks.append((THIRD, corners[2]))
+    diagonal = jnp.sum(jnp.where(r == c, corners[1], 0.0), axis=0, keepdims=True)
+    tail = corners[3][: USED - 384]
+    row = lax.broadcasted_iota(jnp.int32, tail.shape, 0)
+    blocks.append((LAST, jnp.where(row == 47, diagonal, tail)))
+    return blocks
+
+
+def inner_kernel(
+    count_ref, mask_hbm, noise_hbm, smooth_hbm, x_hbm, noise_out, signal_out, pick_ref, taps,
+    x, xs, nf, sg, mask_ref, noise_ref, smooth_ref, sems, small_sems,
+):
+    height = x.shape[0] // 64
+    bands = x.shape[1]
+    chunks = sems.shape[0]
+    size = x.shape[0] // chunks
+    copies = [
+        pltpu.make_async_copy(x_hbm.at[pl.ds(k * size, size)], x.at[pl.ds(k * size, size)], sems.at[k])
+        for k in range(chunks)
+    ]
+    small = [
+        pltpu.make_async_copy(source, target, small_sems.at[k])
+        for k, (source, target) in enumerate(
+            ((mask_hbm, mask_ref), (noise_hbm, noise_ref), (smooth_hbm, smooth_ref))
+        )
+    ]
+    for copy in small + copies:
+        copy.start()
+    clear_gaps(xs, height)
+    for copy in small:
+        copy.wait()
     count = count_ref[0]
-    pitch = xs.shape[0] // 4
-    taps[...] = mm(taps_ref[...], pick_ref[...].astype(F32))
-    xs[...] = jnp.zeros_like(xs)
+    mask = jnp.broadcast_to(mask_ref[...].astype(F32), (16, bands)).astype(BF16)
+    r = lax.broadcasted_iota(jnp.int32, (bands, bands), 0)
+    c = lax.broadcasted_iota(jnp.int32, (bands, bands), 1)
+    ranks = jnp.where(c < r, 1.0, jnp.where(c == r, 1024.0, 0.0)).astype(BF16)
+    position = lax.dot_general(ranks, mask, (((1,), (1,)), ((), ())), preferred_element_type=F32)[:, :1]
+    pick_ref[...] = jnp.where(position == (c + 1024).astype(F32), 1.0, 0.0).astype(BF16)
     pick = pick_ref[...]
-
-    def place(block, first_row, limit):
-        values = jnp.dot(block, pick, preferred_element_type=F32)
-        for k in range(block.shape[0] // 64):
-            row = first_row + k
-            piece = values[k * 64 : (k + 1) * 64]
-            if limit is not None:
-                piece = jnp.where(row < limit, piece, 0.0)
-            start = pl.multiple_of(8 + (row + 2) * PITCH, 8)
-            for tile in range(4):
-                xs[pl.ds(start + tile * pitch, 64), :] = piece[:, tile * LANES : (tile + 1) * LANES]
-
-    place(low_ref[...], -2, None)
-    place(high_ref[...], height, None)
-
-    def place_body(chunk, carry):
-        place(x_ref[pl.ds(pl.multiple_of(chunk * 256, 256), 256), :], chunk * 4, count)
-        return carry
-
-    lax.fori_loop(0, height // 4, place_body, 0)
-
-    def column(base, offset):
-        return xs[pl.ds(base + offset, 32, stride=2), :]
+    wide_pick = pick.astype(F32)
+    taps[:8, :] = mm(noise_ref[...], wide_pick)
+    taps[8:, :] = mm(jnp.concatenate([smooth_ref[...], jnp.zeros((7, bands), F32)], axis=0), wide_pick)
+    for k, copy in enumerate(copies):
+        copy.wait()
+        values = jnp.dot(x[k * size : (k + 1) * size, :], pick, preferred_element_type=F32)
+        place(xs, values, size // 64, k * (size // 64), k * (size // 64), count)
 
     def noise_body(row, carry):
-        valid = row < count
+        start = pl.multiple_of((row - 1) * 64, 64)
         for tile in range(4):
             lanes = slice(tile * LANES, (tile + 1) * LANES)
-            tap = lambda k: taps[k : k + 1, lanes]
-            even = odd = None
-            for index, row_off in enumerate((-1, 0, 1)):
-                base = tile * pitch + 8 + (row + 2 + row_off) * PITCH
-                here_even = column(base, 0)
-                next_even = column(base, 2)
-                prev_odd = column(base, -1)
-                here_odd = column(base, 1)
-                if row_off == 0:
-                    left, right = tap(3), tap(4)
-                    part_even = here_even - left * prev_odd - right * here_odd
-                    part_odd = here_odd - left * here_even - right * next_even
-                else:
-                    first = 0 if row_off == -1 else 5
-                    left, mid, right = tap(first), tap(first + 1), tap(first + 2)
-                    part_even = -(left * prev_odd + mid * here_even + right * here_odd)
-                    part_odd = -(left * here_even + mid * here_odd + right * next_even)
-                even = part_even if even is None else even + part_even
-                odd = part_odd if odd is None else odd + part_odd
-            start = pl.multiple_of(row * 64, 64)
-            nf[pl.ds(start, 32), lanes] = jnp.where(valid, even, 0.0).astype(BF16)
-            nf[pl.ds(start + 32, 32), lanes] = jnp.where(valid, odd, 0.0).astype(BF16)
+            even, odd = noise_tile(xs, taps, row, row < count, tile)
+            nf[pl.ds(start, 32), lanes] = even
+            nf[pl.ds(start + 32, 32), lanes] = odd
         return carry
 
-    lax.fori_loop(0, height, noise_body, 0)
+    lax.fori_loop(1, height - 1, noise_body, 0)
 
     def signal_body(row, carry):
+        start = pl.multiple_of((row - 1) * 32, 32)
+        for tile in range(4):
+            sg[pl.ds(start, 32), tile * LANES : (tile + 1) * LANES] = signal_tile(xs, taps, 2 * row - 2, tile)
+        return carry
+
+    lax.fori_loop(1, height // 2 - 1, signal_body, 0)
+    for field, out_ref in ((nf, noise_out), (sg, signal_out)):
+        for start, block in packed_gram(field):
+            out_ref[start : start + block.shape[0], :] = block
+
+
+def edge_kernel(
+    count_ref, low_hbm, x_hbm, high_hbm, pick_ref, taps, noise_ref, signal_ref, keep_ref, send_ref,
+    rows, both, xs, nf, sg, sems,
+):
+    count, side = count_ref[0], count_ref[1]
+    size = x_hbm.shape[0]
+    height = size // 64
+    pieces = ((low_hbm, 0, 128), (x_hbm.at[pl.ds(0, 192)], 128, 192), (x_hbm.at[pl.ds(size - 256, 256)], 320, 256), (high_hbm, 576, 64))
+    copies = [
+        pltpu.make_async_copy(source, rows.at[pl.ds(start, length)], sems.at[k])
+        for k, (source, start, length) in enumerate(pieces)
+    ]
+    for copy in copies:
+        copy.start()
+    pick = pick_ref[...]
+    clear_gaps(xs, 10)
+    for copy in copies:
+        copy.wait()
+    values = jnp.dot(rows[...], pick, preferred_element_type=F32)
+    place(xs, values[:128], 2, 0, 0, None)
+    place(xs, values[128:320], 3, 2, 0, count)
+    place(xs, values[320:576], 4, 5, height - 4, count)
+    place(xs, values[576:], 1, 9, 0, None)
+    for k, (slot, valid) in enumerate(((2, count > 0), (8, count > height - 1))):
         for tile in range(4):
             lanes = slice(tile * LANES, (tile + 1) * LANES)
-            total = jnp.zeros((32, LANES), F32)
-            for i in range(5):
-                base = tile * pitch + 8 + (2 * row + i) * PITCH
-                for j in range(5):
-                    k = 8 + 5 * i + j
-                    total = total + taps[k : k + 1, lanes] * column(base, j - 2)
-            sg[pl.ds(pl.multiple_of(row * 32, 32), 32), lanes] = total.astype(BF16)
-        return carry
-
-    lax.fori_loop(0, height // 2, signal_body, 0)
-
-    r = lax.broadcasted_iota(jnp.int32, (LANES, LANES), 0)
-    c = lax.broadcasted_iota(jnp.int32, (LANES, LANES), 1)
-    for half, field in enumerate((nf, sg)):
-
-        def put(start, block):
-            @pl.when(count_ref[1] == half)
-            def _():
-                keep_ref[start : start + block.shape[0], :] = block
-
-            @pl.when(count_ref[1] != half)
-            def _():
-                send_ref[start : start + block.shape[0], :] = block
-
-        corners = []
-        for panel in range(4):
-            low = panel * LANES
-            block = lax.dot_general(
-                field[:, low:], field[:, low : low + LANES], (((0,), (0,)), ((), ())), preferred_element_type=F32
-            )
-            corners.append(block[:LANES])
-            if panel < 3:
-                put(BELOW[panel], block[LANES : USED - low])
-        put(SQUARE, jnp.where(r >= c, corners[0], corners[1]))
-        put(THIRD, corners[2])
-        diagonal = jnp.sum(jnp.where(r == c, corners[1], 0.0), axis=0, keepdims=True)
-        tail = corners[3][: USED - 384]
-        row = lax.broadcasted_iota(jnp.int32, tail.shape, 0)
-        tail = jnp.where(row == 47, diagonal, jnp.where(row == 46, count.astype(F32), tail))
-        put(LAST, tail)
-
-
-def front(count, low, x, high, pick, taps):
-    height = x.shape[0] // 64
-    vmem = pl.BlockSpec(memory_space=pltpu.VMEM)
+            even, odd = noise_tile(xs, taps, slot, valid, tile)
+            nf[k * 64 : k * 64 + 32, lanes] = even
+            nf[k * 64 + 32 : k * 64 + 64, lanes] = odd
+            sg[k * 32 : k * 32 + 32, lanes] = signal_tile(xs, taps, 5 * k, tile)
+    for half, (field, inner) in enumerate(((nf, noise_ref), (sg, signal_ref))):
+        for start, block in packed_gram(field):
+            rows = block.shape[0]
+            block = block + inner[start : start + rows, :]
+            if start == LAST:
+                row = lax.broadcasted_iota(jnp.int32, block.shape, 0)
+                block = jnp.where(row == 46, count.astype(F32), block)
+            both[half * PACKED + start : half * PACKED + start + rows, :] = block
+    keep_ref[...] = both[pl.ds(pl.multiple_of(side * PACKED, 8), PACKED), :]
+    send_ref[...] = both[pl.ds(pl.multiple_of((1 - side) * PACKED, 8), PACKED), :]
+
+
+VMEM = pl.BlockSpec(memory_space=pltpu.VMEM)
+SMEM = pl.BlockSpec(memory_space=pltpu.SMEM)
+HBM = pl.BlockSpec(memory_space=pltpu.HBM)
+PARAMS = pltpu.CompilerParams(vmem_limit_bytes=48 << 20)
+
+
+def inner(count, mask, noise_kernel, smooth_kernel, x):
+    height, bands = x.shape[0] // 64, x.shape[1]
+    gram = jax.ShapeDtypeStruct((PACKED, LANES), F32)
     return pl.pallas_call(
-        front_kernel,
-        out_shape=(jax.ShapeDtypeStruct((PACKED, LANES), F32),) * 2,
-        in_specs=[pl.BlockSpec(memory_space=pltpu.SMEM)] + [vmem] * 5,
-        out_specs=(vmem, vmem),
+        inner_kernel,
+        out_shape=(gram, gram, jax.ShapeDtypeStruct((bands, bands), BF16), jax.ShapeDtypeStruct((40, bands), F32)),
+        in_specs=[SMEM] + [HBM] * 4,
+        out_specs=(VMEM,) * 4,
         scratch_shapes=[
-            pltpu.VMEM((4 * (8 + (height + 3) * PITCH + 8), LANES), F32),
-            pltpu.VMEM((40, 512), F32),
-            pltpu.VMEM((height * 64, 512), BF16),
-            pltpu.VMEM((height * 16, 512), BF16),
+            pltpu.VMEM(x.shape, BF16),
+            pltpu.VMEM((4 * (16 + height * PITCH), LANES), F32),
+            pltpu.VMEM(((height - 2) * 64, bands), BF16),
+            pltpu.VMEM(((height // 2 - 2) * 32, bands), BF16),
+            pltpu.VMEM(mask.shape, jnp.int32),
+            pltpu.VMEM(noise_kernel.shape, F32),
+            pltpu.VMEM(smooth_kernel.shape, F32),
+            pltpu.SemaphoreType.DMA((8,)),
+            pltpu.SemaphoreType.DMA((3,)),
         ],
-        compiler_params=pltpu.CompilerParams(vmem_limit_bytes=48 << 20),
-    )(count, low, x, high, pick, taps)
-
-
-def scatter_sum(x, axis):
+        compiler_params=PARAMS,
+        cost_estimate=pl.CostEstimate(flops=6 << 30, transcendentals=0, bytes_accessed=8 << 20),
+        name="inner",
+    )(count, *(pltpu.with_memory_space_constraint(a, pltpu.HBM) for a in (mask, noise_kernel, smooth_kernel, x)))
+
+
+def edge(counts, low, x, high, pick, taps, noise, signal):
+    bands = x.shape[1]
+    gram = jax.ShapeDtypeStruct((PACKED, LANES), F32)
+    return pl.pallas_call(
+        edge_kernel,
+        out_shape=(gram, gram),
+        in_specs=[SMEM, HBM, HBM, HBM, VMEM, VMEM, VMEM, VMEM],
+        out_specs=(VMEM, VMEM),
+        scratch_shapes=[
+            pltpu.VMEM((640, bands), BF16),
+            pltpu.VMEM((2 * PACKED, LANES), F32),
+            pltpu.VMEM((4 * (16 + 10 * PITCH), LANES), F32),
+            pltpu.VMEM((128, bands), BF16),
+            pltpu.VMEM((64, bands), BF16),
+            pltpu.SemaphoreType.DMA((4,)),
+        ],
+        compiler_params=PARAMS,
+        name="edge",
+    )(counts, *(pltpu.with_memory_space_constraint(a, pltpu.HBM) for a in (low, x, high)), pick, taps, noise, signal)
+
+
+def scatter_sum(parts, axis):
     n = lax.axis_size(axis)
-    blocks = x.reshape(n, x.shape[0] // n, x.shape[1])
     me = lax.axis_index(axis)
-    total = lax.dynamic_index_in_dim(blocks, me, 0, keepdims=False)
+
+    def block(k):
+        return [lax.dynamic_index_in_dim(x.reshape(n, -1, LANES), k, 0, keepdims=False) for x in parts]
+
     got = []
     for d in range(1, n):
-        piece = lax.dynamic_index_in_dim(blocks, (me + d) % n, 0, keepdims=False)
-        got.append(lax.ppermute(piece, axis, [(i, (i + d) % n) for i in range(n)]))
-    for piece in got:
-        total = total + piece
-    return total
+        got.append(lax.ppermute(sum(block((me + d) % n)), axis, [(i, (i + d) % n) for i in range(n)]))
+    return block(me) + got
 
 
 def gather_rows(x, axis):
@@ -177,11 +287,12 @@
 
 
 def total_sum(keep, send):
-    x = keep + exchange(send)
+    parts = [keep, exchange(send)]
     short = [axis for axis in ("wide", "narrow") if lax.axis_size(axis) <= 4]
     long = tuple(axis for axis in ("wide", "narrow") if axis not in short)
     for axis in short:
-        x = scatter_sum(x, axis)
+        parts = scatter_sum(parts, axis)
+    x = sum(parts)
     if long:
         x = lax.psum(x, long)
     for axis in reversed(short):
@@ -397,14 +508,11 @@
     low = lax.ppermute(tail.reshape(2 * across, bands), AXES, up)
     high = lax.ppermute(lead.reshape(across, bands), AXES, down)
 
-    order = jnp.arange(bands, dtype=jnp.int32)
-    place = jnp.sum(jnp.where(order[None, :] < order[:, None], band_mask[None, :], 0), axis=1)
-    pick = ((place[:, None] == order[None, :]) & (band_mask[:, None] == 1)).astype(BF16)
-    taps = jnp.concatenate([noise_kernel, smooth_kernel, jnp.zeros((7, bands), F32)])
-
     flat = radiance.reshape(height * across, bands)
+    noise, signal, pick, taps = inner(row_counts, band_mask[None], noise_kernel, smooth_kernel, flat)
     side = lax.axis_index("sub").astype(jnp.int32)
-    keep, send = front(jnp.stack([count, side]), low, flat, high, pick, taps)
+    counts = jnp.stack([count, side])
+    keep, send = edge(counts, low, flat, high, pick, taps, noise, signal)
     mine, other = total_sum(keep, send)
     weights = finish(side[None], mine, other, pick, start_basis)
     keep = jnp.repeat(row < count, across)

time: 92.4 us -> 85.6 us (0.926)
  starting transfers between devices: 22.5 us -> 18.5 us
  other arithmetic: 5.49 us -> 2.86 us
  Pallas kernels: 35 us -> 36.4 us
  local copies, waits for them, and re-layouts: 2.78 us -> 1.73 us
    ppermute x4, starting transfers between devices: 11.3 us -> 6.89 us  [scatter_sum(): lax.ppermute(sum(block((me + d) % n)), axis, [(i, (i + d) % n) for i in r...]
    pallas_call x1 -> x2, Pallas kernels: 13.9 us -> 15.3 us  [the longest x1 12.4 us: inner(): pl.pallas_call(inner_kernel, out_shape=(gram, gram, jax.ShapeDtypeStruct(...]
    unnamed x14 -> x16, local copies, waits for them, and re-layouts: 2.64 us -> 1.72 us
  transfers between devices with their start and end apart: 12 -> 12, of which waited for: 8 -> 8; matrix products, arithmetic and copies ran while one was open for 4% -> 1% of each run, Pallas kernels for 0% -> 15%
where the time goes in v3:
time: 85.6 us; the launch traced here: 85.3 us
  Pallas kernels  36.4 us (43%)
  waiting for transfers between devices  23.2 us (27%)
  starting transfers between devices  18.5 us (22%)
  other arithmetic  2.86 us (3%)
  local copies, waits for them, and re-layouts  1.73 us (2%)
  matrix products  1.72 us (2%)
  between operations  0.89 us (1%)
    pallas_call x1, Pallas kernels, finish(): pl.pallas_call(finish_kernel, out_shape=jax.ShapeDtypeStruct((512, LANES)...  21.1 us
    pallas_call x1, Pallas kernels, inner(): pl.pallas_call(inner_kernel, out_shape=(gram, gram, jax.ShapeDtypeStruct(...  12.4 us
    ppermute x4, waiting for transfers between devices, scatter_sum(): lax.ppermute(sum(block((me + d) % n)), axis, [(i, (i + d) % n) for i in r...  10.7 us
    ppermute x4, waiting for transfers between devices, gather_rows(): lax.ppermute(x, axis, [(i, (i + d) % n) for i in range(n)])  9.31 us
    ppermute x4, starting transfers between devices, scatter_sum(): lax.ppermute(sum(block((me + d) % n)), axis, [(i, (i + d) % n) for i in r...  6.89 us
    ppermute x4, starting transfers between devices, gather_rows(): lax.ppermute(x, axis, [(i, (i + d) % n) for i in range(n)])  4.51 us
    ppermute x2, starting transfers between devices, exchange(): return lax.ppermute(x, 'sub', [(0, 1), (1, 0)])  3.45 us
    ppermute x2, waiting for transfers between devices, exchange(): return lax.ppermute(x, 'sub', [(0, 1), (1, 0)])  3.14 us
  transfers between devices with their start and end apart: 12, of which 8 were waited for; matrix products, arithmetic and copies ran while one was open for 1% of the time, Pallas kernels for 15%

profile of v3, /device:TPU:0, one launch (start us, length us, event | category | flops | bytes accessed | tf_op | source)
XLA Modules:
  0.0 85.3 jit_solution(10904226435603103156)
XLA Ops:
  0.7 0.1 slice_compare_fusion
  0.7 1.0 %slice_select_fusion = bf16[2,64,512]{2,1,0:T(8,128)(2,1)S(1)} fusion(bf16[32,64,512]{2,1,0:T(8,128)(2,1)} %param.6, pred[2]{0:T(512)(128)(4,1)S(1)} %slice_compare_fusion), kind=kLoop, calls=%fused_computation.9 | loop fusion | flops 65536 | bytes 262146 | tf_op jit(solution)/shard_map/jit(_where)/select_n | solution.py:506
  1.7 2.4 %collective-permute-start = (bf16[128,512]{1,0:T(8,128)(2,1)S(1)}, bf16[128,512]{1,0:T(8,128)(2,1)S(1)}, u32[]{:S(2)}, u32[]{:S(2)}) collective-permute-start(bf16[128,512]{1,0:T(8,128)(2,1)S(1)} %bitcast.60), channel_id=1, source_target_pairs={{0,1},{1,2},{2,3},{3,4},{4,5},{5,6},{6,7},{7,8},{8,9},{9,10},{10,1... | collective-permute-start | bytes 393224 | tf_op jit(solution)/shard_map/ppermute | solution.py:508
  4.1 0.8 select_bitcast_fusion
  5.0 1.3 %collective-permute-start.1 = (bf16[64,512]{1,0:T(8,128)(2,1)S(1)}, bf16[64,512]{1,0:T(8,128)(2,1)S(1)}, u32[]{:S(2)}, u32[]{:S(2)}) collective-permute-start(bf16[64,512]{1,0:T(8,128)(2,1)S(1)} %select_bitcast_fusion), channel_id=1, source_target_pairs={{1,0},{2,1},{3,2},{4,3},{5,4},{6,5},{7,6},{8,7},{9,8},{10,9},{11,1... | collective-permute-start | bytes 196616 | tf_op jit(solution)/shard_map/ppermute | solution.py:509
  6.3 12.4 %inner.1 = (f32[832,128]{1,0:T(8,128)S(1)}, f32[832,128]{1,0:T(8,128)S(1)}, bf16[512,512]{1,0:T(8,128)(2,1)S(1)}, f32[40,512]{1,0:T(8,128)S(1)}) custom-call(s32[1]{0:T(128)} %copy.15.count_ref, s32[1,512]{1,0:T(1,128)} %bitcast.64, f32[8,512]{1,0:T(8,128)} %noise_hbm.1, f32[25,512]{1,0:T(8,128)} %smooth_hbm.1, bf16[2048,512]{1,0:T(8,128)(2,1)} %bitcast.50), custom_call_target="tpu_custom_call" | custom-call | flops 6442450944 | bytes 8388608 | tf_op jit(solution)/shard_map/inner/pallas_call | solution.py:219
  18.7 0.1 pad_add_fusion.count_ref
  18.8 0.0 collective-permute-done.1.high_hbm
  18.8 0.0 copy-start.3
  18.8 0.0 collective-permute-done.low_hbm
  18.8 0.0 copy-start.2
  18.8 0.6 copy-done.3
  19.4 0.1 copy-done.2
  19.4 2.9 %edge.1 = (f32[832,128]{1,0:T(8,128)S(1)}, f32[832,128]{1,0:T(8,128)S(1)}) custom-call(s32[2]{0:T(128)S(1)} %pad_add_fusion.count_ref, bf16[128,512]{1,0:T(8,128)(2,1)} %copy-done.2, bf16[2048,512]{1,0:T(8,128)(2,1)} %bitcast.51, bf16[64,512]{1,0:T(8,128)(2,1)} %copy-done.3, bf16[512,512]{1,0:T(8,128)(2,1)S(1)} %get-tuple-element.11.pick_ref, ...), custom_call_target="tpu_custom_call" | custom-call | tf_op jit(solution)/shard_map/edge/pallas_call | solution.py:244
  22.4 3.4 %collective-permute-start.2 = (f32[832,128]{1,0:T(8,128)S(1)}, f32[832,128]{1,0:T(8,128)S(1)}, u32[]{:S(2)}, u32[]{:S(2)}) collective-permute-start(f32[832,128]{1,0:T(8,128)S(1)} %get-tuple-element.16), channel_id=1, source_target_pairs={{0,1},{1,0},{2,3},{3,2},{4,5},{5,4},{6,7},{7,6},{8,9},{9,8},{10,11... | collective-permute-start | bytes 1277960 | tf_op jit(solution)/shard_map/ppermute | solution.py:286
  25.8 1.4 %collective-permute-done.2 = f32[832,128]{1,0:T(8,128)S(1)} collective-permute-done((f32[832,128]{1,0:T(8,128)S(1)}, f32[832,128]{1,0:T(8,128)S(1)}, u32[]{:S(2)}, u32[]{:S(2)}) %collective-permute-start.2) | collective-permute-done | bytes 426016 | tf_op jit(solution)/shard_map/ppermute | solution.py:286
  27.2 0.1 constant_dynamic-slice_fusion.1
  27.2 4.7 %collective-permute-start.3 = (f32[416,128]{1,0:T(8,128)S(1)}, f32[416,128]{1,0:T(8,128)S(1)}, u32[]{:S(2)}, u32[]{:S(2)}) collective-permute-start(f32[416,128]{1,0:T(8,128)S(1)} %get-tuple-element.29), channel_id=1, source_target_pairs={{0,8},{8,0},{1,9},{9,1},{2,10},{10,2},{3,11},{11,3},{4,12},{12,4},... | collective-permute-start | bytes 638984 | tf_op jit(solution)/shard_map/ppermute | solution.py:271
  31.9 5.6 %collective-permute-done.3 = f32[416,128]{1,0:T(8,128)S(1)} collective-permute-done((f32[416,128]{1,0:T(8,128)S(1)}, f32[416,128]{1,0:T(8,128)S(1)}, u32[]{:S(2)}, u32[]{:S(2)}) %collective-permute-start.3) | collective-permute-done | bytes 213024 | tf_op jit(solution)/shard_map/ppermute | solution.py:271
  37.5 1.2 %collective-permute-start.6 = (f32[104,128]{1,0:T(8,128)S(1)}, f32[104,128]{1,0:T(8,128)S(1)}, u32[]{:S(2)}, u32[]{:S(2)}) collective-permute-start(f32[104,128]{1,0:T(8,128)S(1)} %get-tuple-element.26), channel_id=1, source_target_pairs={{0,6},{2,0},{4,2},{6,4},{1,7},{3,1},{5,3},{7,5},{8,14},{10,8},{12,... | collective-permute-start | bytes 159752 | tf_op jit(solution)/shard_map/ppermute | solution.py:271
  38.7 0.0 collective-permute-start.5
  38.7 1.0 %collective-permute-start.4 = (f32[104,128]{1,0:T(8,128)S(1)}, f32[104,128]{1,0:T(8,128)S(1)}, u32[]{:S(2)}, u32[]{:S(2)}) collective-permute-start(f32[104,128]{1,0:T(8,128)S(1)} %get-tuple-element.25), channel_id=1, source_target_pairs={{0,2},{2,4},{4,6},{6,0},{1,3},{3,5},{5,7},{7,1},{8,10},{10,12},{12... | collective-permute-start | bytes 159752 | tf_op jit(solution)/shard_map/ppermute | solution.py:271
  39.7 0.0 copy-start
  39.7 2.5 %collective-permute-done.6 = f32[104,128]{1,0:T(8,128)S(1)} collective-permute-done((f32[104,128]{1,0:T(8,128)S(1)}, f32[104,128]{1,0:T(8,128)S(1)}, u32[]{:S(2)}, u32[]{:S(2)}) %collective-permute-start.6) | collective-permute-done | bytes 53280 | tf_op jit(solution)/shard_map/ppermute | solution.py:271
  42.2 2.6 %collective-permute-done.5 = f32[104,128]{1,0:T(8,128)S(1)} collective-permute-done((f32[104,128]{1,0:T(8,128)S(1)}, f32[104,128]{1,0:T(8,128)S(1)}, u32[]{:S(2)}, u32[]{:S(2)}) %collective-permute-start.5) | collective-permute-done | bytes 53280 | tf_op jit(solution)/shard_map/ppermute | solution.py:271
  44.9 0.0 collective-permute-done.4
  44.9 1.5 %collective-permute-start.9 = (f32[104,128]{1,0:T(8,128)S(1)}, f32[104,128]{1,0:T(8,128)S(1)}, u32[]{:S(2)}, u32[]{:S(2)}) collective-permute-start(f32[104,128]{1,0:T(8,128)S(1)} %fusion.6), channel_id=1, source_target_pairs={{0,6},{2,0},{4,2},{6,4},{1,7},{3,1},{5,3},{7,5},{8,14},{10,8},{12,... | collective-permute-start | bytes 159752 | tf_op jit(solution)/shard_map/ppermute | solution.py:278
  46.4 0.0 collective-permute-start.8
  46.4 1.5 %collective-permute-start.7 = (f32[104,128]{1,0:T(8,128)S(1)}, f32[104,128]{1,0:T(8,128)S(1)}, u32[]{:S(2)}, u32[]{:S(2)}) collective-permute-start(f32[104,128]{1,0:T(8,128)S(1)} %fusion.6), channel_id=1, source_target_pairs={{0,2},{2,4},{4,6},{6,0},{1,3},{3,5},{5,7},{7,1},{8,10},{10,12},{12... | collective-permute-start | bytes 159752 | tf_op jit(solution)/shard_map/ppermute | solution.py:278
  47.9 2.3 %collective-permute-done.9 = f32[104,128]{1,0:T(8,128)S(1)} collective-permute-done((f32[104,128]{1,0:T(8,128)S(1)}, f32[104,128]{1,0:T(8,128)S(1)}, u32[]{:S(2)}, u32[]{:S(2)}) %collective-permute-start.9) | collective-permute-done | bytes 53280 | tf_op jit(solution)/shard_map/ppermute | solution.py:278
  50.2 2.3 %collective-permute-done.8 = f32[104,128]{1,0:T(8,128)S(1)} collective-permute-done((f32[104,128]{1,0:T(8,128)S(1)}, f32[104,128]{1,0:T(8,128)S(1)}, u32[]{:S(2)}, u32[]{:S(2)}) %collective-permute-start.8) | collective-permute-done | bytes 53280 | tf_op jit(solution)/shard_map/ppermute | solution.py:278
  52.6 0.0 collective-permute-done.7
  52.7 0.7 pad_maximum_fusion.1
  53.4 0.0 copy-start.1
  53.4 1.5 %collective-permute-start.10 = (f32[416,128]{1,0:T(8,128)}, f32[416,128]{1,0:T(8,128)}, u32[]{:S(2)}, u32[]{:S(2)}) collective-permute-start(f32[416,128]{1,0:T(8,128)} %pad_maximum_fusion.1), channel_id=1, source_target_pairs={{0,8},{8,0},{1,9},{9,1},{2,10},{10,2},{3,11},{11,3},{4,12},{12,4},... | collective-permute-start | bytes 638984 | tf_op jit(solution)/shard_map/ppermute | solution.py:278
  54.9 4.6 %collective-permute-done.10 = f32[416,128]{1,0:T(8,128)} collective-permute-done((f32[416,128]{1,0:T(8,128)}, f32[416,128]{1,0:T(8,128)}, u32[]{:S(2)}, u32[]{:S(2)}) %collective-permute-start.10) | collective-permute-done | bytes 213024 | tf_op jit(solution)/shard_map/ppermute | solution.py:278
  59.5 1.0 %constant_dynamic-update-slice_fusion.9 = (f32[832,128]{1,0:T(8,128)S(1)}, f32[832,128]{1,0:T(8,128)S(1)}) fusion(f32[416,128]{1,0:T(8,128)} %collective-permute-done.10, f32[832,128]{1,0:T(8,128)S(1)} %get-tuple-element.17), kind=kLoop, calls=%fused_computation.30 | loop fusion | bytes 638976
  60.6 0.1 collective-permute-start.11
  60.7 1.7 %collective-permute-done.11.other_ref = f32[832,128]{1,0:T(8,128)S(1)} collective-permute-done((f32[832,128]{1,0:T(8,128)S(1)}, f32[832,128]{1,0:T(8,128)S(1)}, u32[]{:S(2)}, u32[]{:S(2)}) %collective-permute-start.11) | collective-permute-done | bytes 426016 | tf_op jit(solution)/shard_map/ppermute | solution.py:286
  62.5 0.0 copy-done
  62.5 21.1 %shard_map.64 = bf16[512,128]{1,0:T(8,128)(2,1)S(1)} custom-call(s32[1]{0:T(128)} %bitcast.1.side_ref, f32[832,128]{1,0:T(8,128)S(1)} %broadcast_select_fusion.mine_ref, f32[832,128]{1,0:T(8,128)S(1)} %collective-permute-done.11.other_ref, bf16[512,512]{1,0:T(8,128)(2,1)S(1)} %get-tuple-element.11.pick_ref, f32[512,128]{1,0:T(8,128)S(1)} %copy-done), custom_call_target="tpu_custom_call" | custom-call | tf_op jit(solution)/shard_map/pallas_call | solution.py:482
  83.6 0.0 copy-done.1
  83.6 1.7 %fusion = f32[32,64,128]{2,1,0:T(8,128)} fusion(bf16[32,64,512]{2,1,0:T(8,128)(2,1)S(1)} %copy-done.1, pred[32]{0:T(512)(128)(4,1)S(1)} %iota_compare_fusion, bf16[512,128]{1,0:T(8,128)(2,1)S(1)} %shard_map.64), kind=kOutput, calls=%fused_computation | convolution fusion | flops 269484032 | bytes 3276832 | tf_op jit(solution)/shard_map/dot_general | solution.py:520
  (15 shorter events, 0.2 us)
Async XLA Ops:
  1.7 17.0 %collective-permute-start = (bf16[128,512]{1,0:T(8,128)(2,1)S(1)}, bf16[128,512]{1,0:T(8,128)(2,1)S(1)}, u32[]{:S(2)}, u32[]{:S(2)}) collective-permute-start(bf16[128,512]{1,0:T(8,128)(2,1)S(1)} %bitcast.60), channel_id=1, source_target_pairs={{0,1},{1,2},{2,3},{3,4},{4,5},{5,6},{6,7},{7,8},{8,9},{9,10},{10,1... | collective-permute-start | bytes 393224 | tf_op jit(solution)/shard_map/ppermute | solution.py:508
  5.0 13.8 %collective-permute-start.1 = (bf16[64,512]{1,0:T(8,128)(2,1)S(1)}, bf16[64,512]{1,0:T(8,128)(2,1)S(1)}, u32[]{:S(2)}, u32[]{:S(2)}) collective-permute-start(bf16[64,512]{1,0:T(8,128)(2,1)S(1)} %select_bitcast_fusion), channel_id=1, source_target_pairs={{1,0},{2,1},{3,2},{4,3},{5,4},{6,5},{7,6},{8,7},{9,8},{10,9},{11,1... | collective-permute-start | bytes 196616 | tf_op jit(solution)/shard_map/ppermute | solution.py:509
  18.8 0.6 copy-start.3
  18.8 0.7 copy-start.2
  22.4 4.8 %collective-permute-start.2 = (f32[832,128]{1,0:T(8,128)S(1)}, f32[832,128]{1,0:T(8,128)S(1)}, u32[]{:S(2)}, u32[]{:S(2)}) collective-permute-start(f32[832,128]{1,0:T(8,128)S(1)} %get-tuple-element.16), channel_id=1, source_target_pairs={{0,1},{1,0},{2,3},{3,2},{4,5},{5,4},{6,7},{7,6},{8,9},{9,8},{10,11... | collective-permute-start | bytes 1277960 | tf_op jit(solution)/shard_map/ppermute | solution.py:286
  27.2 10.2 %collective-permute-start.3 = (f32[416,128]{1,0:T(8,128)S(1)}, f32[416,128]{1,0:T(8,128)S(1)}, u32[]{:S(2)}, u32[]{:S(2)}) collective-permute-start(f32[416,128]{1,0:T(8,128)S(1)} %get-tuple-element.29), channel_id=1, source_target_pairs={{0,8},{8,0},{1,9},{9,1},{2,10},{10,2},{3,11},{11,3},{4,12},{12,4},... | collective-permute-start | bytes 638984 | tf_op jit(solution)/shard_map/ppermute | solution.py:271
  37.5 4.8 %collective-permute-start.6 = (f32[104,128]{1,0:T(8,128)S(1)}, f32[104,128]{1,0:T(8,128)S(1)}, u32[]{:S(2)}, u32[]{:S(2)}) collective-permute-start(f32[104,128]{1,0:T(8,128)S(1)} %get-tuple-element.26), channel_id=1, source_target_pairs={{0,6},{2,0},{4,2},{6,4},{1,7},{3,1},{5,3},{7,5},{8,14},{10,8},{12,... | collective-permute-start | bytes 159752 | tf_op jit(solution)/shard_map/ppermute | solution.py:271
  38.7 6.2 %collective-permute-start.5 = (f32[104,128]{1,0:T(8,128)S(1)}, f32[104,128]{1,0:T(8,128)S(1)}, u32[]{:S(2)}, u32[]{:S(2)}) collective-permute-start(f32[104,128]{1,0:T(8,128)S(1)} %get-tuple-element.27), channel_id=1, source_target_pairs={{0,4},{2,6},{4,0},{6,2},{1,5},{3,7},{5,1},{7,3},{8,12},{10,14},{12... | collective-permute-start | bytes 159752 | tf_op jit(solution)/shard_map/ppermute | solution.py:271
  38.7 6.2 %collective-permute-start.4 = (f32[104,128]{1,0:T(8,128)S(1)}, f32[104,128]{1,0:T(8,128)S(1)}, u32[]{:S(2)}, u32[]{:S(2)}) collective-permute-start(f32[104,128]{1,0:T(8,128)S(1)} %get-tuple-element.25), channel_id=1, source_target_pairs={{0,2},{2,4},{4,6},{6,0},{1,3},{3,5},{5,7},{7,1},{8,10},{10,12},{12... | collective-permute-start | bytes 159752 | tf_op jit(solution)/shard_map/ppermute | solution.py:271
  39.7 22.8 %copy-start = (f32[512,128]{1,0:T(8,128)S(1)}, f32[512,128]{1,0:T(8,128)}, u32[]{:S(2)}) copy-start(f32[512,128]{1,0:T(8,128)} %start_ref.1) | copy-start | bytes 786436
  44.9 5.3 %collective-permute-start.9 = (f32[104,128]{1,0:T(8,128)S(1)}, f32[104,128]{1,0:T(8,128)S(1)}, u32[]{:S(2)}, u32[]{:S(2)}) collective-permute-start(f32[104,128]{1,0:T(8,128)S(1)} %fusion.6), channel_id=1, source_target_pairs={{0,6},{2,0},{4,2},{6,4},{1,7},{3,1},{5,3},{7,5},{8,14},{10,8},{12,... | collective-permute-start | bytes 159752 | tf_op jit(solution)/shard_map/ppermute | solution.py:278
  46.4 6.2 %collective-permute-start.8 = (f32[104,128]{1,0:T(8,128)S(1)}, f32[104,128]{1,0:T(8,128)S(1)}, u32[]{:S(2)}, u32[]{:S(2)}) collective-permute-start(f32[104,128]{1,0:T(8,128)S(1)} %fusion.6), channel_id=1, source_target_pairs={{0,4},{2,6},{4,0},{6,2},{1,5},{3,7},{5,1},{7,3},{8,12},{10,14},{12... | collective-permute-start | bytes 159752 | tf_op jit(solution)/shard_map/ppermute | solution.py:278
  46.4 6.2 %collective-permute-start.7 = (f32[104,128]{1,0:T(8,128)S(1)}, f32[104,128]{1,0:T(8,128)S(1)}, u32[]{:S(2)}, u32[]{:S(2)}) collective-permute-start(f32[104,128]{1,0:T(8,128)S(1)} %fusion.6), channel_id=1, source_target_pairs={{0,2},{2,4},{4,6},{6,0},{1,3},{3,5},{5,7},{7,1},{8,10},{10,12},{12... | collective-permute-start | bytes 159752 | tf_op jit(solution)/shard_map/ppermute | solution.py:278
  53.4 30.2 %copy-start.1 = (bf16[32,64,512]{2,1,0:T(8,128)(2,1)S(1)}, bf16[32,64,512]{2,1,0:T(8,128)(2,1)}, u32[]{:S(2)}) copy-start(bf16[32,64,512]{2,1,0:T(8,128)(2,1)} %param.6) | copy-start | bytes 6291460
  53.4 6.2 %collective-permute-start.10 = (f32[416,128]{1,0:T(8,128)}, f32[416,128]{1,0:T(8,128)}, u32[]{:S(2)}, u32[]{:S(2)}) collective-permute-start(f32[416,128]{1,0:T(8,128)} %pad_maximum_fusion.1), channel_id=1, source_target_pairs={{0,8},{8,0},{1,9},{9,1},{2,10},{10,2},{3,11},{11,3},{4,12},{12,4},... | collective-permute-start | bytes 638984 | tf_op jit(solution)/shard_map/ppermute | solution.py:278
  60.6 1.8 %collective-permute-start.11 = (f32[832,128]{1,0:T(8,128)S(1)}, f32[832,128]{1,0:T(8,128)S(1)}, u32[]{:S(2)}, u32[]{:S(2)}) collective-permute-start(f32[832,128]{1,0:T(8,128)S(1)} %broadcast_select_fusion.mine_ref), channel_id=1, source_target_pairs={{0,1},{1,0},{2,3},{3,2},{4,5},{5,4},{6,7},{7,6},{8,9},{9,8},{10,11... | collective-permute-start | bytes 1277960 | tf_op jit(solution)/shard_map/ppermute | solution.py:286

commit v4 on v3

--- a/solution.py
+++ b/solution.py
@@ -82,18 +82,20 @@
     return total.astype(BF16)
 
 
-def packed_gram(field):
+def panel_grams(field):
+    return [
+        lax.dot_general(
+            field[:, low:], field[:, low : low + LANES], (((0,), (0,)), ((), ())), preferred_element_type=F32
+        )
+        for low in range(0, 4 * LANES, LANES)
+    ]
+
+
+def packed(panels):
     r = lax.broadcasted_iota(jnp.int32, (LANES, LANES), 0)
     c = lax.broadcasted_iota(jnp.int32, (LANES, LANES), 1)
-    corners, blocks = [], []
-    for panel in range(4):
-        low = panel * LANES
-        block = lax.dot_general(
-            field[:, low:], field[:, low : low + LANES], (((0,), (0,)), ((), ())), preferred_element_type=F32
-        )
-        corners.append(block[:LANES])
-        if panel < 3:
-            blocks.append((BELOW[panel], block[LANES : USED - low]))
+    corners = [block[:LANES] for block in panels]
+    blocks = [(BELOW[k], panels[k][LANES : USED - k * LANES]) for k in range(3)]
     blocks.append((SQUARE, jnp.where(r >= c, corners[0], corners[1])))
     blocks.append((THIRD, corners[2]))
     diagonal = jnp.sum(jnp.where(r == c, corners[1], 0.0), axis=0, keepdims=True)
@@ -105,7 +107,7 @@
 
 def inner_kernel(
     count_ref, mask_hbm, noise_hbm, smooth_hbm, x_hbm, noise_out, signal_out, pick_ref, taps,
-    x, xs, nf, sg, mask_ref, noise_ref, smooth_ref, sems, small_sems,
+    x, xs, nf, sg, sums, mask_ref, noise_ref, smooth_ref, sems, small_sems,
 ):
     height = x.shape[0] // 64
     bands = x.shape[1]
@@ -134,34 +136,59 @@
     position = lax.dot_general(ranks, mask, (((1,), (1,)), ((), ())), preferred_element_type=F32)[:, :1]
     pick_ref[...] = jnp.where(position == (c + 1024).astype(F32), 1.0, 0.0).astype(BF16)
     pick = pick_ref[...]
-    wide_pick = pick.astype(F32)
-    taps[:8, :] = mm(noise_ref[...], wide_pick)
-    taps[8:, :] = mm(jnp.concatenate([smooth_ref[...], jnp.zeros((7, bands), F32)], axis=0), wide_pick)
-    for k, copy in enumerate(copies):
+    weights = jnp.concatenate([noise_ref[...], smooth_ref[...], jnp.zeros((7, bands), F32)], axis=0)
+    weights = jnp.concatenate(three_parts(weights), axis=0).astype(BF16)
+    weights = jnp.dot(weights, pick, preferred_element_type=F32)
+    taps[...] = weights[:40] + (weights[40:80] + weights[80:])
+    for copy in copies:
         copy.wait()
-        values = jnp.dot(x[k * size : (k + 1) * size, :], pick, preferred_element_type=F32)
-        place(xs, values, size // 64, k * (size // 64), k * (size // 64), count)
-
-    def noise_body(row, carry):
-        start = pl.multiple_of((row - 1) * 64, 64)
+
+    def picked(k):
+        return jnp.dot(x[pl.ds(pl.multiple_of(k * 256, 256), 256), :], pick, preferred_element_type=F32)
+
+    def noise_row(row):
+        start = pl.multiple_of((row + 1) * 64, 64)
         for tile in range(4):
             lanes = slice(tile * LANES, (tile + 1) * LANES)
             even, odd = noise_tile(xs, taps, row, row < count, tile)
             nf[pl.ds(start, 32), lanes] = even
             nf[pl.ds(start + 32, 32), lanes] = odd
+
+    def add_gram(k):
+        chunk = nf[pl.ds(pl.multiple_of(k * 256, 256), 256), :]
+        for panel in range(4):
+            low = panel * LANES
+            sums[panel, low:, :] += lax.dot_general(
+                chunk[:, low:], chunk[:, low : low + LANES], (((0,), (0,)), ((), ())), preferred_element_type=F32
+            )
+
+    groups = height // 4
+    place(xs, picked(0), 4, 0, 0, count)
+    place(xs, picked(1), 4, 4, 4, count)
+    sums[...] = jnp.zeros_like(sums)
+    nf[:128, :] = jnp.zeros((128, bands), BF16)
+    noise_row(1)
+    noise_row(2)
+
+    def body(k, carry):
+        following = jnp.minimum(k + 1, groups - 1)
+        values = picked(following)
+        add_gram(k - 1)
+        for row in range(4):
+            noise_row(4 * k - 1 + row)
+        for half in range(2):
+            slot = 4 * k - 4 + 2 * half
+            start = pl.multiple_of((2 * k - 2 + half) * 32, 32)
+            for tile in range(4):
+                sg[pl.ds(start, 32), tile * LANES : (tile + 1) * LANES] = signal_tile(xs, taps, slot, tile)
+        place(xs, values, 4, following * 4, following * 4, count)
         return carry
 
-    lax.fori_loop(1, height - 1, noise_body, 0)
-
-    def signal_body(row, carry):
-        start = pl.multiple_of((row - 1) * 32, 32)
-        for tile in range(4):
-            sg[pl.ds(start, 32), tile * LANES : (tile + 1) * LANES] = signal_tile(xs, taps, 2 * row - 2, tile)
-        return carry
-
-    lax.fori_loop(1, height // 2 - 1, signal_body, 0)
-    for field, out_ref in ((nf, noise_out), (sg, signal_out)):
-        for start, block in packed_gram(field):
+    lax.fori_loop(1, groups, body, 0)
+    add_gram(groups - 1)
+    corners = [[sums[panel, panel * LANES :, :] for panel in range(4)], panel_grams(sg)]
+    for panels, out_ref in zip(corners, (noise_out, signal_out)):
+        for start, block in packed(panels):
             out_ref[start : start + block.shape[0], :] = block
 
 
@@ -196,7 +223,7 @@
             nf[k * 64 + 32 : k * 64 + 64, lanes] = odd
             sg[k * 32 : k * 32 + 32, lanes] = signal_tile(xs, taps, 5 * k, tile)
     for half, (field, inner) in enumerate(((nf, noise_ref), (sg, signal_ref))):
-        for start, block in packed_gram(field):
+        for start, block in packed(panel_grams(field)):
             rows = block.shape[0]
             block = block + inner[start : start + rows, :]
             if start == LAST:
@@ -210,7 +237,7 @@
 VMEM = pl.BlockSpec(memory_space=pltpu.VMEM)
 SMEM = pl.BlockSpec(memory_space=pltpu.SMEM)
 HBM = pl.BlockSpec(memory_space=pltpu.HBM)
-PARAMS = pltpu.CompilerParams(vmem_limit_bytes=48 << 20)
+PARAMS = pltpu.CompilerParams(vmem_limit_bytes=20 << 20)
 
 
 def inner(count, mask, noise_kernel, smooth_kernel, x):
@@ -224,8 +251,9 @@
         scratch_shapes=[
             pltpu.VMEM(x.shape, BF16),
             pltpu.VMEM((4 * (16 + height * PITCH), LANES), F32),
-            pltpu.VMEM(((height - 2) * 64, bands), BF16),
+            pltpu.VMEM((height * 64, bands), BF16),
             pltpu.VMEM(((height // 2 - 2) * 32, bands), BF16),
+            pltpu.VMEM((4, bands, LANES), F32),
             pltpu.VMEM(mask.shape, jnp.int32),
             pltpu.VMEM(noise_kernel.shape, F32),
             pltpu.VMEM(smooth_kernel.shape, F32),
@@ -489,7 +517,7 @@
             pltpu.VMEM((USED, 512), F32),
             pltpu.VMEM((USED, 512), F32),
         ],
-        compiler_params=pltpu.CompilerParams(vmem_limit_bytes=48 << 20),
+        compiler_params=pltpu.CompilerParams(vmem_limit_bytes=20 << 20),
     )(side, mine, other, pick, start_basis)
 
 

time: 85.6 us -> 83.3 us (0.973)
  Pallas kernels: 36.4 us -> 34.2 us
    pallas_call x1, Pallas kernels: 12.4 us -> 10.1 us  [inner(): pl.pallas_call(inner_kernel, out_shape=(gram, gram, jax.ShapeDtypeStruct(...]
  transfers between devices with their start and end apart: 12 -> 12, of which waited for: 8 -> 8; matrix products, arithmetic and copies ran while one was open for 1% -> 1% of each run, Pallas kernels for 15% -> 12%
where the time goes in v4:
time: 83.3 us; the launch traced here: 83.1 us
  Pallas kernels  34.2 us (41%)
  waiting for transfers between devices  23.2 us (28%)
  starting transfers between devices  18.5 us (22%)
  other arithmetic  2.87 us (3%)
  local copies, waits for them, and re-layouts  1.73 us (2%)
  matrix products  1.72 us (2%)
  between operations  0.88 us (1%)
    pallas_call x1, Pallas kernels, finish(): pl.pallas_call(finish_kernel, out_shape=jax.ShapeDtypeStruct((512, LANES)...  21.1 us
    ppermute x4, waiting for transfers between devices, scatter_sum(): lax.ppermute(sum(block((me + d) % n)), axis, [(i, (i + d) % n) for i in r...  10.7 us
    pallas_call x1, Pallas kernels, inner(): pl.pallas_call(inner_kernel, out_shape=(gram, gram, jax.ShapeDtypeStruct(...  10.1 us
    ppermute x4, waiting for transfers between devices, gather_rows(): lax.ppermute(x, axis, [(i, (i + d) % n) for i in range(n)])  9.3 us
    ppermute x4, starting transfers between devices, scatter_sum(): lax.ppermute(sum(block((me + d) % n)), axis, [(i, (i + d) % n) for i in r...  6.9 us
    ppermute x4, starting transfers between devices, gather_rows(): lax.ppermute(x, axis, [(i, (i + d) % n) for i in range(n)])  4.52 us
    ppermute x2, starting transfers between devices, exchange(): return lax.ppermute(x, 'sub', [(0, 1), (1, 0)])  3.44 us
    ppermute x2, waiting for transfers between devices, exchange(): return lax.ppermute(x, 'sub', [(0, 1), (1, 0)])  3.14 us
  transfers between devices with their start and end apart: 12, of which 8 were waited for; matrix products, arithmetic and copies ran while one was open for 1% of the time, Pallas kernels for 12%

profile of v4, /device:TPU:0, one launch (start us, length us, event | category | flops | bytes accessed | tf_op | source)
XLA Modules:
  0.0 83.1 jit_solution(16261619426655364701)
XLA Ops:
  0.7 0.1 slice_compare_fusion
  0.7 1.0 %slice_select_fusion = bf16[2,64,512]{2,1,0:T(8,128)(2,1)S(1)} fusion(bf16[32,64,512]{2,1,0:T(8,128)(2,1)} %param.6, pred[2]{0:T(512)(128)(4,1)S(1)} %slice_compare_fusion), kind=kLoop, calls=%fused_computation.9 | loop fusion | flops 65536 | bytes 262146 | tf_op jit(solution)/shard_map/jit(_where)/select_n | solution.py:534
  1.7 2.4 %collective-permute-start = (bf16[128,512]{1,0:T(8,128)(2,1)S(1)}, bf16[128,512]{1,0:T(8,128)(2,1)S(1)}, u32[]{:S(2)}, u32[]{:S(2)}) collective-permute-start(bf16[128,512]{1,0:T(8,128)(2,1)S(1)} %bitcast.60), channel_id=1, source_target_pairs={{0,1},{1,2},{2,3},{3,4},{4,5},{5,6},{6,7},{7,8},{8,9},{9,10},{10,1... | collective-permute-start | bytes 393224 | tf_op jit(solution)/shard_map/ppermute | solution.py:536
  4.1 0.8 %select_bitcast_fusion = bf16[64,512]{1,0:T(8,128)(2,1)S(1)} fusion(bf16[32,64,512]{2,1,0:T(8,128)(2,1)} %param.6, pred[]{:T(512)} %bitcast.4), kind=kLoop, calls=%fused_computation.10 | loop fusion | flops 32768 | bytes 131073 | tf_op jit(solution)/shard_map/reshape | solution.py:537
  5.0 1.3 %collective-permute-start.1 = (bf16[64,512]{1,0:T(8,128)(2,1)S(1)}, bf16[64,512]{1,0:T(8,128)(2,1)S(1)}, u32[]{:S(2)}, u32[]{:S(2)}) collective-permute-start(bf16[64,512]{1,0:T(8,128)(2,1)S(1)} %select_bitcast_fusion), channel_id=1, source_target_pairs={{1,0},{2,1},{3,2},{4,3},{5,4},{6,5},{7,6},{8,7},{9,8},{10,9},{11,1... | collective-permute-start | bytes 196616 | tf_op jit(solution)/shard_map/ppermute | solution.py:537
  6.3 10.1 %inner.1 = (f32[832,128]{1,0:T(8,128)S(1)}, f32[832,128]{1,0:T(8,128)S(1)}, bf16[512,512]{1,0:T(8,128)(2,1)S(1)}, f32[40,512]{1,0:T(8,128)S(1)}) custom-call(s32[1]{0:T(128)} %copy.15.count_ref, s32[1,512]{1,0:T(1,128)} %bitcast.64, f32[8,512]{1,0:T(8,128)} %noise_hbm.1, f32[25,512]{1,0:T(8,128)} %smooth_hbm.1, bf16[2048,512]{1,0:T(8,128)(2,1)} %bitcast.50), custom_call_target="tpu_custom_call" | custom-call | flops 6442450944 | bytes 8388608 | tf_op jit(solution)/shard_map/inner/pallas_call | solution.py:246
  16.4 0.1 pad_add_fusion.count_ref
  16.5 0.0 collective-permute-done.1.high_hbm
  16.5 0.0 copy-start.3
  16.5 0.0 collective-permute-done.low_hbm
  16.5 0.0 copy-start.2
  16.5 0.6 copy-done.3
  17.1 0.1 copy-done.2
  17.2 2.9 %edge.1 = (f32[832,128]{1,0:T(8,128)S(1)}, f32[832,128]{1,0:T(8,128)S(1)}) custom-call(s32[2]{0:T(128)S(1)} %pad_add_fusion.count_ref, bf16[128,512]{1,0:T(8,128)(2,1)} %copy-done.2, bf16[2048,512]{1,0:T(8,128)(2,1)} %bitcast.51, bf16[64,512]{1,0:T(8,128)(2,1)} %copy-done.3, bf16[512,512]{1,0:T(8,128)(2,1)S(1)} %get-tuple-element.11.pick_ref, ...), custom_call_target="tpu_custom_call" | custom-call | tf_op jit(solution)/shard_map/edge/pallas_call | solution.py:272
  20.2 3.4 %collective-permute-start.2 = (f32[832,128]{1,0:T(8,128)S(1)}, f32[832,128]{1,0:T(8,128)S(1)}, u32[]{:S(2)}, u32[]{:S(2)}) collective-permute-start(f32[832,128]{1,0:T(8,128)S(1)} %get-tuple-element.16), channel_id=1, source_target_pairs={{0,1},{1,0},{2,3},{3,2},{4,5},{5,4},{6,7},{7,6},{8,9},{9,8},{10,11... | collective-permute-start | bytes 1277960 | tf_op jit(solution)/shard_map/ppermute | solution.py:314
  23.5 1.4 %collective-permute-done.2 = f32[832,128]{1,0:T(8,128)S(1)} collective-permute-done((f32[832,128]{1,0:T(8,128)S(1)}, f32[832,128]{1,0:T(8,128)S(1)}, u32[]{:S(2)}, u32[]{:S(2)}) %collective-permute-start.2) | collective-permute-done | bytes 426016 | tf_op jit(solution)/shard_map/ppermute | solution.py:314
  24.9 0.1 constant_dynamic-slice_fusion.1
  25.0 4.7 %collective-permute-start.3 = (f32[416,128]{1,0:T(8,128)S(1)}, f32[416,128]{1,0:T(8,128)S(1)}, u32[]{:S(2)}, u32[]{:S(2)}) collective-permute-start(f32[416,128]{1,0:T(8,128)S(1)} %get-tuple-element.29), channel_id=1, source_target_pairs={{0,8},{8,0},{1,9},{9,1},{2,10},{10,2},{3,11},{11,3},{4,12},{12,4},... | collective-permute-start | bytes 638984 | tf_op jit(solution)/shard_map/ppermute | solution.py:299
  29.7 5.6 %collective-permute-done.3 = f32[416,128]{1,0:T(8,128)S(1)} collective-permute-done((f32[416,128]{1,0:T(8,128)S(1)}, f32[416,128]{1,0:T(8,128)S(1)}, u32[]{:S(2)}, u32[]{:S(2)}) %collective-permute-start.3) | collective-permute-done | bytes 213024 | tf_op jit(solution)/shard_map/ppermute | solution.py:299
  35.2 1.2 %collective-permute-start.6 = (f32[104,128]{1,0:T(8,128)S(1)}, f32[104,128]{1,0:T(8,128)S(1)}, u32[]{:S(2)}, u32[]{:S(2)}) collective-permute-start(f32[104,128]{1,0:T(8,128)S(1)} %get-tuple-element.26), channel_id=1, source_target_pairs={{0,6},{2,0},{4,2},{6,4},{1,7},{3,1},{5,3},{7,5},{8,14},{10,8},{12,... | collective-permute-start | bytes 159752 | tf_op jit(solution)/shard_map/ppermute | solution.py:299
  36.5 0.0 collective-permute-start.5
  36.5 1.0 %collective-permute-start.4 = (f32[104,128]{1,0:T(8,128)S(1)}, f32[104,128]{1,0:T(8,128)S(1)}, u32[]{:S(2)}, u32[]{:S(2)}) collective-permute-start(f32[104,128]{1,0:T(8,128)S(1)} %get-tuple-element.25), channel_id=1, source_target_pairs={{0,2},{2,4},{4,6},{6,0},{1,3},{3,5},{5,7},{7,1},{8,10},{10,12},{12... | collective-permute-start | bytes 159752 | tf_op jit(solution)/shard_map/ppermute | solution.py:299
  37.5 0.0 copy-start
  37.5 2.5 %collective-permute-done.6 = f32[104,128]{1,0:T(8,128)S(1)} collective-permute-done((f32[104,128]{1,0:T(8,128)S(1)}, f32[104,128]{1,0:T(8,128)S(1)}, u32[]{:S(2)}, u32[]{:S(2)}) %collective-permute-start.6) | collective-permute-done | bytes 53280 | tf_op jit(solution)/shard_map/ppermute | solution.py:299
  40.0 2.6 %collective-permute-done.5 = f32[104,128]{1,0:T(8,128)S(1)} collective-permute-done((f32[104,128]{1,0:T(8,128)S(1)}, f32[104,128]{1,0:T(8,128)S(1)}, u32[]{:S(2)}, u32[]{:S(2)}) %collective-permute-start.5) | collective-permute-done | bytes 53280 | tf_op jit(solution)/shard_map/ppermute | solution.py:299
  42.6 0.0 collective-permute-done.4
  42.7 1.5 %collective-permute-start.9 = (f32[104,128]{1,0:T(8,128)S(1)}, f32[104,128]{1,0:T(8,128)S(1)}, u32[]{:S(2)}, u32[]{:S(2)}) collective-permute-start(f32[104,128]{1,0:T(8,128)S(1)} %fusion.6), channel_id=1, source_target_pairs={{0,6},{2,0},{4,2},{6,4},{1,7},{3,1},{5,3},{7,5},{8,14},{10,8},{12,... | collective-permute-start | bytes 159752 | tf_op jit(solution)/shard_map/ppermute | solution.py:306
  44.1 0.0 collective-permute-start.8
  44.1 1.5 %collective-permute-start.7 = (f32[104,128]{1,0:T(8,128)S(1)}, f32[104,128]{1,0:T(8,128)S(1)}, u32[]{:S(2)}, u32[]{:S(2)}) collective-permute-start(f32[104,128]{1,0:T(8,128)S(1)} %fusion.6), channel_id=1, source_target_pairs={{0,2},{2,4},{4,6},{6,0},{1,3},{3,5},{5,7},{7,1},{8,10},{10,12},{12... | collective-permute-start | bytes 159752 | tf_op jit(solution)/shard_map/ppermute | solution.py:306
  45.7 2.3 %collective-permute-done.9 = f32[104,128]{1,0:T(8,128)S(1)} collective-permute-done((f32[104,128]{1,0:T(8,128)S(1)}, f32[104,128]{1,0:T(8,128)S(1)}, u32[]{:S(2)}, u32[]{:S(2)}) %collective-permute-start.9) | collective-permute-done | bytes 53280 | tf_op jit(solution)/shard_map/ppermute | solution.py:306
  48.0 2.3 %collective-permute-done.8 = f32[104,128]{1,0:T(8,128)S(1)} collective-permute-done((f32[104,128]{1,0:T(8,128)S(1)}, f32[104,128]{1,0:T(8,128)S(1)}, u32[]{:S(2)}, u32[]{:S(2)}) %collective-permute-start.8) | collective-permute-done | bytes 53280 | tf_op jit(solution)/shard_map/ppermute | solution.py:306
  50.3 0.0 collective-permute-done.7
  50.4 0.7 pad_maximum_fusion.1
  51.1 0.0 copy-start.1
  51.1 1.5 %collective-permute-start.10 = (f32[416,128]{1,0:T(8,128)}, f32[416,128]{1,0:T(8,128)}, u32[]{:S(2)}, u32[]{:S(2)}) collective-permute-start(f32[416,128]{1,0:T(8,128)} %pad_maximum_fusion.1), channel_id=1, source_target_pairs={{0,8},{8,0},{1,9},{9,1},{2,10},{10,2},{3,11},{11,3},{4,12},{12,4},... | collective-permute-start | bytes 638984 | tf_op jit(solution)/shard_map/ppermute | solution.py:306
  52.7 4.6 %collective-permute-done.10 = f32[416,128]{1,0:T(8,128)} collective-permute-done((f32[416,128]{1,0:T(8,128)}, f32[416,128]{1,0:T(8,128)}, u32[]{:S(2)}, u32[]{:S(2)}) %collective-permute-start.10) | collective-permute-done | bytes 213024 | tf_op jit(solution)/shard_map/ppermute | solution.py:306
  57.3 1.0 %constant_dynamic-update-slice_fusion.9 = (f32[832,128]{1,0:T(8,128)S(1)}, f32[832,128]{1,0:T(8,128)S(1)}) fusion(f32[416,128]{1,0:T(8,128)} %collective-permute-done.10, f32[832,128]{1,0:T(8,128)S(1)} %get-tuple-element.17), kind=kLoop, calls=%fused_computation.30 | loop fusion | bytes 638976
  58.3 0.1 broadcast_select_fusion.mine_ref
  58.4 0.1 collective-permute-start.11
  58.5 1.7 %collective-permute-done.11.other_ref = f32[832,128]{1,0:T(8,128)S(1)} collective-permute-done((f32[832,128]{1,0:T(8,128)S(1)}, f32[832,128]{1,0:T(8,128)S(1)}, u32[]{:S(2)}, u32[]{:S(2)}) %collective-permute-start.11) | collective-permute-done | bytes 426016 | tf_op jit(solution)/shard_map/ppermute | solution.py:314
  60.2 0.0 copy-done
  60.2 21.1 %shard_map.64 = bf16[512,128]{1,0:T(8,128)(2,1)S(1)} custom-call(s32[1]{0:T(128)} %bitcast.1.side_ref, f32[832,128]{1,0:T(8,128)S(1)} %broadcast_select_fusion.mine_ref, f32[832,128]{1,0:T(8,128)S(1)} %collective-permute-done.11.other_ref, bf16[512,512]{1,0:T(8,128)(2,1)S(1)} %get-tuple-element.11.pick_ref, f32[512,128]{1,0:T(8,128)S(1)} %copy-done), custom_call_target="tpu_custom_call" | custom-call | tf_op jit(solution)/shard_map/pallas_call | solution.py:510
  81.3 0.0 copy-done.1
  81.3 1.7 %fusion = f32[32,64,128]{2,1,0:T(8,128)} fusion(bf16[32,64,512]{2,1,0:T(8,128)(2,1)S(1)} %copy-done.1, pred[32]{0:T(512)(128)(4,1)S(1)} %iota_compare_fusion, bf16[512,128]{1,0:T(8,128)(2,1)S(1)} %shard_map.64), kind=kOutput, calls=%fused_computation | convolution fusion | flops 269484032 | bytes 3276832 | tf_op jit(solution)/shard_map/dot_general | solution.py:548
  (14 shorter events, 0.2 us)
Async XLA Ops:
  1.7 14.8 %collective-permute-start = (bf16[128,512]{1,0:T(8,128)(2,1)S(1)}, bf16[128,512]{1,0:T(8,128)(2,1)S(1)}, u32[]{:S(2)}, u32[]{:S(2)}) collective-permute-start(bf16[128,512]{1,0:T(8,128)(2,1)S(1)} %bitcast.60), channel_id=1, source_target_pairs={{0,1},{1,2},{2,3},{3,4},{4,5},{5,6},{6,7},{7,8},{8,9},{9,10},{10,1... | collective-permute-start | bytes 393224 | tf_op jit(solution)/shard_map/ppermute | solution.py:536
  5.0 11.5 %collective-permute-start.1 = (bf16[64,512]{1,0:T(8,128)(2,1)S(1)}, bf16[64,512]{1,0:T(8,128)(2,1)S(1)}, u32[]{:S(2)}, u32[]{:S(2)}) collective-permute-start(bf16[64,512]{1,0:T(8,128)(2,1)S(1)} %select_bitcast_fusion), channel_id=1, source_target_pairs={{1,0},{2,1},{3,2},{4,3},{5,4},{6,5},{7,6},{8,7},{9,8},{10,9},{11,1... | collective-permute-start | bytes 196616 | tf_op jit(solution)/shard_map/ppermute | solution.py:537
  16.5 0.6 copy-start.3
  16.5 0.7 copy-start.2
  20.2 4.8 %collective-permute-start.2 = (f32[832,128]{1,0:T(8,128)S(1)}, f32[832,128]{1,0:T(8,128)S(1)}, u32[]{:S(2)}, u32[]{:S(2)}) collective-permute-start(f32[832,128]{1,0:T(8,128)S(1)} %get-tuple-element.16), channel_id=1, source_target_pairs={{0,1},{1,0},{2,3},{3,2},{4,5},{5,4},{6,7},{7,6},{8,9},{9,8},{10,11... | collective-permute-start | bytes 1277960 | tf_op jit(solution)/shard_map/ppermute | solution.py:314
  25.0 10.2 %collective-permute-start.3 = (f32[416,128]{1,0:T(8,128)S(1)}, f32[416,128]{1,0:T(8,128)S(1)}, u32[]{:S(2)}, u32[]{:S(2)}) collective-permute-start(f32[416,128]{1,0:T(8,128)S(1)} %get-tuple-element.29), channel_id=1, source_target_pairs={{0,8},{8,0},{1,9},{9,1},{2,10},{10,2},{3,11},{11,3},{4,12},{12,4},... | collective-permute-start | bytes 638984 | tf_op jit(solution)/shard_map/ppermute | solution.py:299
  35.2 4.8 %collective-permute-start.6 = (f32[104,128]{1,0:T(8,128)S(1)}, f32[104,128]{1,0:T(8,128)S(1)}, u32[]{:S(2)}, u32[]{:S(2)}) collective-permute-start(f32[104,128]{1,0:T(8,128)S(1)} %get-tuple-element.26), channel_id=1, source_target_pairs={{0,6},{2,0},{4,2},{6,4},{1,7},{3,1},{5,3},{7,5},{8,14},{10,8},{12,... | collective-permute-start | bytes 159752 | tf_op jit(solution)/shard_map/ppermute | solution.py:299
  36.5 6.2 %collective-permute-start.5 = (f32[104,128]{1,0:T(8,128)S(1)}, f32[104,128]{1,0:T(8,128)S(1)}, u32[]{:S(2)}, u32[]{:S(2)}) collective-permute-start(f32[104,128]{1,0:T(8,128)S(1)} %get-tuple-element.27), channel_id=1, source_target_pairs={{0,4},{2,6},{4,0},{6,2},{1,5},{3,7},{5,1},{7,3},{8,12},{10,14},{12... | collective-permute-start | bytes 159752 | tf_op jit(solution)/shard_map/ppermute | solution.py:299
  36.5 6.2 %collective-permute-start.4 = (f32[104,128]{1,0:T(8,128)S(1)}, f32[104,128]{1,0:T(8,128)S(1)}, u32[]{:S(2)}, u32[]{:S(2)}) collective-permute-start(f32[104,128]{1,0:T(8,128)S(1)} %get-tuple-element.25), channel_id=1, source_target_pairs={{0,2},{2,4},{4,6},{6,0},{1,3},{3,5},{5,7},{7,1},{8,10},{10,12},{12... | collective-permute-start | bytes 159752 | tf_op jit(solution)/shard_map/ppermute | solution.py:299
  37.5 22.8 %copy-start = (f32[512,128]{1,0:T(8,128)S(1)}, f32[512,128]{1,0:T(8,128)}, u32[]{:S(2)}) copy-start(f32[512,128]{1,0:T(8,128)} %start_ref.1) | copy-start | bytes 786436
  42.7 5.3 %collective-permute-start.9 = (f32[104,128]{1,0:T(8,128)S(1)}, f32[104,128]{1,0:T(8,128)S(1)}, u32[]{:S(2)}, u32[]{:S(2)}) collective-permute-start(f32[104,128]{1,0:T(8,128)S(1)} %fusion.6), channel_id=1, source_target_pairs={{0,6},{2,0},{4,2},{6,4},{1,7},{3,1},{5,3},{7,5},{8,14},{10,8},{12,... | collective-permute-start | bytes 159752 | tf_op jit(solution)/shard_map/ppermute | solution.py:306
  44.1 6.2 %collective-permute-start.8 = (f32[104,128]{1,0:T(8,128)S(1)}, f32[104,128]{1,0:T(8,128)S(1)}, u32[]{:S(2)}, u32[]{:S(2)}) collective-permute-start(f32[104,128]{1,0:T(8,128)S(1)} %fusion.6), channel_id=1, source_target_pairs={{0,4},{2,6},{4,0},{6,2},{1,5},{3,7},{5,1},{7,3},{8,12},{10,14},{12... | collective-permute-start | bytes 159752 | tf_op jit(solution)/shard_map/ppermute | solution.py:306
  44.1 6.2 %collective-permute-start.7 = (f32[104,128]{1,0:T(8,128)S(1)}, f32[104,128]{1,0:T(8,128)S(1)}, u32[]{:S(2)}, u32[]{:S(2)}) collective-permute-start(f32[104,128]{1,0:T(8,128)S(1)} %fusion.6), channel_id=1, source_target_pairs={{0,2},{2,4},{4,6},{6,0},{1,3},{3,5},{5,7},{7,1},{8,10},{10,12},{12... | collective-permute-start | bytes 159752 | tf_op jit(solution)/shard_map/ppermute | solution.py:306
  51.1 30.2 %copy-start.1 = (bf16[32,64,512]{2,1,0:T(8,128)(2,1)S(1)}, bf16[32,64,512]{2,1,0:T(8,128)(2,1)}, u32[]{:S(2)}) copy-start(bf16[32,64,512]{2,1,0:T(8,128)(2,1)} %param.6) | copy-start | bytes 6291460
  51.1 6.2 %collective-permute-start.10 = (f32[416,128]{1,0:T(8,128)}, f32[416,128]{1,0:T(8,128)}, u32[]{:S(2)}, u32[]{:S(2)}) collective-permute-start(f32[416,128]{1,0:T(8,128)} %pad_maximum_fusion.1), channel_id=1, source_target_pairs={{0,8},{8,0},{1,9},{9,1},{2,10},{10,2},{3,11},{11,3},{4,12},{12,4},... | collective-permute-start | bytes 638984 | tf_op jit(solution)/shard_map/ppermute | solution.py:306
  58.4 1.8 %collective-permute-start.11 = (f32[832,128]{1,0:T(8,128)S(1)}, f32[832,128]{1,0:T(8,128)S(1)}, u32[]{:S(2)}, u32[]{:S(2)}) collective-permute-start(f32[832,128]{1,0:T(8,128)S(1)} %broadcast_select_fusion.mine_ref), channel_id=1, source_target_pairs={{0,1},{1,0},{2,3},{3,2},{4,5},{5,4},{6,7},{7,6},{8,9},{9,8},{10,11... | collective-permute-start | bytes 1277960 | tf_op jit(solution)/shard_map/ppermute | solution.py:314

commit v5 on v4

--- a/solution.py
+++ b/solution.py
@@ -69,7 +69,7 @@
     return jnp.where(valid, even, 0.0).astype(BF16), jnp.where(valid, odd, 0.0).astype(BF16)
 
 
-def signal_tile(xs, taps, slot, tile):
+def signal_tile(xs, taps, slot, tile, valid=None):
     pitch = xs.shape[0] // 4
     lanes = slice(tile * LANES, (tile + 1) * LANES)
     total = None
@@ -79,6 +79,8 @@
             k = 8 + 5 * i + j
             term = taps[k : k + 1, lanes] * xs[pl.ds(base + j - 2, 32, stride=2), :]
             total = term if total is None else total + term
+    if valid is not None:
+        total = jnp.where(valid, total, 0.0)
     return total.astype(BF16)
 
 
@@ -193,13 +195,12 @@
 
 
 def edge_kernel(
-    count_ref, low_hbm, x_hbm, high_hbm, pick_ref, taps, noise_ref, signal_ref, keep_ref, send_ref,
-    rows, both, xs, nf, sg, sems,
+    state_ref, low_hbm, x_hbm, pick_ref, taps, noise_ref, signal_ref, keep_ref, send_ref, rows, both, xs, nf, sg, sems
 ):
-    count, side = count_ref[0], count_ref[1]
+    count, side, first, last = [state_ref[k] for k in range(4)]
     size = x_hbm.shape[0]
     height = size // 64
-    pieces = ((low_hbm, 0, 128), (x_hbm.at[pl.ds(0, 192)], 128, 192), (x_hbm.at[pl.ds(size - 256, 256)], 320, 256), (high_hbm, 576, 64))
+    pieces = ((low_hbm, 0, 272), (x_hbm.at[pl.ds(0, 192)], 272, 192), (x_hbm.at[pl.ds(size - 256, 256)], 464, 256))
     copies = [
         pltpu.make_async_copy(source, rows.at[pl.ds(start, length)], sems.at[k])
         for k, (source, start, length) in enumerate(pieces)
@@ -207,29 +208,36 @@
     for copy in copies:
         copy.start()
     pick = pick_ref[...]
-    clear_gaps(xs, 10)
+    clear_gaps(xs, 12)
+    pitch = xs.shape[0] // 4
+    for tile in range(4):
+        start = tile * pitch + 8 + 11 * PITCH
+        xs[start : start + 64, :] = jnp.zeros((64, LANES), F32)
     for copy in copies:
         copy.wait()
     values = jnp.dot(rows[...], pick, preferred_element_type=F32)
-    place(xs, values[:128], 2, 0, 0, None)
-    place(xs, values[128:320], 3, 2, 0, count)
-    place(xs, values[320:576], 4, 5, height - 4, count)
-    place(xs, values[576:], 1, 9, 0, None)
-    for k, (slot, valid) in enumerate(((2, count > 0), (8, count > height - 1))):
-        for tile in range(4):
-            lanes = slice(tile * LANES, (tile + 1) * LANES)
+    place(xs, values[:256], 4, 0, 0, None)
+    place(xs, values[272:464], 3, 4, 0, count)
+    place(xs, values[464:], 4, 7, height - 4, count)
+    before = jnp.broadcast_to(rows[256:272, :LANES].astype(F32)[:1], (32, LANES))
+    noise_rows = ((3, before > float(height - 1)), (4, count > 0), (10, (last == 1) & (count > height - 1)))
+    signal_rows = ((0, first == 0), (2, None), (7, last == 1))
+    for tile in range(4):
+        lanes = slice(tile * LANES, (tile + 1) * LANES)
+        for k, (slot, valid) in enumerate(noise_rows):
             even, odd = noise_tile(xs, taps, slot, valid, tile)
             nf[k * 64 : k * 64 + 32, lanes] = even
             nf[k * 64 + 32 : k * 64 + 64, lanes] = odd
-            sg[k * 32 : k * 32 + 32, lanes] = signal_tile(xs, taps, 5 * k, tile)
+        for k, (slot, valid) in enumerate(signal_rows):
+            sg[k * 32 : k * 32 + 32, lanes] = signal_tile(xs, taps, slot, tile, valid)
     for half, (field, inner) in enumerate(((nf, noise_ref), (sg, signal_ref))):
         for start, block in packed(panel_grams(field)):
-            rows = block.shape[0]
-            block = block + inner[start : start + rows, :]
+            length = block.shape[0]
+            block = block + inner[start : start + length, :]
             if start == LAST:
                 row = lax.broadcasted_iota(jnp.int32, block.shape, 0)
                 block = jnp.where(row == 46, count.astype(F32), block)
-            both[half * PACKED + start : half * PACKED + start + rows, :] = block
+            both[half * PACKED + start : half * PACKED + start + length, :] = block
     keep_ref[...] = both[pl.ds(pl.multiple_of(side * PACKED, 8), PACKED), :]
     send_ref[...] = both[pl.ds(pl.multiple_of((1 - side) * PACKED, 8), PACKED), :]
 
@@ -266,25 +274,25 @@
     )(count, *(pltpu.with_memory_space_constraint(a, pltpu.HBM) for a in (mask, noise_kernel, smooth_kernel, x)))
 
 
-def edge(counts, low, x, high, pick, taps, noise, signal):
+def edge(state, low, x, pick, taps, noise, signal):
     bands = x.shape[1]
     gram = jax.ShapeDtypeStruct((PACKED, LANES), F32)
     return pl.pallas_call(
         edge_kernel,
         out_shape=(gram, gram),
-        in_specs=[SMEM, HBM, HBM, HBM, VMEM, VMEM, VMEM, VMEM],
+        in_specs=[SMEM, HBM, HBM, VMEM, VMEM, VMEM, VMEM],
         out_specs=(VMEM, VMEM),
         scratch_shapes=[
-            pltpu.VMEM((640, bands), BF16),
+            pltpu.VMEM((720, bands), BF16),
             pltpu.VMEM((2 * PACKED, LANES), F32),
-            pltpu.VMEM((4 * (16 + 10 * PITCH), LANES), F32),
-            pltpu.VMEM((128, bands), BF16),
-            pltpu.VMEM((64, bands), BF16),
-            pltpu.SemaphoreType.DMA((4,)),
+            pltpu.VMEM((4 * (16 + 12 * PITCH), LANES), F32),
+            pltpu.VMEM((192, bands), BF16),
+            pltpu.VMEM((96, bands), BF16),
+            pltpu.SemaphoreType.DMA((3,)),
         ],
         compiler_params=PARAMS,
         name="edge",
-    )(counts, *(pltpu.with_memory_space_constraint(a, pltpu.HBM) for a in (low, x, high)), pick, taps, noise, signal)
+    )(state, *(pltpu.with_memory_space_constraint(a, pltpu.HBM) for a in (low, x)), pick, taps, noise, signal)
 
 
 def scatter_sum(parts, axis):
@@ -414,6 +422,21 @@
     return tiles
 
 
+def split_parts(x):
+    return [part.astype(BF16) for part in three_parts(x)]
+
+
+def stacked(a, parts, side=0):
+    n = a.shape[0]
+    rows = jnp.concatenate(split_parts(a), axis=0)
+    first, second, third = [
+        lax.dot_general(rows[: (3 - k) * n], part, (((1,), (side,)), ((), ())), preferred_element_type=F32)
+        for k, part in enumerate(parts)
+    ]
+    small = first[2 * n :] + second[n:] + third
+    return first[:n] + (first[n : 2 * n] + second[:n] + small)
+
+
 def factor_block(block):
     tiles = [block[8 * m : 8 * m + 8, :] for m in range(block.shape[0] // 8)]
     return jnp.concatenate(inverse_factor(tiles), axis=0)
@@ -489,13 +512,15 @@
             inverse[low : low + LANES, :low] = left
             known = jnp.concatenate([known[LANES:] + mm(below, left), gain], axis=1)
 
-    turned = mm(basis, inverse[...])
-    mapped = mm(mm(turned[:, :USED], signal[...]), inverse[...], ((1,), (1,)))
+    inverse_parts = split_parts(inverse[...])
+    signal_parts = split_parts(signal[...])
+    turned = stacked(basis, inverse_parts)
+    mapped = stacked(stacked(turned[:, :USED], signal_parts), inverse_parts, 1)
     for sweep in range(SWEEPS):
         square = mm(mapped, mapped, ((1,), (1,)))
-        turned = mm(mapped, inverse[...])
+        turned = stacked(mapped, inverse_parts)
         if sweep + 1 < SWEEPS:
-            ahead = mm(mm(turned[:, :USED], signal[...]), inverse[...], ((1,), (1,)))
+            ahead = stacked(stacked(turned[:, :USED], signal_parts), inverse_parts, 1)
         scale = factor_block(square)
         if sweep + 1 < SWEEPS:
             mapped = mm(scale, ahead)
@@ -528,21 +553,20 @@
     for axis in AXES:
         chain *= lax.axis_size(axis)
     up = [(i, i + 1) for i in range(chain - 1)]
-    down = [(i + 1, i) for i in range(chain - 1)]
     row = jnp.arange(height, dtype=jnp.int32)
     zero = jnp.zeros((), radiance.dtype)
-    tail = jnp.where((row[-2:] < count)[:, None, None], radiance[-2:], zero)
-    lead = jnp.where((row[:1] < count)[:, None, None], radiance[:1], zero)
-    low = lax.ppermute(tail.reshape(2 * across, bands), AXES, up)
-    high = lax.ppermute(lead.reshape(across, bands), AXES, down)
-
     flat = radiance.reshape(height * across, bands)
+    tail = jnp.where((row[-4:] < count)[:, None, None], radiance[-4:], zero).reshape(4 * across, bands)
+    tail = jnp.concatenate([tail, jnp.full((16, bands), count, radiance.dtype)], axis=0)
+    low = lax.ppermute(tail, AXES, up)
+
     noise, signal, pick, taps = inner(row_counts, band_mask[None], noise_kernel, smooth_kernel, flat)
-    side = lax.axis_index("sub").astype(jnp.int32)
-    counts = jnp.stack([count, side])
-    keep, send = edge(counts, low, flat, high, pick, taps, noise, signal)
+    side = lax.axis_index("sub")
+    place_in_chain = lax.axis_index(AXES)
+    state = jnp.stack([count, side, place_in_chain == 0, place_in_chain == chain - 1]).astype(jnp.int32)
+    keep, send = edge(state, low, flat, pick, taps, noise, signal)
     mine, other = total_sum(keep, send)
-    weights = finish(side[None], mine, other, pick, start_basis)
+    weights = finish(state[1:2], mine, other, pick, start_basis)
     keep = jnp.repeat(row < count, across)
     masked = jnp.where(keep[:, None], flat, zero)
     result = jnp.dot(masked, weights, preferred_element_type=F32)

time: 83.3 us -> 79.8 us (0.958)
  starting transfers between devices: 18.5 us -> 15.9 us
    ppermute x2 -> x1, starting transfers between devices: 3.64 us -> 2.37 us  [local(): low = lax.ppermute(tail, AXES, up)]
    reshape x1 -> x0, other arithmetic: 0.85 us -> none  [local(): high = lax.ppermute(lead.reshape(across, bands), AXES, down)]
    unnamed x16 -> x14, local copies, waits for them, and re-layouts: 1.72 us -> 1.76 us
  transfers between devices with their start and end apart: 12 -> 11, of which waited for: 8 -> 10; matrix products, arithmetic and copies ran while one was open for 1% -> 0% of each run, Pallas kernels for 12% -> 13%
where the time goes in v5:
time: 79.8 us; the launch traced here: 79.6 us
  Pallas kernels  34.2 us (43%)
  waiting for transfers between devices  23 us (29%)
  starting transfers between devices  15.9 us (20%)
  other arithmetic  2.08 us (3%)
  local copies, waits for them, and re-layouts  1.79 us (2%)
  matrix products  1.72 us (2%)
  between operations  0.84 us (1%)
    pallas_call x1, Pallas kernels, finish(): pl.pallas_call(finish_kernel, out_shape=jax.ShapeDtypeStruct((512, LANES)...  20.8 us
    ppermute x4, waiting for transfers between devices, scatter_sum(): lax.ppermute(sum(block((me + d) % n)), axis, [(i, (i + d) % n) for i in r...  10.5 us
    pallas_call x1, Pallas kernels, inner(): pl.pallas_call(inner_kernel, out_shape=(gram, gram, jax.ShapeDtypeStruct(...  10.1 us
    ppermute x4, waiting for transfers between devices, gather_rows(): lax.ppermute(x, axis, [(i, (i + d) % n) for i in range(n)])  9.33 us
    ppermute x4, starting transfers between devices, scatter_sum(): lax.ppermute(sum(block((me + d) % n)), axis, [(i, (i + d) % n) for i in r...  6.23 us
    ppermute x4, starting transfers between devices, gather_rows(): lax.ppermute(x, axis, [(i, (i + d) % n) for i in range(n)])  4.52 us
    pallas_call x1, Pallas kernels, edge(): pl.pallas_call(edge_kernel, out_shape=(gram, gram), in_specs=[SMEM, HBM,...  3.32 us
    ppermute x2, waiting for transfers between devices, exchange(): return lax.ppermute(x, 'sub', [(0, 1), (1, 0)])  3.14 us
  transfers between devices with their start and end apart: 11, of which 10 were waited for; matrix products, arithmetic and copies ran while one was open for 0% of the time, Pallas kernels for 13%

profile of v5, /device:TPU:0, one launch (start us, length us, event | category | flops | bytes accessed | tf_op | source)
XLA Modules:
  0.0 79.6 jit_solution(5028267930089801035)
XLA Ops:
  0.7 0.1 slice_compare_fusion
  0.7 1.0 %slice_select_fusion = bf16[4,64,512]{2,1,0:T(8,128)(2,1)S(1)} fusion(bf16[32,64,512]{2,1,0:T(8,128)(2,1)} %param.6, pred[4]{0:T(512)(128)(4,1)S(1)} %slice_compare_fusion), kind=kLoop, calls=%fused_computation.4 | loop fusion | flops 131072 | bytes 524292 | tf_op jit(solution)/shard_map/jit(_where)/select_n | solution.py:559
  1.8 2.4 %collective-permute-start = (bf16[272,512]{1,0:T(8,128)(2,1)S(1)}, bf16[272,512]{1,0:T(8,128)(2,1)S(1)}, u32[]{:S(2)}, u32[]{:S(2)}) collective-permute-start(bf16[272,512]{1,0:T(8,128)(2,1)S(1)} %concatenate.14), channel_id=1, source_target_pairs={{0,1},{1,2},{2,3},{3,4},{4,5},{5,6},{6,7},{7,8},{8,9},{9,10},{10,1... | collective-permute-start | bytes 835592 | tf_op jit(solution)/shard_map/ppermute | solution.py:561
  4.2 10.1 %inner.1 = (f32[832,128]{1,0:T(8,128)S(1)}, f32[832,128]{1,0:T(8,128)S(1)}, bf16[512,512]{1,0:T(8,128)(2,1)S(1)}, f32[40,512]{1,0:T(8,128)S(1)}) custom-call(s32[1]{0:T(128)} %copy.15.count_ref, s32[1,512]{1,0:T(1,128)} %bitcast.63, f32[8,512]{1,0:T(8,128)} %noise_hbm.1, f32[25,512]{1,0:T(8,128)} %smooth_hbm.1, bf16[2048,512]{1,0:T(8,128)(2,1)} %bitcast.49), custom_call_target="tpu_custom_call" | custom-call | flops 6442450944 | bytes 8388608 | tf_op jit(solution)/shard_map/inner/pallas_call | solution.py:254
  14.4 0.1 pad_add_fusion.state_ref
  14.4 0.0 collective-permute-done.low_hbm
  14.4 0.0 copy-start.2
  14.4 0.7 copy-done.2
  15.2 3.3 %edge.1 = (f32[832,128]{1,0:T(8,128)S(1)}, f32[832,128]{1,0:T(8,128)S(1)}) custom-call(s32[4]{0:T(128)S(1)} %pad_add_fusion.state_ref, bf16[272,512]{1,0:T(8,128)(2,1)} %copy-done.2, bf16[2048,512]{1,0:T(8,128)(2,1)} %bitcast.50, bf16[512,512]{1,0:T(8,128)(2,1)S(1)} %get-tuple-element.11.pick_ref, f32[40,512]{1,0:T(8,128)S(1)} %get-tuple-element.12.taps, ...), custom_call_target="tpu_custom_call" | custom-call | tf_op jit(solution)/shard_map/edge/pallas_call | solution.py:280
  18.5 2.7 %collective-permute-start.1 = (f32[832,128]{1,0:T(8,128)S(1)}, f32[832,128]{1,0:T(8,128)S(1)}, u32[]{:S(2)}, u32[]{:S(2)}) collective-permute-start(f32[832,128]{1,0:T(8,128)S(1)} %get-tuple-element.16), channel_id=1, source_target_pairs={{0,1},{1,0},{2,3},{3,2},{4,5},{5,4},{6,7},{7,6},{8,9},{9,8},{10,11... | collective-permute-start | bytes 1277960 | tf_op jit(solution)/shard_map/ppermute | solution.py:322
  21.2 1.4 %collective-permute-done.1 = f32[832,128]{1,0:T(8,128)S(1)} collective-permute-done((f32[832,128]{1,0:T(8,128)S(1)}, f32[832,128]{1,0:T(8,128)S(1)}, u32[]{:S(2)}, u32[]{:S(2)}) %collective-permute-start.1) | collective-permute-done | bytes 426016 | tf_op jit(solution)/shard_map/ppermute | solution.py:322
  22.6 0.1 constant_dynamic-slice_fusion.1
  22.7 1.6 %collective-permute-start.2 = (f32[416,128]{1,0:T(8,128)S(1)}, f32[416,128]{1,0:T(8,128)S(1)}, u32[]{:S(2)}, u32[]{:S(2)}) collective-permute-start(f32[416,128]{1,0:T(8,128)S(1)} %get-tuple-element.29), channel_id=1, source_target_pairs={{0,8},{8,0},{1,9},{9,1},{2,10},{10,2},{3,11},{11,3},{4,12},{12,4},... | collective-permute-start | bytes 638984 | tf_op jit(solution)/shard_map/ppermute | solution.py:307
  24.2 6.0 %collective-permute-done.2 = f32[416,128]{1,0:T(8,128)S(1)} collective-permute-done((f32[416,128]{1,0:T(8,128)S(1)}, f32[416,128]{1,0:T(8,128)S(1)}, u32[]{:S(2)}, u32[]{:S(2)}) %collective-permute-start.2) | collective-permute-done | bytes 213024 | tf_op jit(solution)/shard_map/ppermute | solution.py:307
  30.3 3.2 %collective-permute-start.5 = (f32[104,128]{1,0:T(8,128)S(1)}, f32[104,128]{1,0:T(8,128)S(1)}, u32[]{:S(2)}, u32[]{:S(2)}) collective-permute-start(f32[104,128]{1,0:T(8,128)S(1)} %get-tuple-element.26), channel_id=1, source_target_pairs={{0,6},{2,0},{4,2},{6,4},{1,7},{3,1},{5,3},{7,5},{8,14},{10,8},{12,... | collective-permute-start | bytes 159752 | tf_op jit(solution)/shard_map/ppermute | solution.py:307
  33.5 0.0 collective-permute-start.4
  33.5 1.4 %collective-permute-start.3 = (f32[104,128]{1,0:T(8,128)S(1)}, f32[104,128]{1,0:T(8,128)S(1)}, u32[]{:S(2)}, u32[]{:S(2)}) collective-permute-start(f32[104,128]{1,0:T(8,128)S(1)} %get-tuple-element.25), channel_id=1, source_target_pairs={{0,2},{2,4},{4,6},{6,0},{1,3},{3,5},{5,7},{7,1},{8,10},{10,12},{12... | collective-permute-start | bytes 159752 | tf_op jit(solution)/shard_map/ppermute | solution.py:307
  35.0 0.0 copy-start
  35.0 0.5 collective-permute-done.5
  35.5 3.1 %collective-permute-done.4 = f32[104,128]{1,0:T(8,128)S(1)} collective-permute-done((f32[104,128]{1,0:T(8,128)S(1)}, f32[104,128]{1,0:T(8,128)S(1)}, u32[]{:S(2)}, u32[]{:S(2)}) %collective-permute-start.4) | collective-permute-done | bytes 53280 | tf_op jit(solution)/shard_map/ppermute | solution.py:307
  38.6 0.9 %collective-permute-done.3 = f32[104,128]{1,0:T(8,128)S(1)} collective-permute-done((f32[104,128]{1,0:T(8,128)S(1)}, f32[104,128]{1,0:T(8,128)S(1)}, u32[]{:S(2)}, u32[]{:S(2)}) %collective-permute-start.3) | collective-permute-done | bytes 53280 | tf_op jit(solution)/shard_map/ppermute | solution.py:307
  39.5 1.7 %collective-permute-start.8 = (f32[104,128]{1,0:T(8,128)S(1)}, f32[104,128]{1,0:T(8,128)S(1)}, u32[]{:S(2)}, u32[]{:S(2)}) collective-permute-start(f32[104,128]{1,0:T(8,128)S(1)} %fusion.6), channel_id=1, source_target_pairs={{0,6},{2,0},{4,2},{6,4},{1,7},{3,1},{5,3},{7,5},{8,14},{10,8},{12,... | collective-permute-start | bytes 159752 | tf_op jit(solution)/shard_map/ppermute | solution.py:314
  41.2 0.0 collective-permute-start.7
  41.2 1.8 %collective-permute-start.6 = (f32[104,128]{1,0:T(8,128)S(1)}, f32[104,128]{1,0:T(8,128)S(1)}, u32[]{:S(2)}, u32[]{:S(2)}) collective-permute-start(f32[104,128]{1,0:T(8,128)S(1)} %fusion.6), channel_id=1, source_target_pairs={{0,2},{2,4},{4,6},{6,0},{1,3},{3,5},{5,7},{7,1},{8,10},{10,12},{12... | collective-permute-start | bytes 159752 | tf_op jit(solution)/shard_map/ppermute | solution.py:314
  42.9 0.7 collective-permute-done.8
  43.7 2.9 %collective-permute-done.7 = f32[104,128]{1,0:T(8,128)S(1)} collective-permute-done((f32[104,128]{1,0:T(8,128)S(1)}, f32[104,128]{1,0:T(8,128)S(1)}, u32[]{:S(2)}, u32[]{:S(2)}) %collective-permute-start.7) | collective-permute-done | bytes 53280 | tf_op jit(solution)/shard_map/ppermute | solution.py:314
  46.6 0.6 collective-permute-done.6
  47.3 0.7 pad_maximum_fusion.1
  48.0 0.0 copy-start.1
  48.0 1.1 %collective-permute-start.9 = (f32[416,128]{1,0:T(8,128)}, f32[416,128]{1,0:T(8,128)}, u32[]{:S(2)}, u32[]{:S(2)}) collective-permute-start(f32[416,128]{1,0:T(8,128)} %pad_maximum_fusion.1), channel_id=1, source_target_pairs={{0,8},{8,0},{1,9},{9,1},{2,10},{10,2},{3,11},{11,3},{4,12},{12,4},... | collective-permute-start | bytes 638984 | tf_op jit(solution)/shard_map/ppermute | solution.py:314
  49.1 5.1 %collective-permute-done.9 = f32[416,128]{1,0:T(8,128)} collective-permute-done((f32[416,128]{1,0:T(8,128)}, f32[416,128]{1,0:T(8,128)}, u32[]{:S(2)}, u32[]{:S(2)}) %collective-permute-start.9) | collective-permute-done | bytes 213024 | tf_op jit(solution)/shard_map/ppermute | solution.py:314
  54.2 1.0 %constant_dynamic-update-slice_fusion.9 = (f32[832,128]{1,0:T(8,128)S(1)}, f32[832,128]{1,0:T(8,128)S(1)}) fusion(f32[416,128]{1,0:T(8,128)} %collective-permute-done.9, f32[832,128]{1,0:T(8,128)S(1)} %get-tuple-element.17), kind=kLoop, calls=%fused_computation.29 | loop fusion | bytes 638976
  55.2 0.1 broadcast_select_fusion.mine_ref
  55.2 0.1 collective-permute-start.10
  55.3 1.7 %collective-permute-done.10.other_ref = f32[832,128]{1,0:T(8,128)S(1)} collective-permute-done((f32[832,128]{1,0:T(8,128)S(1)}, f32[832,128]{1,0:T(8,128)S(1)}, u32[]{:S(2)}, u32[]{:S(2)}) %collective-permute-start.10) | collective-permute-done | bytes 426016 | tf_op jit(solution)/shard_map/ppermute | solution.py:322
  57.1 0.0 copy-done
  57.1 20.8 %shard_map.64 = bf16[512,128]{1,0:T(8,128)(2,1)S(1)} custom-call(s32[1]{0:T(128)} %bitcast.1.side_ref, f32[832,128]{1,0:T(8,128)S(1)} %broadcast_select_fusion.mine_ref, f32[832,128]{1,0:T(8,128)S(1)} %collective-permute-done.10.other_ref, bf16[512,512]{1,0:T(8,128)(2,1)S(1)} %get-tuple-element.11.pick_ref, f32[512,128]{1,0:T(8,128)S(1)} %copy-done), custom_call_target="tpu_custom_call" | custom-call | tf_op jit(solution)/shard_map/pallas_call | solution.py:535
  77.9 0.0 copy-done.1
  77.9 1.7 %fusion = f32[32,64,128]{2,1,0:T(8,128)} fusion(bf16[32,64,512]{2,1,0:T(8,128)(2,1)S(1)} %copy-done.1, pred[32]{0:T(512)(128)(4,1)S(1)} %iota_compare_fusion, bf16[512,128]{1,0:T(8,128)(2,1)S(1)} %shard_map.64), kind=kOutput, calls=%fused_computation | convolution fusion | flops 269484032 | bytes 3276832 | tf_op jit(solution)/shard_map/dot_general | solution.py:572
  (14 shorter events, 0.2 us)
Async XLA Ops:
  1.8 12.6 %collective-permute-start = (bf16[272,512]{1,0:T(8,128)(2,1)S(1)}, bf16[272,512]{1,0:T(8,128)(2,1)S(1)}, u32[]{:S(2)}, u32[]{:S(2)}) collective-permute-start(bf16[272,512]{1,0:T(8,128)(2,1)S(1)} %concatenate.14), channel_id=1, source_target_pairs={{0,1},{1,2},{2,3},{3,4},{4,5},{5,6},{6,7},{7,8},{8,9},{9,10},{10,1... | collective-permute-start | bytes 835592 | tf_op jit(solution)/shard_map/ppermute | solution.py:561
  14.4 0.7 copy-start.2
  18.5 4.1 %collective-permute-start.1 = (f32[832,128]{1,0:T(8,128)S(1)}, f32[832,128]{1,0:T(8,128)S(1)}, u32[]{:S(2)}, u32[]{:S(2)}) collective-permute-start(f32[832,128]{1,0:T(8,128)S(1)} %get-tuple-element.16), channel_id=1, source_target_pairs={{0,1},{1,0},{2,3},{3,2},{4,5},{5,4},{6,7},{7,6},{8,9},{9,8},{10,11... | collective-permute-start | bytes 1277960 | tf_op jit(solution)/shard_map/ppermute | solution.py:322
  22.7 7.6 %collective-permute-start.2 = (f32[416,128]{1,0:T(8,128)S(1)}, f32[416,128]{1,0:T(8,128)S(1)}, u32[]{:S(2)}, u32[]{:S(2)}) collective-permute-start(f32[416,128]{1,0:T(8,128)S(1)} %get-tuple-element.29), channel_id=1, source_target_pairs={{0,8},{8,0},{1,9},{9,1},{2,10},{10,2},{3,11},{11,3},{4,12},{12,4},... | collective-permute-start | bytes 638984 | tf_op jit(solution)/shard_map/ppermute | solution.py:307
  30.3 5.2 %collective-permute-start.5 = (f32[104,128]{1,0:T(8,128)S(1)}, f32[104,128]{1,0:T(8,128)S(1)}, u32[]{:S(2)}, u32[]{:S(2)}) collective-permute-start(f32[104,128]{1,0:T(8,128)S(1)} %get-tuple-element.26), channel_id=1, source_target_pairs={{0,6},{2,0},{4,2},{6,4},{1,7},{3,1},{5,3},{7,5},{8,14},{10,8},{12,... | collective-permute-start | bytes 159752 | tf_op jit(solution)/shard_map/ppermute | solution.py:307
  33.5 5.1 %collective-permute-start.4 = (f32[104,128]{1,0:T(8,128)S(1)}, f32[104,128]{1,0:T(8,128)S(1)}, u32[]{:S(2)}, u32[]{:S(2)}) collective-permute-start(f32[104,128]{1,0:T(8,128)S(1)} %get-tuple-element.27), channel_id=1, source_target_pairs={{0,4},{2,6},{4,0},{6,2},{1,5},{3,7},{5,1},{7,3},{8,12},{10,14},{12... | collective-permute-start | bytes 159752 | tf_op jit(solution)/shard_map/ppermute | solution.py:307
  33.5 5.9 %collective-permute-start.3 = (f32[104,128]{1,0:T(8,128)S(1)}, f32[104,128]{1,0:T(8,128)S(1)}, u32[]{:S(2)}, u32[]{:S(2)}) collective-permute-start(f32[104,128]{1,0:T(8,128)S(1)} %get-tuple-element.25), channel_id=1, source_target_pairs={{0,2},{2,4},{4,6},{6,0},{1,3},{3,5},{5,7},{7,1},{8,10},{10,12},{12... | collective-permute-start | bytes 159752 | tf_op jit(solution)/shard_map/ppermute | solution.py:307
  35.0 22.1 %copy-start = (f32[512,128]{1,0:T(8,128)S(1)}, f32[512,128]{1,0:T(8,128)}, u32[]{:S(2)}) copy-start(f32[512,128]{1,0:T(8,128)} %start_ref.1) | copy-start | bytes 786436
  39.5 4.2 %collective-permute-start.8 = (f32[104,128]{1,0:T(8,128)S(1)}, f32[104,128]{1,0:T(8,128)S(1)}, u32[]{:S(2)}, u32[]{:S(2)}) collective-permute-start(f32[104,128]{1,0:T(8,128)S(1)} %fusion.6), channel_id=1, source_target_pairs={{0,6},{2,0},{4,2},{6,4},{1,7},{3,1},{5,3},{7,5},{8,14},{10,8},{12,... | collective-permute-start | bytes 159752 | tf_op jit(solution)/shard_map/ppermute | solution.py:314
  41.2 5.4 %collective-permute-start.7 = (f32[104,128]{1,0:T(8,128)S(1)}, f32[104,128]{1,0:T(8,128)S(1)}, u32[]{:S(2)}, u32[]{:S(2)}) collective-permute-start(f32[104,128]{1,0:T(8,128)S(1)} %fusion.6), channel_id=1, source_target_pairs={{0,4},{2,6},{4,0},{6,2},{1,5},{3,7},{5,1},{7,3},{8,12},{10,14},{12... | collective-permute-start | bytes 159752 | tf_op jit(solution)/shard_map/ppermute | solution.py:314
  41.2 6.0 %collective-permute-start.6 = (f32[104,128]{1,0:T(8,128)S(1)}, f32[104,128]{1,0:T(8,128)S(1)}, u32[]{:S(2)}, u32[]{:S(2)}) collective-permute-start(f32[104,128]{1,0:T(8,128)S(1)} %fusion.6), channel_id=1, source_target_pairs={{0,2},{2,4},{4,6},{6,0},{1,3},{3,5},{5,7},{7,1},{8,10},{10,12},{12... | collective-permute-start | bytes 159752 | tf_op jit(solution)/shard_map/ppermute | solution.py:314
  48.0 29.9 %copy-start.1 = (bf16[32,64,512]{2,1,0:T(8,128)(2,1)S(1)}, bf16[32,64,512]{2,1,0:T(8,128)(2,1)}, u32[]{:S(2)}) copy-start(bf16[32,64,512]{2,1,0:T(8,128)(2,1)} %param.6) | copy-start | bytes 6291460
  48.0 6.2 %collective-permute-start.9 = (f32[416,128]{1,0:T(8,128)}, f32[416,128]{1,0:T(8,128)}, u32[]{:S(2)}, u32[]{:S(2)}) collective-permute-start(f32[416,128]{1,0:T(8,128)} %pad_maximum_fusion.1), channel_id=1, source_target_pairs={{0,8},{8,0},{1,9},{9,1},{2,10},{10,2},{3,11},{11,3},{4,12},{12,4},... | collective-permute-start | bytes 638984 | tf_op jit(solution)/shard_map/ppermute | solution.py:314
  55.2 1.8 %collective-permute-start.10 = (f32[832,128]{1,0:T(8,128)S(1)}, f32[832,128]{1,0:T(8,128)S(1)}, u32[]{:S(2)}, u32[]{:S(2)}) collective-permute-start(f32[832,128]{1,0:T(8,128)S(1)} %broadcast_select_fusion.mine_ref), channel_id=1, source_target_pairs={{0,1},{1,0},{2,3},{3,2},{4,5},{5,4},{6,7},{7,6},{8,9},{9,8},{10,11... | collective-permute-start | bytes 1277960 | tf_op jit(solution)/shard_map/ppermute | solution.py:322

commit v6 on v5

--- a/solution.py
+++ b/solution.py
@@ -280,7 +280,7 @@
     return pl.pallas_call(
         edge_kernel,
         out_shape=(gram, gram),
-        in_specs=[SMEM, HBM, HBM, VMEM, VMEM, VMEM, VMEM],
+        in_specs=[SMEM, pl.BlockSpec(memory_space=pl.ANY), HBM, VMEM, VMEM, VMEM, VMEM],
         out_specs=(VMEM, VMEM),
         scratch_shapes=[
             pltpu.VMEM((720, bands), BF16),
@@ -292,7 +292,7 @@
         ],
         compiler_params=PARAMS,
         name="edge",
-    )(state, *(pltpu.with_memory_space_constraint(a, pltpu.HBM) for a in (low, x)), pick, taps, noise, signal)
+    )(state, low, pltpu.with_memory_space_constraint(x, pltpu.HBM), pick, taps, noise, signal)
 
 
 def scatter_sum(parts, axis):
@@ -313,7 +313,7 @@
     me = lax.axis_index(axis)
     got = [x] + [lax.ppermute(x, axis, [(i, (i + d) % n) for i in range(n)]) for d in range(1, n)]
     if n == 2:
-        return jnp.where(me == 0, jnp.concatenate(got), jnp.concatenate(got[::-1]))
+        return jnp.concatenate([jnp.where(me == 0, got[0], got[1]), jnp.where(me == 0, got[1], got[0])])
     stacked = jnp.stack(got)
     return jnp.concatenate([lax.dynamic_index_in_dim(stacked, (me - j) % n, 0, keepdims=False) for j in range(n)])
 

time: 79.8 us -> 77.1 us (0.966)
  local copies, waits for them, and re-layouts: 1.79 us -> 0.06 us
    unnamed x14 -> x4, local copies, waits for them, and re-layouts: 1.76 us -> 0.01 us
where the time goes in v6:
time: 77.1 us; the launch traced here: 76.9 us
  Pallas kernels  34.2 us (44%)
  waiting for transfers between devices  22.7 us (29%)
  starting transfers between devices  16 us (21%)
  matrix products  1.72 us (2%)
  other arithmetic  1.4 us (2%)
  between operations  0.8 us (1%)
    pallas_call x1, Pallas kernels, finish(): pl.pallas_call(finish_kernel, out_shape=jax.ShapeDtypeStruct((512, LANES)...  20.8 us
    ppermute x4, waiting for transfers between devices, scatter_sum(): lax.ppermute(sum(block((me + d) % n)), axis, [(i, (i + d) % n) for i in r...  10.5 us
    pallas_call x1, Pallas kernels, inner(): pl.pallas_call(inner_kernel, out_shape=(gram, gram, jax.ShapeDtypeStruct(...  10.1 us
    ppermute x4, waiting for transfers between devices, gather_rows(): lax.ppermute(x, axis, [(i, (i + d) % n) for i in range(n)])  9.01 us
    ppermute x4, starting transfers between devices, scatter_sum(): lax.ppermute(sum(block((me + d) % n)), axis, [(i, (i + d) % n) for i in r...  6.23 us
    ppermute x4, starting transfers between devices, gather_rows(): lax.ppermute(x, axis, [(i, (i + d) % n) for i in range(n)])  4.58 us
    pallas_call x1, Pallas kernels, edge(): pl.pallas_call(edge_kernel, out_shape=(gram, gram), in_specs=[SMEM, pl.Bl...  3.29 us
    ppermute x2, waiting for transfers between devices, exchange(): return lax.ppermute(x, 'sub', [(0, 1), (1, 0)])  3.14 us
  transfers between devices with their start and end apart: 11, of which 10 were waited for; matrix products, arithmetic and copies ran while one was open for 0% of the time, Pallas kernels for 13%

profile of v6, /device:TPU:0, one launch (start us, length us, event | category | flops | bytes accessed | tf_op | source)
XLA Modules:
  0.0 76.9 jit_solution(6113022043356725029)
XLA Ops:
  0.7 0.1 slice_compare_fusion
  0.7 1.0 %slice_select_fusion = bf16[4,64,512]{2,1,0:T(8,128)(2,1)S(1)} fusion(bf16[32,64,512]{2,1,0:T(8,128)(2,1)} %param.6, pred[4]{0:T(512)(128)(4,1)S(1)} %slice_compare_fusion), kind=kLoop, calls=%fused_computation.5 | loop fusion | flops 131072 | bytes 524292 | tf_op jit(solution)/shard_map/jit(_where)/select_n | solution.py:559
  1.8 2.4 %collective-permute-start = (bf16[272,512]{1,0:T(8,128)(2,1)S(1)}, bf16[272,512]{1,0:T(8,128)(2,1)S(1)}, u32[]{:S(2)}, u32[]{:S(2)}) collective-permute-start(bf16[272,512]{1,0:T(8,128)(2,1)S(1)} %concatenate.9), channel_id=1, source_target_pairs={{0,1},{1,2},{2,3},{3,4},{4,5},{5,6},{6,7},{7,8},{8,9},{9,10},{10,1... | collective-permute-start | bytes 835592 | tf_op jit(solution)/shard_map/ppermute | solution.py:561
  4.2 10.1 %inner.1 = (f32[832,128]{1,0:T(8,128)S(1)}, f32[832,128]{1,0:T(8,128)S(1)}, bf16[512,512]{1,0:T(8,128)(2,1)S(1)}, f32[40,512]{1,0:T(8,128)S(1)}) custom-call(s32[1]{0:T(128)} %copy.7.count_ref, s32[1,512]{1,0:T(1,128)} %bitcast.59, f32[8,512]{1,0:T(8,128)} %noise_hbm.1, f32[25,512]{1,0:T(8,128)} %smooth_hbm.1, bf16[2048,512]{1,0:T(8,128)(2,1)} %bitcast.45), custom_call_target="tpu_custom_call" | custom-call | flops 6442450944 | bytes 8388608 | tf_op jit(solution)/shard_map/inner/pallas_call | solution.py:254
  14.4 0.1 pad_add_fusion.state_ref
  14.4 0.0 collective-permute-done.low_hbm
  14.4 3.3 %edge.1 = (f32[832,128]{1,0:T(8,128)S(1)}, f32[832,128]{1,0:T(8,128)S(1)}) custom-call(s32[4]{0:T(128)S(1)} %pad_add_fusion.state_ref, bf16[272,512]{1,0:T(8,128)(2,1)S(1)} %collective-permute-done.low_hbm, bf16[2048,512]{1,0:T(8,128)(2,1)} %bitcast.46, bf16[512,512]{1,0:T(8,128)(2,1)S(1)} %get-tuple-element.11.pick_ref, ...), custom_call_target="tpu_custom_call" | custom-call | tf_op jit(solution)/shard_map/edge/pallas_call | solution.py:280
  17.7 2.7 %collective-permute-start.1 = (f32[832,128]{1,0:T(8,128)S(1)}, f32[832,128]{1,0:T(8,128)S(1)}, u32[]{:S(2)}, u32[]{:S(2)}) collective-permute-start(f32[832,128]{1,0:T(8,128)S(1)} %get-tuple-element.16), channel_id=1, source_target_pairs={{0,1},{1,0},{2,3},{3,2},{4,5},{5,4},{6,7},{7,6},{8,9},{9,8},{10,11... | collective-permute-start | bytes 1277960 | tf_op jit(solution)/shard_map/ppermute | solution.py:322
  20.5 1.4 %collective-permute-done.1 = f32[832,128]{1,0:T(8,128)S(1)} collective-permute-done((f32[832,128]{1,0:T(8,128)S(1)}, f32[832,128]{1,0:T(8,128)S(1)}, u32[]{:S(2)}, u32[]{:S(2)}) %collective-permute-start.1) | collective-permute-done | bytes 426016 | tf_op jit(solution)/shard_map/ppermute | solution.py:322
  21.9 0.1 constant_dynamic-slice_fusion.1
  21.9 1.6 %collective-permute-start.2 = (f32[416,128]{1,0:T(8,128)S(1)}, f32[416,128]{1,0:T(8,128)S(1)}, u32[]{:S(2)}, u32[]{:S(2)}) collective-permute-start(f32[416,128]{1,0:T(8,128)S(1)} %get-tuple-element.23), channel_id=1, source_target_pairs={{0,8},{8,0},{1,9},{9,1},{2,10},{10,2},{3,11},{11,3},{4,12},{12,4},... | collective-permute-start | bytes 638984 | tf_op jit(solution)/shard_map/ppermute | solution.py:307
  23.5 0.0 copy-start
  23.5 6.0 %collective-permute-done.2 = f32[416,128]{1,0:T(8,128)S(1)} collective-permute-done((f32[416,128]{1,0:T(8,128)S(1)}, f32[416,128]{1,0:T(8,128)S(1)}, u32[]{:S(2)}, u32[]{:S(2)}) %collective-permute-start.2) | collective-permute-done | bytes 213024 | tf_op jit(solution)/shard_map/ppermute | solution.py:307
  29.6 3.2 %collective-permute-start.5 = (f32[104,128]{1,0:T(8,128)S(1)}, f32[104,128]{1,0:T(8,128)S(1)}, u32[]{:S(2)}, u32[]{:S(2)}) collective-permute-start(f32[104,128]{1,0:T(8,128)S(1)} %get-tuple-element.18), channel_id=1, source_target_pairs={{0,6},{2,0},{4,2},{6,4},{1,7},{3,1},{5,3},{7,5},{8,14},{10,8},{12,... | collective-permute-start | bytes 159752 | tf_op jit(solution)/shard_map/ppermute | solution.py:307
  32.8 0.0 collective-permute-start.4
  32.8 1.4 %collective-permute-start.3 = (f32[104,128]{1,0:T(8,128)S(1)}, f32[104,128]{1,0:T(8,128)S(1)}, u32[]{:S(2)}, u32[]{:S(2)}) collective-permute-start(f32[104,128]{1,0:T(8,128)S(1)} %get-tuple-element.17), channel_id=1, source_target_pairs={{0,2},{2,4},{4,6},{6,0},{1,3},{3,5},{5,7},{7,1},{8,10},{10,12},{12... | collective-permute-start | bytes 159752 | tf_op jit(solution)/shard_map/ppermute | solution.py:307
  34.2 0.6 collective-permute-done.5
  34.8 3.1 %collective-permute-done.4 = f32[104,128]{1,0:T(8,128)S(1)} collective-permute-done((f32[104,128]{1,0:T(8,128)S(1)}, f32[104,128]{1,0:T(8,128)S(1)}, u32[]{:S(2)}, u32[]{:S(2)}) %collective-permute-start.4) | collective-permute-done | bytes 53280 | tf_op jit(solution)/shard_map/ppermute | solution.py:307
  37.8 0.9 %collective-permute-done.3 = f32[104,128]{1,0:T(8,128)S(1)} collective-permute-done((f32[104,128]{1,0:T(8,128)S(1)}, f32[104,128]{1,0:T(8,128)S(1)}, u32[]{:S(2)}, u32[]{:S(2)}) %collective-permute-start.3) | collective-permute-done | bytes 53280 | tf_op jit(solution)/shard_map/ppermute | solution.py:307
  38.7 1.7 %collective-permute-start.8 = (f32[104,128]{1,0:T(8,128)S(1)}, f32[104,128]{1,0:T(8,128)S(1)}, u32[]{:S(2)}, u32[]{:S(2)}) collective-permute-start(f32[104,128]{1,0:T(8,128)S(1)} %fusion.6), channel_id=1, source_target_pairs={{0,6},{2,0},{4,2},{6,4},{1,7},{3,1},{5,3},{7,5},{8,14},{10,8},{12,... | collective-permute-start | bytes 159752 | tf_op jit(solution)/shard_map/ppermute | solution.py:314
  40.5 0.0 collective-permute-start.7
  40.5 1.8 %collective-permute-start.6 = (f32[104,128]{1,0:T(8,128)S(1)}, f32[104,128]{1,0:T(8,128)S(1)}, u32[]{:S(2)}, u32[]{:S(2)}) collective-permute-start(f32[104,128]{1,0:T(8,128)S(1)} %fusion.6), channel_id=1, source_target_pairs={{0,2},{2,4},{4,6},{6,0},{1,3},{3,5},{5,7},{7,1},{8,10},{10,12},{12... | collective-permute-start | bytes 159752 | tf_op jit(solution)/shard_map/ppermute | solution.py:314
  42.2 0.7 collective-permute-done.8
  42.9 2.9 %collective-permute-done.7 = f32[104,128]{1,0:T(8,128)S(1)} collective-permute-done((f32[104,128]{1,0:T(8,128)S(1)}, f32[104,128]{1,0:T(8,128)S(1)}, u32[]{:S(2)}, u32[]{:S(2)}) %collective-permute-start.7) | collective-permute-done | bytes 53280 | tf_op jit(solution)/shard_map/ppermute | solution.py:314
  45.9 0.6 collective-permute-done.6
  46.5 0.0 copy-start.1
  46.5 1.1 %collective-permute-start.9 = (f32[416,128]{1,0:T(8,128)S(1)}, f32[416,128]{1,0:T(8,128)S(1)}, u32[]{:S(2)}, u32[]{:S(2)}) collective-permute-start(f32[416,128]{1,0:T(8,128)S(1)} %pad_maximum_fusion.2), channel_id=1, source_target_pairs={{0,8},{8,0},{1,9},{9,1},{2,10},{10,2},{3,11},{11,3},{4,12},{12,4},... | collective-permute-start | bytes 638984 | tf_op jit(solution)/shard_map/ppermute | solution.py:314
  47.7 4.8 %collective-permute-done.9 = f32[416,128]{1,0:T(8,128)S(1)} collective-permute-done((f32[416,128]{1,0:T(8,128)S(1)}, f32[416,128]{1,0:T(8,128)S(1)}, u32[]{:S(2)}, u32[]{:S(2)}) %collective-permute-start.9) | collective-permute-done | bytes 213024 | tf_op jit(solution)/shard_map/ppermute | solution.py:314
  52.5 0.1 collective-permute-start.10
  52.6 1.7 %collective-permute-done.10.other_ref = f32[832,128]{1,0:T(8,128)S(1)} collective-permute-done((f32[832,128]{1,0:T(8,128)S(1)}, f32[832,128]{1,0:T(8,128)S(1)}, u32[]{:S(2)}, u32[]{:S(2)}) %collective-permute-start.10) | collective-permute-done | bytes 426016 | tf_op jit(solution)/shard_map/ppermute | solution.py:322
  54.3 0.0 copy-done
  54.4 20.8 %shard_map.64 = bf16[512,128]{1,0:T(8,128)(2,1)S(1)} custom-call(s32[1]{0:T(128)} %bitcast.1.side_ref, f32[832,128]{1,0:T(8,128)S(1)} %pad_maximum_fusion.mine_ref, f32[832,128]{1,0:T(8,128)S(1)} %collective-permute-done.10.other_ref, bf16[512,512]{1,0:T(8,128)(2,1)S(1)} %get-tuple-element.11.pick_ref, f32[512,128]{1,0:T(8,128)S(1)} %copy-done), custom_call_target="tpu_custom_call" | custom-call | tf_op jit(solution)/shard_map/pallas_call | solution.py:535
  75.1 0.0 copy-done.1
  75.2 1.7 %fusion = f32[32,64,128]{2,1,0:T(8,128)} fusion(bf16[32,64,512]{2,1,0:T(8,128)(2,1)S(1)} %copy-done.1, pred[32]{0:T(512)(128)(4,1)S(1)} %iota_compare_fusion, bf16[512,128]{1,0:T(8,128)(2,1)S(1)} %shard_map.64), kind=kOutput, calls=%fused_computation | convolution fusion | flops 269484032 | bytes 3276832 | tf_op jit(solution)/shard_map/dot_general | solution.py:572
  (10 shorter events, 0.2 us)
Async XLA Ops:
  1.8 12.6 %collective-permute-start = (bf16[272,512]{1,0:T(8,128)(2,1)S(1)}, bf16[272,512]{1,0:T(8,128)(2,1)S(1)}, u32[]{:S(2)}, u32[]{:S(2)}) collective-permute-start(bf16[272,512]{1,0:T(8,128)(2,1)S(1)} %concatenate.9), channel_id=1, source_target_pairs={{0,1},{1,2},{2,3},{3,4},{4,5},{5,6},{6,7},{7,8},{8,9},{9,10},{10,1... | collective-permute-start | bytes 835592 | tf_op jit(solution)/shard_map/ppermute | solution.py:561
  17.7 4.1 %collective-permute-start.1 = (f32[832,128]{1,0:T(8,128)S(1)}, f32[832,128]{1,0:T(8,128)S(1)}, u32[]{:S(2)}, u32[]{:S(2)}) collective-permute-start(f32[832,128]{1,0:T(8,128)S(1)} %get-tuple-element.16), channel_id=1, source_target_pairs={{0,1},{1,0},{2,3},{3,2},{4,5},{5,4},{6,7},{7,6},{8,9},{9,8},{10,11... | collective-permute-start | bytes 1277960 | tf_op jit(solution)/shard_map/ppermute | solution.py:322
  21.9 7.6 %collective-permute-start.2 = (f32[416,128]{1,0:T(8,128)S(1)}, f32[416,128]{1,0:T(8,128)S(1)}, u32[]{:S(2)}, u32[]{:S(2)}) collective-permute-start(f32[416,128]{1,0:T(8,128)S(1)} %get-tuple-element.23), channel_id=1, source_target_pairs={{0,8},{8,0},{1,9},{9,1},{2,10},{10,2},{3,11},{11,3},{4,12},{12,4},... | collective-permute-start | bytes 638984 | tf_op jit(solution)/shard_map/ppermute | solution.py:307
  23.5 30.8 %copy-start = (f32[512,128]{1,0:T(8,128)S(1)}, f32[512,128]{1,0:T(8,128)}, u32[]{:S(2)}) copy-start(f32[512,128]{1,0:T(8,128)} %start_ref.1) | copy-start | bytes 786436
  29.6 5.2 %collective-permute-start.5 = (f32[104,128]{1,0:T(8,128)S(1)}, f32[104,128]{1,0:T(8,128)S(1)}, u32[]{:S(2)}, u32[]{:S(2)}) collective-permute-start(f32[104,128]{1,0:T(8,128)S(1)} %get-tuple-element.18), channel_id=1, source_target_pairs={{0,6},{2,0},{4,2},{6,4},{1,7},{3,1},{5,3},{7,5},{8,14},{10,8},{12,... | collective-permute-start | bytes 159752 | tf_op jit(solution)/shard_map/ppermute | solution.py:307
  32.8 5.1 %collective-permute-start.4 = (f32[104,128]{1,0:T(8,128)S(1)}, f32[104,128]{1,0:T(8,128)S(1)}, u32[]{:S(2)}, u32[]{:S(2)}) collective-permute-start(f32[104,128]{1,0:T(8,128)S(1)} %get-tuple-element.19), channel_id=1, source_target_pairs={{0,4},{2,6},{4,0},{6,2},{1,5},{3,7},{5,1},{7,3},{8,12},{10,14},{12... | collective-permute-start | bytes 159752 | tf_op jit(solution)/shard_map/ppermute | solution.py:307
  32.8 5.9 %collective-permute-start.3 = (f32[104,128]{1,0:T(8,128)S(1)}, f32[104,128]{1,0:T(8,128)S(1)}, u32[]{:S(2)}, u32[]{:S(2)}) collective-permute-start(f32[104,128]{1,0:T(8,128)S(1)} %get-tuple-element.17), channel_id=1, source_target_pairs={{0,2},{2,4},{4,6},{6,0},{1,3},{3,5},{5,7},{7,1},{8,10},{10,12},{12... | collective-permute-start | bytes 159752 | tf_op jit(solution)/shard_map/ppermute | solution.py:307
  38.7 4.2 %collective-permute-start.8 = (f32[104,128]{1,0:T(8,128)S(1)}, f32[104,128]{1,0:T(8,128)S(1)}, u32[]{:S(2)}, u32[]{:S(2)}) collective-permute-start(f32[104,128]{1,0:T(8,128)S(1)} %fusion.6), channel_id=1, source_target_pairs={{0,6},{2,0},{4,2},{6,4},{1,7},{3,1},{5,3},{7,5},{8,14},{10,8},{12,... | collective-permute-start | bytes 159752 | tf_op jit(solution)/shard_map/ppermute | solution.py:314
  40.5 5.4 %collective-permute-start.7 = (f32[104,128]{1,0:T(8,128)S(1)}, f32[104,128]{1,0:T(8,128)S(1)}, u32[]{:S(2)}, u32[]{:S(2)}) collective-permute-start(f32[104,128]{1,0:T(8,128)S(1)} %fusion.6), channel_id=1, source_target_pairs={{0,4},{2,6},{4,0},{6,2},{1,5},{3,7},{5,1},{7,3},{8,12},{10,14},{12... | collective-permute-start | bytes 159752 | tf_op jit(solution)/shard_map/ppermute | solution.py:314
  40.5 6.0 %collective-permute-start.6 = (f32[104,128]{1,0:T(8,128)S(1)}, f32[104,128]{1,0:T(8,128)S(1)}, u32[]{:S(2)}, u32[]{:S(2)}) collective-permute-start(f32[104,128]{1,0:T(8,128)S(1)} %fusion.6), channel_id=1, source_target_pairs={{0,2},{2,4},{4,6},{6,0},{1,3},{3,5},{5,7},{7,1},{8,10},{10,12},{12... | collective-permute-start | bytes 159752 | tf_op jit(solution)/shard_map/ppermute | solution.py:314
  46.5 28.7 %copy-start.1 = (bf16[32,64,512]{2,1,0:T(8,128)(2,1)S(1)}, bf16[32,64,512]{2,1,0:T(8,128)(2,1)}, u32[]{:S(2)}) copy-start(bf16[32,64,512]{2,1,0:T(8,128)(2,1)} %param.6) | copy-start | bytes 6291460
  46.5 5.9 %collective-permute-start.9 = (f32[416,128]{1,0:T(8,128)S(1)}, f32[416,128]{1,0:T(8,128)S(1)}, u32[]{:S(2)}, u32[]{:S(2)}) collective-permute-start(f32[416,128]{1,0:T(8,128)S(1)} %pad_maximum_fusion.2), channel_id=1, source_target_pairs={{0,8},{8,0},{1,9},{9,1},{2,10},{10,2},{3,11},{11,3},{4,12},{12,4},... | collective-permute-start | bytes 638984 | tf_op jit(solution)/shard_map/ppermute | solution.py:314
  52.5 1.8 %collective-permute-start.10 = (f32[832,128]{1,0:T(8,128)S(1)}, f32[832,128]{1,0:T(8,128)S(1)}, u32[]{:S(2)}, u32[]{:S(2)}) collective-permute-start(f32[832,128]{1,0:T(8,128)S(1)} %pad_maximum_fusion.mine_ref), channel_id=1, source_target_pairs={{0,1},{1,0},{2,3},{3,2},{4,5},{5,4},{6,7},{7,6},{8,9},{9,8},{10,11... | collective-permute-start | bytes 1277960 | tf_op jit(solution)/shard_map/ppermute | solution.py:322

commit v7 on v6

--- a/solution.py
+++ b/solution.py
@@ -108,7 +108,7 @@
 
 
 def inner_kernel(
-    count_ref, mask_hbm, noise_hbm, smooth_hbm, x_hbm, noise_out, signal_out, pick_ref, taps,
+    count_ref, mask_hbm, noise_hbm, smooth_hbm, x_hbm, noise_out, signal_out, pick_ref, taps, ends_ref,
     x, xs, nf, sg, sums, mask_ref, noise_ref, smooth_ref, sems, small_sems,
 ):
     height = x.shape[0] // 64
@@ -145,6 +145,9 @@
     for copy in copies:
         copy.wait()
 
+    ends_ref[:192, :] = x[:192, :]
+    ends_ref[192:, :] = x[x.shape[0] - 256 :, :]
+
     def picked(k):
         return jnp.dot(x[pl.ds(pl.multiple_of(k * 256, 256), 256), :], pick, preferred_element_type=F32)
 
@@ -195,32 +198,24 @@
 
 
 def edge_kernel(
-    state_ref, low_hbm, x_hbm, pick_ref, taps, noise_ref, signal_ref, keep_ref, send_ref, rows, both, xs, nf, sg, sems
+    state_ref, low_hbm, ends_ref, pick_ref, taps, noise_ref, signal_ref, keep_ref, send_ref, rows, both, xs, nf, sg, sems
 ):
-    count, side, first, last = [state_ref[k] for k in range(4)]
-    size = x_hbm.shape[0]
-    height = size // 64
-    pieces = ((low_hbm, 0, 272), (x_hbm.at[pl.ds(0, 192)], 272, 192), (x_hbm.at[pl.ds(size - 256, 256)], 464, 256))
-    copies = [
-        pltpu.make_async_copy(source, rows.at[pl.ds(start, length)], sems.at[k])
-        for k, (source, start, length) in enumerate(pieces)
-    ]
-    for copy in copies:
-        copy.start()
+    count, side, first, last, height = [state_ref[k] for k in range(5)]
+    copy = pltpu.make_async_copy(low_hbm, rows, sems.at[0])
+    copy.start()
     pick = pick_ref[...]
     clear_gaps(xs, 12)
     pitch = xs.shape[0] // 4
     for tile in range(4):
         start = tile * pitch + 8 + 11 * PITCH
         xs[start : start + 64, :] = jnp.zeros((64, LANES), F32)
-    for copy in copies:
-        copy.wait()
-    values = jnp.dot(rows[...], pick, preferred_element_type=F32)
-    place(xs, values[:256], 4, 0, 0, None)
-    place(xs, values[272:464], 3, 4, 0, count)
-    place(xs, values[464:], 4, 7, height - 4, count)
+    values = jnp.dot(ends_ref[...], pick, preferred_element_type=F32)
+    place(xs, values[:192], 3, 4, 0, count)
+    place(xs, values[192:], 4, 7, height - 4, count)
+    copy.wait()
+    place(xs, jnp.dot(rows[:256, :], pick, preferred_element_type=F32), 4, 0, 0, None)
     before = jnp.broadcast_to(rows[256:272, :LANES].astype(F32)[:1], (32, LANES))
-    noise_rows = ((3, before > float(height - 1)), (4, count > 0), (10, (last == 1) & (count > height - 1)))
+    noise_rows = ((3, before > (height - 1).astype(F32)), (4, count > 0), (10, (last == 1) & (count > height - 1)))
     signal_rows = ((0, first == 0), (2, None), (7, last == 1))
     for tile in range(4):
         lanes = slice(tile * LANES, (tile + 1) * LANES)
@@ -253,9 +248,12 @@
     gram = jax.ShapeDtypeStruct((PACKED, LANES), F32)
     return pl.pallas_call(
         inner_kernel,
-        out_shape=(gram, gram, jax.ShapeDtypeStruct((bands, bands), BF16), jax.ShapeDtypeStruct((40, bands), F32)),
+        out_shape=(
+            gram, gram, jax.ShapeDtypeStruct((bands, bands), BF16), jax.ShapeDtypeStruct((40, bands), F32),
+            jax.ShapeDtypeStruct((448, bands), BF16),
+        ),
         in_specs=[SMEM] + [HBM] * 4,
-        out_specs=(VMEM,) * 4,
+        out_specs=(VMEM,) * 5,
         scratch_shapes=[
             pltpu.VMEM(x.shape, BF16),
             pltpu.VMEM((4 * (16 + height * PITCH), LANES), F32),
@@ -274,25 +272,25 @@
     )(count, *(pltpu.with_memory_space_constraint(a, pltpu.HBM) for a in (mask, noise_kernel, smooth_kernel, x)))
 
 
-def edge(state, low, x, pick, taps, noise, signal):
-    bands = x.shape[1]
+def edge(state, low, ends, pick, taps, noise, signal):
+    bands = ends.shape[1]
     gram = jax.ShapeDtypeStruct((PACKED, LANES), F32)
     return pl.pallas_call(
         edge_kernel,
         out_shape=(gram, gram),
-        in_specs=[SMEM, pl.BlockSpec(memory_space=pl.ANY), HBM, VMEM, VMEM, VMEM, VMEM],
+        in_specs=[SMEM, pl.BlockSpec(memory_space=pl.ANY), VMEM, VMEM, VMEM, VMEM, VMEM],
         out_specs=(VMEM, VMEM),
         scratch_shapes=[
-            pltpu.VMEM((720, bands), BF16),
+            pltpu.VMEM((272, bands), BF16),
             pltpu.VMEM((2 * PACKED, LANES), F32),
             pltpu.VMEM((4 * (16 + 12 * PITCH), LANES), F32),
             pltpu.VMEM((192, bands), BF16),
             pltpu.VMEM((96, bands), BF16),
-            pltpu.SemaphoreType.DMA((3,)),
+            pltpu.SemaphoreType.DMA((1,)),
         ],
         compiler_params=PARAMS,
         name="edge",
-    )(state, low, pltpu.with_memory_space_constraint(x, pltpu.HBM), pick, taps, noise, signal)
+    )(state, low, ends, pick, taps, noise, signal)
 
 
 def scatter_sum(parts, axis):
@@ -560,11 +558,11 @@
     tail = jnp.concatenate([tail, jnp.full((16, bands), count, radiance.dtype)], axis=0)
     low = lax.ppermute(tail, AXES, up)
 
-    noise, signal, pick, taps = inner(row_counts, band_mask[None], noise_kernel, smooth_kernel, flat)
+    noise, signal, pick, taps, ends = inner(row_counts, band_mask[None], noise_kernel, smooth_kernel, flat)
     side = lax.axis_index("sub")
     place_in_chain = lax.axis_index(AXES)
-    state = jnp.stack([count, side, place_in_chain == 0, place_in_chain == chain - 1]).astype(jnp.int32)
-    keep, send = edge(state, low, flat, pick, taps, noise, signal)
+    state = jnp.stack([count, side, place_in_chain == 0, place_in_chain == chain - 1, height]).astype(jnp.int32)
+    keep, send = edge(state, low, ends, pick, taps, noise, signal)
     mine, other = total_sum(keep, send)
     weights = finish(state[1:2], mine, other, pick, start_basis)
     keep = jnp.repeat(row < count, across)

time: 77.1 us -> 76 us (0.986)
  Pallas kernels: 34.2 us -> 33.2 us
    pallas_call x1, Pallas kernels: 3.29 us -> 2.22 us  [edge(): pl.pallas_call(edge_kernel, out_shape=(gram, gram), in_specs=[SMEM, pl.Bl...]
where the time goes in v7:
time: 76 us; the launch traced here: 75.8 us
  Pallas kernels  33.2 us (44%)
  waiting for transfers between devices  22.7 us (30%)
  starting transfers between devices  16 us (21%)
  matrix products  1.72 us (2%)
  other arithmetic  1.32 us (2%)
  between operations  0.81 us (1%)
    pallas_call x1, Pallas kernels, finish(): pl.pallas_call(finish_kernel, out_shape=jax.ShapeDtypeStruct((512, LANES)...  20.8 us
    ppermute x4, waiting for transfers between devices, scatter_sum(): lax.ppermute(sum(block((me + d) % n)), axis, [(i, (i + d) % n) for i in r...  10.5 us
    pallas_call x1, Pallas kernels, inner(): pl.pallas_call(inner_kernel, out_shape=(gram, gram, jax.ShapeDtypeStruct(...  10.2 us
    ppermute x4, waiting for transfers between devices, gather_rows(): lax.ppermute(x, axis, [(i, (i + d) % n) for i in range(n)])  9.02 us
    ppermute x4, starting transfers between devices, scatter_sum(): lax.ppermute(sum(block((me + d) % n)), axis, [(i, (i + d) % n) for i in r...  6.24 us
    ppermute x4, starting transfers between devices, gather_rows(): lax.ppermute(x, axis, [(i, (i + d) % n) for i in range(n)])  4.58 us
    ppermute x2, waiting for transfers between devices, exchange(): return lax.ppermute(x, 'sub', [(0, 1), (1, 0)])  3.14 us
    ppermute x2, starting transfers between devices, exchange(): return lax.ppermute(x, 'sub', [(0, 1), (1, 0)])  2.81 us
  transfers between devices with their start and end apart: 11, of which 10 were waited for; matrix products, arithmetic and copies ran while one was open for 0% of the time, Pallas kernels for 13%

profile of v7, /device:TPU:0, one launch (start us, length us, event | category | flops | bytes accessed | tf_op | source)
XLA Modules:
  0.0 75.8 jit_solution(5396312489775593774)
XLA Ops:
  0.7 0.1 slice_compare_fusion
  0.7 1.0 %slice_select_fusion = bf16[4,64,512]{2,1,0:T(8,128)(2,1)S(1)} fusion(bf16[32,64,512]{2,1,0:T(8,128)(2,1)} %param.6, pred[4]{0:T(512)(128)(4,1)S(1)} %slice_compare_fusion), kind=kLoop, calls=%fused_computation.5 | loop fusion | flops 131072 | bytes 524292 | tf_op jit(solution)/shard_map/jit(_where)/select_n | solution.py:557
  1.8 2.4 %collective-permute-start = (bf16[272,512]{1,0:T(8,128)(2,1)S(1)}, bf16[272,512]{1,0:T(8,128)(2,1)S(1)}, u32[]{:S(2)}, u32[]{:S(2)}) collective-permute-start(bf16[272,512]{1,0:T(8,128)(2,1)S(1)} %concatenate.9), channel_id=1, source_target_pairs={{0,1},{1,2},{2,3},{3,4},{4,5},{5,6},{6,7},{7,8},{8,9},{9,10},{10,1... | collective-permute-start | bytes 835592 | tf_op jit(solution)/shard_map/ppermute | solution.py:559
  4.2 10.2 %inner.1 = (f32[832,128]{1,0:T(8,128)S(1)}, f32[832,128]{1,0:T(8,128)S(1)}, bf16[512,512]{1,0:T(8,128)(2,1)S(1)}, f32[40,512]{1,0:T(8,128)S(1)}, bf16[448,512]{1,0:T(8,128)(2,1)S(1)}) custom-call(s32[1]{0:T(128)} %copy.7.count_ref, s32[1,512]{1,0:T(1,128)} %bitcast.58, f32[8,512]{1,0:T(8,128)} %noise_hbm.1, f32[25,512]{1,0:T(8,128)} %smooth_hbm.1, ...), custom_call_target="tpu_custom_call" | custom-call | flops 6442450944 | bytes 8388608 | tf_op jit(solution)/shard_map/inner/pallas_call | solution.py:249
  14.4 0.1 stack.38.state_ref
  14.5 0.0 collective-permute-done.low_hbm
  14.5 2.2 %edge.1 = (f32[832,128]{1,0:T(8,128)S(1)}, f32[832,128]{1,0:T(8,128)S(1)}) custom-call(s32[5]{0:T(128)S(1)} %stack.38.state_ref, bf16[272,512]{1,0:T(8,128)(2,1)S(1)} %collective-permute-done.low_hbm, bf16[448,512]{1,0:T(8,128)(2,1)S(1)} %get-tuple-element.12.ends_ref, bf16[512,512]{1,0:T(8,128)(2,1)S(1)} %get-tuple-element.13.pick_ref, ...), custom_call_target="tpu_custom_call" | custom-call | tf_op jit(solution)/shard_map/edge/pallas_call | solution.py:278
  16.7 2.7 %collective-permute-start.1 = (f32[832,128]{1,0:T(8,128)S(1)}, f32[832,128]{1,0:T(8,128)S(1)}, u32[]{:S(2)}, u32[]{:S(2)}) collective-permute-start(f32[832,128]{1,0:T(8,128)S(1)} %get-tuple-element.18), channel_id=1, source_target_pairs={{0,1},{1,0},{2,3},{3,2},{4,5},{5,4},{6,7},{7,6},{8,9},{9,8},{10,11... | collective-permute-start | bytes 1277960 | tf_op jit(solution)/shard_map/ppermute | solution.py:320
  19.5 1.4 %collective-permute-done.1 = f32[832,128]{1,0:T(8,128)S(1)} collective-permute-done((f32[832,128]{1,0:T(8,128)S(1)}, f32[832,128]{1,0:T(8,128)S(1)}, u32[]{:S(2)}, u32[]{:S(2)}) %collective-permute-start.1) | collective-permute-done | bytes 426016 | tf_op jit(solution)/shard_map/ppermute | solution.py:320
  20.9 0.1 constant_dynamic-slice_fusion.1
  20.9 1.6 %collective-permute-start.2 = (f32[416,128]{1,0:T(8,128)S(1)}, f32[416,128]{1,0:T(8,128)S(1)}, u32[]{:S(2)}, u32[]{:S(2)}) collective-permute-start(f32[416,128]{1,0:T(8,128)S(1)} %get-tuple-element.25), channel_id=1, source_target_pairs={{0,8},{8,0},{1,9},{9,1},{2,10},{10,2},{3,11},{11,3},{4,12},{12,4},... | collective-permute-start | bytes 638984 | tf_op jit(solution)/shard_map/ppermute | solution.py:305
  22.5 0.0 copy-start
  22.5 6.0 %collective-permute-done.2 = f32[416,128]{1,0:T(8,128)S(1)} collective-permute-done((f32[416,128]{1,0:T(8,128)S(1)}, f32[416,128]{1,0:T(8,128)S(1)}, u32[]{:S(2)}, u32[]{:S(2)}) %collective-permute-start.2) | collective-permute-done | bytes 213024 | tf_op jit(solution)/shard_map/ppermute | solution.py:305
  28.5 3.2 %collective-permute-start.5 = (f32[104,128]{1,0:T(8,128)S(1)}, f32[104,128]{1,0:T(8,128)S(1)}, u32[]{:S(2)}, u32[]{:S(2)}) collective-permute-start(f32[104,128]{1,0:T(8,128)S(1)} %get-tuple-element.20), channel_id=1, source_target_pairs={{0,6},{2,0},{4,2},{6,4},{1,7},{3,1},{5,3},{7,5},{8,14},{10,8},{12,... | collective-permute-start | bytes 159752 | tf_op jit(solution)/shard_map/ppermute | solution.py:305
  31.8 0.0 collective-permute-start.4
  31.8 1.4 %collective-permute-start.3 = (f32[104,128]{1,0:T(8,128)S(1)}, f32[104,128]{1,0:T(8,128)S(1)}, u32[]{:S(2)}, u32[]{:S(2)}) collective-permute-start(f32[104,128]{1,0:T(8,128)S(1)} %get-tuple-element.19), channel_id=1, source_target_pairs={{0,2},{2,4},{4,6},{6,0},{1,3},{3,5},{5,7},{7,1},{8,10},{10,12},{12... | collective-permute-start | bytes 159752 | tf_op jit(solution)/shard_map/ppermute | solution.py:305
  33.2 0.6 collective-permute-done.5
  33.8 3.1 %collective-permute-done.4 = f32[104,128]{1,0:T(8,128)S(1)} collective-permute-done((f32[104,128]{1,0:T(8,128)S(1)}, f32[104,128]{1,0:T(8,128)S(1)}, u32[]{:S(2)}, u32[]{:S(2)}) %collective-permute-start.4) | collective-permute-done | bytes 53280 | tf_op jit(solution)/shard_map/ppermute | solution.py:305
  36.8 0.9 %collective-permute-done.3 = f32[104,128]{1,0:T(8,128)S(1)} collective-permute-done((f32[104,128]{1,0:T(8,128)S(1)}, f32[104,128]{1,0:T(8,128)S(1)}, u32[]{:S(2)}, u32[]{:S(2)}) %collective-permute-start.3) | collective-permute-done | bytes 53280 | tf_op jit(solution)/shard_map/ppermute | solution.py:305
  37.7 1.7 %collective-permute-start.8 = (f32[104,128]{1,0:T(8,128)S(1)}, f32[104,128]{1,0:T(8,128)S(1)}, u32[]{:S(2)}, u32[]{:S(2)}) collective-permute-start(f32[104,128]{1,0:T(8,128)S(1)} %fusion.6), channel_id=1, source_target_pairs={{0,6},{2,0},{4,2},{6,4},{1,7},{3,1},{5,3},{7,5},{8,14},{10,8},{12,... | collective-permute-start | bytes 159752 | tf_op jit(solution)/shard_map/ppermute | solution.py:312
  39.4 0.0 collective-permute-start.7
  39.4 1.8 %collective-permute-start.6 = (f32[104,128]{1,0:T(8,128)S(1)}, f32[104,128]{1,0:T(8,128)S(1)}, u32[]{:S(2)}, u32[]{:S(2)}) collective-permute-start(f32[104,128]{1,0:T(8,128)S(1)} %fusion.6), channel_id=1, source_target_pairs={{0,2},{2,4},{4,6},{6,0},{1,3},{3,5},{5,7},{7,1},{8,10},{10,12},{12... | collective-permute-start | bytes 159752 | tf_op jit(solution)/shard_map/ppermute | solution.py:312
  41.2 0.7 collective-permute-done.8
  41.9 2.9 %collective-permute-done.7 = f32[104,128]{1,0:T(8,128)S(1)} collective-permute-done((f32[104,128]{1,0:T(8,128)S(1)}, f32[104,128]{1,0:T(8,128)S(1)}, u32[]{:S(2)}, u32[]{:S(2)}) %collective-permute-start.7) | collective-permute-done | bytes 53280 | tf_op jit(solution)/shard_map/ppermute | solution.py:312
  44.9 0.6 collective-permute-done.6
  45.4 0.0 copy-start.1
  45.5 1.1 %collective-permute-start.9 = (f32[416,128]{1,0:T(8,128)S(1)}, f32[416,128]{1,0:T(8,128)S(1)}, u32[]{:S(2)}, u32[]{:S(2)}) collective-permute-start(f32[416,128]{1,0:T(8,128)S(1)} %pad_maximum_fusion.2), channel_id=1, source_target_pairs={{0,8},{8,0},{1,9},{9,1},{2,10},{10,2},{3,11},{11,3},{4,12},{12,4},... | collective-permute-start | bytes 638984 | tf_op jit(solution)/shard_map/ppermute | solution.py:312
  46.6 4.8 %collective-permute-done.9 = f32[416,128]{1,0:T(8,128)S(1)} collective-permute-done((f32[416,128]{1,0:T(8,128)S(1)}, f32[416,128]{1,0:T(8,128)S(1)}, u32[]{:S(2)}, u32[]{:S(2)}) %collective-permute-start.9) | collective-permute-done | bytes 213024 | tf_op jit(solution)/shard_map/ppermute | solution.py:312
  51.5 0.1 collective-permute-start.10
  51.6 1.7 %collective-permute-done.10.other_ref = f32[832,128]{1,0:T(8,128)S(1)} collective-permute-done((f32[832,128]{1,0:T(8,128)S(1)}, f32[832,128]{1,0:T(8,128)S(1)}, u32[]{:S(2)}, u32[]{:S(2)}) %collective-permute-start.10) | collective-permute-done | bytes 426016 | tf_op jit(solution)/shard_map/ppermute | solution.py:320
  53.3 0.0 copy-done
  53.3 20.8 %shard_map.64 = bf16[512,128]{1,0:T(8,128)(2,1)S(1)} custom-call(s32[1]{0:T(128)} %bitcast.1.side_ref, f32[832,128]{1,0:T(8,128)S(1)} %pad_maximum_fusion.mine_ref, f32[832,128]{1,0:T(8,128)S(1)} %collective-permute-done.10.other_ref, bf16[512,512]{1,0:T(8,128)(2,1)S(1)} %get-tuple-element.13.pick_ref, f32[512,128]{1,0:T(8,128)S(1)} %copy-done), custom_call_target="tpu_custom_call" | custom-call | tf_op jit(solution)/shard_map/pallas_call | solution.py:533
  74.1 0.0 copy-done.1
  74.1 1.7 %fusion = f32[32,64,128]{2,1,0:T(8,128)} fusion(bf16[32,64,512]{2,1,0:T(8,128)(2,1)S(1)} %copy-done.1, pred[32]{0:T(512)(128)(4,1)S(1)} %iota_compare_fusion, bf16[512,128]{1,0:T(8,128)(2,1)S(1)} %shard_map.64), kind=kOutput, calls=%fused_computation | convolution fusion | flops 269484032 | bytes 3276832 | tf_op jit(solution)/shard_map/dot_general | solution.py:570
  (10 shorter events, 0.2 us)
Async XLA Ops:
  1.8 12.7 %collective-permute-start = (bf16[272,512]{1,0:T(8,128)(2,1)S(1)}, bf16[272,512]{1,0:T(8,128)(2,1)S(1)}, u32[]{:S(2)}, u32[]{:S(2)}) collective-permute-start(bf16[272,512]{1,0:T(8,128)(2,1)S(1)} %concatenate.9), channel_id=1, source_target_pairs={{0,1},{1,2},{2,3},{3,4},{4,5},{5,6},{6,7},{7,8},{8,9},{9,10},{10,1... | collective-permute-start | bytes 835592 | tf_op jit(solution)/shard_map/ppermute | solution.py:559
  16.7 4.1 %collective-permute-start.1 = (f32[832,128]{1,0:T(8,128)S(1)}, f32[832,128]{1,0:T(8,128)S(1)}, u32[]{:S(2)}, u32[]{:S(2)}) collective-permute-start(f32[832,128]{1,0:T(8,128)S(1)} %get-tuple-element.18), channel_id=1, source_target_pairs={{0,1},{1,0},{2,3},{3,2},{4,5},{5,4},{6,7},{7,6},{8,9},{9,8},{10,11... | collective-permute-start | bytes 1277960 | tf_op jit(solution)/shard_map/ppermute | solution.py:320
  20.9 7.6 %collective-permute-start.2 = (f32[416,128]{1,0:T(8,128)S(1)}, f32[416,128]{1,0:T(8,128)S(1)}, u32[]{:S(2)}, u32[]{:S(2)}) collective-permute-start(f32[416,128]{1,0:T(8,128)S(1)} %get-tuple-element.25), channel_id=1, source_target_pairs={{0,8},{8,0},{1,9},{9,1},{2,10},{10,2},{3,11},{11,3},{4,12},{12,4},... | collective-permute-start | bytes 638984 | tf_op jit(solution)/shard_map/ppermute | solution.py:305
  22.5 30.9 %copy-start = (f32[512,128]{1,0:T(8,128)S(1)}, f32[512,128]{1,0:T(8,128)}, u32[]{:S(2)}) copy-start(f32[512,128]{1,0:T(8,128)} %start_ref.1) | copy-start | bytes 786436
  28.5 5.2 %collective-permute-start.5 = (f32[104,128]{1,0:T(8,128)S(1)}, f32[104,128]{1,0:T(8,128)S(1)}, u32[]{:S(2)}, u32[]{:S(2)}) collective-permute-start(f32[104,128]{1,0:T(8,128)S(1)} %get-tuple-element.20), channel_id=1, source_target_pairs={{0,6},{2,0},{4,2},{6,4},{1,7},{3,1},{5,3},{7,5},{8,14},{10,8},{12,... | collective-permute-start | bytes 159752 | tf_op jit(solution)/shard_map/ppermute | solution.py:305
  31.8 5.1 %collective-permute-start.4 = (f32[104,128]{1,0:T(8,128)S(1)}, f32[104,128]{1,0:T(8,128)S(1)}, u32[]{:S(2)}, u32[]{:S(2)}) collective-permute-start(f32[104,128]{1,0:T(8,128)S(1)} %get-tuple-element.21), channel_id=1, source_target_pairs={{0,4},{2,6},{4,0},{6,2},{1,5},{3,7},{5,1},{7,3},{8,12},{10,14},{12... | collective-permute-start | bytes 159752 | tf_op jit(solution)/shard_map/ppermute | solution.py:305
  31.8 5.9 %collective-permute-start.3 = (f32[104,128]{1,0:T(8,128)S(1)}, f32[104,128]{1,0:T(8,128)S(1)}, u32[]{:S(2)}, u32[]{:S(2)}) collective-permute-start(f32[104,128]{1,0:T(8,128)S(1)} %get-tuple-element.19), channel_id=1, source_target_pairs={{0,2},{2,4},{4,6},{6,0},{1,3},{3,5},{5,7},{7,1},{8,10},{10,12},{12... | collective-permute-start | bytes 159752 | tf_op jit(solution)/shard_map/ppermute | solution.py:305
  37.7 4.2 %collective-permute-start.8 = (f32[104,128]{1,0:T(8,128)S(1)}, f32[104,128]{1,0:T(8,128)S(1)}, u32[]{:S(2)}, u32[]{:S(2)}) collective-permute-start(f32[104,128]{1,0:T(8,128)S(1)} %fusion.6), channel_id=1, source_target_pairs={{0,6},{2,0},{4,2},{6,4},{1,7},{3,1},{5,3},{7,5},{8,14},{10,8},{12,... | collective-permute-start | bytes 159752 | tf_op jit(solution)/shard_map/ppermute | solution.py:312
  39.4 5.4 %collective-permute-start.7 = (f32[104,128]{1,0:T(8,128)S(1)}, f32[104,128]{1,0:T(8,128)S(1)}, u32[]{:S(2)}, u32[]{:S(2)}) collective-permute-start(f32[104,128]{1,0:T(8,128)S(1)} %fusion.6), channel_id=1, source_target_pairs={{0,4},{2,6},{4,0},{6,2},{1,5},{3,7},{5,1},{7,3},{8,12},{10,14},{12... | collective-permute-start | bytes 159752 | tf_op jit(solution)/shard_map/ppermute | solution.py:312
  39.4 6.0 %collective-permute-start.6 = (f32[104,128]{1,0:T(8,128)S(1)}, f32[104,128]{1,0:T(8,128)S(1)}, u32[]{:S(2)}, u32[]{:S(2)}) collective-permute-start(f32[104,128]{1,0:T(8,128)S(1)} %fusion.6), channel_id=1, source_target_pairs={{0,2},{2,4},{4,6},{6,0},{1,3},{3,5},{5,7},{7,1},{8,10},{10,12},{12... | collective-permute-start | bytes 159752 | tf_op jit(solution)/shard_map/ppermute | solution.py:312
  45.4 28.7 %copy-start.1 = (bf16[32,64,512]{2,1,0:T(8,128)(2,1)S(1)}, bf16[32,64,512]{2,1,0:T(8,128)(2,1)}, u32[]{:S(2)}) copy-start(bf16[32,64,512]{2,1,0:T(8,128)(2,1)} %param.6) | copy-start | bytes 6291460
  45.5 5.9 %collective-permute-start.9 = (f32[416,128]{1,0:T(8,128)S(1)}, f32[416,128]{1,0:T(8,128)S(1)}, u32[]{:S(2)}, u32[]{:S(2)}) collective-permute-start(f32[416,128]{1,0:T(8,128)S(1)} %pad_maximum_fusion.2), channel_id=1, source_target_pairs={{0,8},{8,0},{1,9},{9,1},{2,10},{10,2},{3,11},{11,3},{4,12},{12,4},... | collective-permute-start | bytes 638984 | tf_op jit(solution)/shard_map/ppermute | solution.py:312
  51.5 1.8 %collective-permute-start.10 = (f32[832,128]{1,0:T(8,128)S(1)}, f32[832,128]{1,0:T(8,128)S(1)}, u32[]{:S(2)}, u32[]{:S(2)}) collective-permute-start(f32[832,128]{1,0:T(8,128)S(1)} %pad_maximum_fusion.mine_ref), channel_id=1, source_target_pairs={{0,1},{1,0},{2,3},{3,2},{4,5},{5,4},{6,7},{7,6},{8,9},{9,8},{10,11... | collective-permute-start | bytes 1277960 | tf_op jit(solution)/shard_map/ppermute | solution.py:320
